TPU v7x, 32 devices: a whole 2x2x4 slice. The times are simulated.
32 devices in a mesh: grp: 2 (over y), fsdp: 8 (over z, x), seq: 2 (over core).
Axes of the slice: x: 2, y: 2, z: 4, core: 2. Of those that a mesh axis runs over, the one named last changes fastest.
Arguments:
- prompt_in: bfloat16 [2, 1024, 768], P('grp', ('fsdp', 'seq')), may hold values from -6 to 6
- cont_in: bfloat16 [2, 16, 1024, 768], P('grp', 'fsdp', 'seq'), may hold values from -6 to 6
- enc_in: bfloat16 [2, 1024, 768], P('grp', ('fsdp', 'seq')), may hold values from -6 to 6
- prefix: int32 [2, 16], P('grp', 'fsdp'), may hold values from 1 to 1024, as said below
- cot_prompt: bfloat16 [2, 1024, 768], P('grp', ('fsdp', 'seq')), may hold values from -6 to 6
- cot_cont: bfloat16 [2, 16, 1024, 768], P('grp', 'fsdp', 'seq'), may hold values from -6 to 6
- w_qkv: bfloat16 [768, 2304], P('fsdp'), may hold values from -0.3125 to 0.3125
- w_attn_out: bfloat16 [768, 768], P('fsdp'), may hold values from -0.75 to 0.75
- w_cross_q: bfloat16 [768, 768], P('fsdp'), may hold values from -0.3125 to 0.3125
- w_cross_kv: bfloat16 [768, 1536], P('fsdp'), may hold values from -0.3125 to 0.3125
- w_cross_out: bfloat16 [768, 768], P('fsdp'), may hold values from -0.75 to 0.75
- w_ffn_in: bfloat16 [768, 3072], P('fsdp'), may hold values from -0.21875 to 0.21875
- w_ffn_out: bfloat16 [3072, 768], P('fsdp'), may hold values from -0.109375 to 0.109375
- norm_gain: bfloat16 [3, 768], P(None, 'fsdp'), may hold values from 0.099609375 to 1.8984375
- norm_bias: bfloat16 [3, 768], P(None, 'fsdp'), may hold values from -3 to 3
Outputs:
- out_prompt: bfloat16 [2, 1024, 768], P('grp', ('fsdp', 'seq'))
- out_cont: bfloat16 [2, 16, 1024, 768], P('grp', 'fsdp', 'seq')
- grad_prompt: float32 [2, 1024, 768], P('grp', ('fsdp', 'seq'))
- grad_cont: float32 [2, 16, 1024, 768], P('grp', 'fsdp', 'seq')
- grad_enc: float32 [2, 1024, 768], P('grp', ('fsdp', 'seq'))
- grad_w_qkv: float32 [768, 2304], P('fsdp')
- grad_w_attn_out: float32 [768, 768], P('fsdp')
- grad_w_cross_q: float32 [768, 768], P('fsdp')
- grad_w_cross_kv: float32 [768, 1536], P('fsdp')
- grad_w_cross_out: float32 [768, 768], P('fsdp')
- grad_w_ffn_in: float32 [768, 3072], P('fsdp')
- grad_w_ffn_out: float32 [3072, 768], P('fsdp')
- grad_norm_gain: float32 [3, 768], P(None, 'fsdp')
- grad_norm_bias: float32 [3, 768], P(None, 'fsdp')
Inputs may be any that keep to these rules, and one draw needn't show every extreme that they name: Continuation c sees prompt positions below prefix[c]; in every group some continuation sees the whole prompt of 1024 tokens.
All inputs are finite; a program needn't handle non-finite values.
Results may differ from a plain program's by a relative error of at most 0.034.
The roundings to bfloat16 on the way count: a program that leaves them out, or rounds other values in their place, can miss the bound.
Values may be sent and summed in bfloat16 or wider, within the bound.
A program may use at most 448 MiB of HBM per device.

v0:
```python
import jax
import jax.numpy as jnp
from jax import lax
from jax.sharding import PartitionSpec as P

HEADS = 12
HEAD_DIM = 64


SCALE = 0.125
EPS = 1e-05
MASKED = -1e30


def cut_along(value, dim, devices):
    shape = value.shape
    pieces = value.reshape(*shape[:dim], devices, shape[dim] // devices, *shape[dim + 1 :])
    return jnp.moveaxis(pieces, dim, 0)


def sum_at_owner(value, axis, dim):
    pieces = cut_along(value, dim, lax.axis_size(axis))
    arrived = lax.all_to_all(pieces, axis, split_axis=0, concat_axis=0, tiled=True)
    return arrived.astype(jnp.float32).sum(axis=0)


def side_by_side(arrays, axis, dim, along):
    widths = [a.shape[along] for a in arrays]
    both = jnp.concatenate(arrays, axis=along)
    out = sum_at_owner(both, axis, dim)
    return tuple(jnp.split(out, [sum(widths[:k]) for k in range(1, len(widths))], axis=along))


def product(left, right):
    return jnp.dot(left, right, preferred_element_type=jnp.float32)


def weight_grad(left, right):
    return lax.dot_general(
        left, right, (((0,), (0,)), ((), ())), preferred_element_type=jnp.float32
    )


def back_product(left, right):
    return lax.dot_general(
        left, right, (((1,), (1,)), ((), ())), preferred_element_type=jnp.float32
    )


def norm_rows(resid, gain, shift):
    average = jnp.mean(resid, axis=-1, keepdims=True)
    centred = resid - average
    variance = jnp.mean(centred * centred, axis=-1, keepdims=True)
    return centred * lax.rsqrt(variance + EPS) * gain + shift


def gelu_exact(values):
    return jax.nn.gelu(values, approximate=False)


def to_heads(spread, seq_count, prompt_rows):
    tail = spread.shape[1:]
    grouped = spread.reshape((seq_count, -1) + tail)
    prompt_part = grouped[:, :prompt_rows].reshape((-1,) + tail)
    cont_part = grouped[:, prompt_rows:].reshape((-1,) + tail)
    return jnp.concatenate([prompt_part, cont_part], 0)


def to_rows(joined, seq_count, prompt_rows):
    tail = joined.shape[1:]
    block_rows = seq_count * prompt_rows
    prompt_part = joined[:block_rows].reshape((seq_count, prompt_rows) + tail)
    cont_part = joined[block_rows:].reshape((seq_count, -1) + tail)
    return jnp.concatenate([prompt_part, cont_part], 1).reshape((-1,) + tail)


def head_scores(queries, key_heads):
    return (
        jnp.einsum("qhe,khe->hqk", queries, key_heads, preferred_element_type=jnp.float32) * SCALE
    )


def online_update(running, scores, allowed, value_heads):
    row_top, totals, accumulated = running
    masked = jnp.where(allowed, scores, MASKED)
    new_top = jnp.maximum(row_top, jnp.max(masked, axis=-1))
    shrink = jnp.exp(row_top - new_top)
    raised = jnp.exp(jnp.where(allowed, scores - new_top[..., None], MASKED))
    new_totals = totals * shrink + jnp.sum(raised, axis=-1)
    update = jnp.einsum(
        "hqk,khe->qhe", raised.astype(jnp.bfloat16), value_heads, preferred_element_type=jnp.float32
    )
    return (new_top, new_totals, accumulated * jnp.transpose(shrink)[..., None] + update)


def attention_grads(queries, grad_heads, log_sum, row_delta, key_heads, value_heads, allowed):
    scores = head_scores(queries, key_heads)
    prob_rows = jnp.exp(jnp.where(allowed, scores - log_sum[..., None], MASKED))
    grad_prob = jnp.einsum(
        "qhe,khe->hqk", grad_heads, value_heads, preferred_element_type=jnp.float32
    )
    grad_score = (prob_rows * (grad_prob - row_delta[..., None])).astype(jnp.bfloat16)
    grad_q = (
        jnp.einsum("hqk,khe->qhe", grad_score, key_heads, preferred_element_type=jnp.float32)
        * SCALE
    )
    grad_k = (
        jnp.einsum("hqk,qhe->khe", grad_score, queries, preferred_element_type=jnp.float32) * SCALE
    )
    grad_v = jnp.einsum(
        "hqk,qhe->khe",
        prob_rows.astype(jnp.bfloat16),
        grad_heads,
        preferred_element_type=jnp.float32,
    )
    return (grad_q, grad_k, grad_v)


def micro_step(weights, prompt_x, cont_x, encoder, enc_kv, reach_len, cot_rows):
    (
        w_qkv,
        w_attn_out,
        w_cross_q,
        w_cross_kv,
        w_cross_out,
        w_ffn_in,
        w_ffn_out,
        gain_all,
        bias_all,
    ) = weights
    gain_rows = gain_all.astype(jnp.float32)
    bias_rows = bias_all.astype(jnp.float32)
    seq_count = lax.axis_size("seq")
    prompt_rows = prompt_x.shape[0]
    block_rows = seq_count * prompt_rows
    cont_len = seq_count * cont_x.shape[0]
    inputs = jnp.concatenate([prompt_x, cont_x], 0)
    row_total = inputs.shape[0]
    model_width = inputs.shape[1]
    head_width = model_width // seq_count
    head_count = head_width // HEAD_DIM
    query_total = block_rows + cont_len
    qkv_rows = product(inputs, w_qkv).astype(jnp.bfloat16).reshape(row_total, 3, model_width)
    joined = to_heads(
        lax.all_to_all(qkv_rows, "seq", split_axis=2, concat_axis=0, tiled=True),
        seq_count,
        prompt_rows,
    )
    queries = joined[:, 0].reshape(query_total, head_count, HEAD_DIM)
    prompt_keys = joined[:block_rows, 1]
    prompt_values = joined[:block_rows, 2]
    cont_keys = joined[block_rows:, 1].reshape(cont_len, head_count, HEAD_DIM)
    cont_values = joined[block_rows:, 2].reshape(cont_len, head_count, HEAD_DIM)
    positions = lax.axis_index("fsdp") * block_rows + lax.iota(jnp.int32, block_rows) + 1
    limits = jnp.concatenate([positions, jnp.full((cont_len,), reach_len, jnp.int32)], 0)
    causal = lax.iota(jnp.int32, cont_len)[:, None] >= lax.iota(jnp.int32, cont_len)[None, :]
    empty_state = (
        jnp.full((head_count, cont_len), MASKED, jnp.float32),
        jnp.zeros((head_count, cont_len), jnp.float32),
        jnp.zeros((cont_len, head_count, HEAD_DIM), jnp.float32),
    )
    cont_top, cont_totals, cont_accum = online_update(
        empty_state, head_scores(queries[block_rows:], cont_keys), causal[None], cont_values
    )
    start_state = (
        jnp.concatenate([jnp.full((head_count, block_rows), MASKED, jnp.float32), cont_top], 1),
        jnp.concatenate([jnp.zeros((head_count, block_rows), jnp.float32), cont_totals], 1),
        jnp.concatenate(
            [jnp.zeros((block_rows, head_count, HEAD_DIM), jnp.float32), cont_accum], 0
        ),
    )
    shard_pair = (
        lax.all_gather(prompt_keys, "fsdp", axis=0, tiled=True),
        lax.all_gather(prompt_values, "fsdp", axis=0, tiled=True),
    )
    key_count = shard_pair[0].shape[0]
    key_heads = shard_pair[0].reshape(key_count, head_count, HEAD_DIM)
    value_heads = shard_pair[1].reshape(key_count, head_count, HEAD_DIM)
    allowed = lax.iota(jnp.int32, key_count)[None, :] < limits[:, None]
    row_top, totals, accumulated = online_update(
        start_state, head_scores(queries, key_heads), allowed[None], value_heads
    )
    attended = accumulated / jnp.transpose(totals)[..., None]
    log_sum = row_top + jnp.log(totals)
    att_heads = attended.astype(jnp.bfloat16).reshape(query_total, head_width)
    att_rows = lax.all_to_all(
        to_rows(att_heads, seq_count, prompt_rows), "seq", split_axis=0, concat_axis=1, tiled=True
    )
    resid_one = inputs.astype(jnp.float32) + product(att_rows, w_attn_out)
    first_out, first_pull = jax.vjp(norm_rows, resid_one, gain_rows[0], bias_rows[0])
    first_low = first_out.astype(jnp.bfloat16)
    cross_q = product(first_low, w_cross_q).astype(jnp.bfloat16).reshape(row_total, HEADS, HEAD_DIM)
    enc_total = enc_kv.shape[0]
    cross_k = enc_kv[:, :model_width].reshape(enc_total, HEADS, HEAD_DIM)
    cross_v = enc_kv[:, model_width:].reshape(enc_total, HEADS, HEAD_DIM)
    cross_prob = jax.nn.softmax(head_scores(cross_q, cross_k), axis=-1)
    cross_low = cross_prob.astype(jnp.bfloat16)
    cross_att = jnp.einsum("hqk,khe->qhe", cross_low, cross_v, preferred_element_type=jnp.float32)
    cross_att = cross_att.astype(jnp.bfloat16).reshape(row_total, model_width)
    resid_two = first_out + product(cross_att, w_cross_out)
    second, second_pull = jax.vjp(norm_rows, resid_two, gain_rows[1], bias_rows[1])
    second_low = second.astype(jnp.bfloat16)
    pre_act = product(second_low, w_ffn_in)
    activated, gelu_pull = jax.vjp(gelu_exact, pre_act)
    act_low = activated.astype(jnp.bfloat16)
    resid_three = second + product(act_low, w_ffn_out)
    third_out, third_pull = jax.vjp(norm_rows, resid_three, gain_rows[2], bias_rows[2])
    grad_three, gain_three, bias_three = third_pull(cot_rows)
    grad_ffn_out = grad_three.astype(jnp.bfloat16)
    grad_w_ffn_out = weight_grad(act_low, grad_ffn_out)
    grad_pre = gelu_pull(back_product(grad_ffn_out, w_ffn_out))[0].astype(jnp.bfloat16)
    grad_w_ffn_in = weight_grad(second_low, grad_pre)
    grad_second = grad_three + back_product(grad_pre, w_ffn_in)
    grad_two, gain_two, bias_two = second_pull(grad_second)
    grad_cross_proj = grad_two.astype(jnp.bfloat16)
    grad_w_cross_out = weight_grad(cross_att, grad_cross_proj)
    grad_cross_att = (
        back_product(grad_cross_proj, w_cross_out)
        .astype(jnp.bfloat16)
        .reshape(row_total, HEADS, HEAD_DIM)
    )
    grad_cross_prob = jnp.einsum(
        "qhe,khe->hqk", grad_cross_att, cross_v, preferred_element_type=jnp.float32
    )
    grad_cross_score = cross_prob * (
        grad_cross_prob - jnp.sum(cross_prob * grad_cross_prob, axis=-1, keepdims=True)
    )
    grad_cross_score = grad_cross_score.astype(jnp.bfloat16)
    grad_cross_q = (
        jnp.einsum("hqk,khe->qhe", grad_cross_score, cross_k, preferred_element_type=jnp.float32)
        * SCALE
    )
    grad_cross_q = grad_cross_q.astype(jnp.bfloat16).reshape(row_total, model_width)
    grad_cross_k = (
        jnp.einsum("hqk,qhe->khe", grad_cross_score, cross_q, preferred_element_type=jnp.float32)
        * SCALE
    )
    grad_cross_v = jnp.einsum(
        "hqk,qhe->khe", cross_low, grad_cross_att, preferred_element_type=jnp.float32
    )
    enc_terms = jnp.concatenate(
        [
            grad_cross_k.reshape(enc_total, model_width),
            grad_cross_v.reshape(enc_total, model_width),
        ],
        1,
    )
    grad_enc_kv = lax.psum_scatter(
        enc_terms, ("fsdp", "seq"), scatter_dimension=0, tiled=True
    ).astype(jnp.bfloat16)
    grad_w_cross_kv = weight_grad(encoder, grad_enc_kv)
    grad_encoder = back_product(grad_enc_kv, w_cross_kv)
    grad_w_cross_q = weight_grad(first_low, grad_cross_q)
    grad_first = grad_two + back_product(grad_cross_q, w_cross_q)
    grad_one, gain_one, bias_one = first_pull(grad_first)
    grad_attn_proj = grad_one.astype(jnp.bfloat16)
    grad_w_attn_out = weight_grad(att_rows, grad_attn_proj)
    grad_att_rows = back_product(grad_attn_proj, w_attn_out).astype(jnp.bfloat16)
    grad_spread = lax.all_to_all(grad_att_rows, "seq", split_axis=1, concat_axis=0, tiled=True)
    grad_heads = to_heads(grad_spread, seq_count, prompt_rows).reshape(
        query_total, head_count, HEAD_DIM
    )
    row_delta = jnp.transpose(jnp.sum(grad_heads.astype(jnp.float32) * attended, axis=-1))
    local_q, local_k, local_v = attention_grads(
        queries[block_rows:],
        grad_heads[block_rows:],
        log_sum[:, block_rows:],
        row_delta[:, block_rows:],
        cont_keys,
        cont_values,
        causal[None],
    )
    query_start = jnp.concatenate(
        [jnp.zeros((block_rows, head_count, HEAD_DIM), jnp.float32), local_q], 0
    )
    shard_pair = (
        lax.all_gather(prompt_keys, "fsdp", axis=0, tiled=True),
        lax.all_gather(prompt_values, "fsdp", axis=0, tiled=True),
    )
    key_count = shard_pair[0].shape[0]
    key_heads = shard_pair[0].reshape(key_count, head_count, HEAD_DIM)
    value_heads = shard_pair[1].reshape(key_count, head_count, HEAD_DIM)
    allowed = lax.iota(jnp.int32, key_count)[None, :] < limits[:, None]
    part_q, part_k, part_v = attention_grads(
        queries, grad_heads, log_sum, row_delta, key_heads, value_heads, allowed[None]
    )
    run_k = part_k.reshape(key_count, head_width)
    run_v = part_v.reshape(key_count, head_width)
    grad_q = query_start + part_q
    grad_kp, grad_vp = side_by_side(
        (run_k.astype(jnp.bfloat16), run_v.astype(jnp.bfloat16)), "fsdp", 0, 1
    )
    grad_joined = jnp.stack(
        [
            grad_q.reshape(query_total, head_width),
            jnp.concatenate([grad_kp, local_k.reshape(cont_len, head_width)], 0),
            jnp.concatenate([grad_vp, local_v.reshape(cont_len, head_width)], 0),
        ],
        1,
    ).astype(jnp.bfloat16)
    grad_qkv = lax.all_to_all(
        to_rows(grad_joined, seq_count, prompt_rows), "seq", split_axis=0, concat_axis=2, tiled=True
    )
    grad_qkv = grad_qkv.reshape(row_total, 3 * model_width)
    grad_w_qkv = weight_grad(inputs, grad_qkv)
    grad_inputs = grad_one + back_product(grad_qkv, w_qkv)
    gradients = (
        grad_w_qkv,
        grad_w_attn_out,
        grad_w_cross_q,
        grad_w_cross_kv,
        grad_w_cross_out,
        grad_w_ffn_in,
        grad_w_ffn_out,
        jnp.stack([gain_one, gain_two, gain_three], 0),
        jnp.stack([bias_one, bias_two, bias_three], 0),
    )
    return (third_out.astype(jnp.bfloat16), grad_inputs, grad_encoder, gradients)


def on_device(
    prompt_in,
    cont_in,
    enc_in,
    prefix,
    cot_prompt,
    cot_cont,
    w_qkv,
    w_attn_out,
    w_cross_q,
    w_cross_kv,
    w_cross_out,
    w_ffn_in,
    w_ffn_out,
    norm_gain,
    norm_bias,
):
    prompt_x = prompt_in[0]
    encoder = enc_in[0]
    prompt_rows = prompt_x.shape[0]
    micro_count = cont_in.shape[1]
    outputs_cont, grads_cont = ([], [])
    prompt_output = None
    prompt_grad = None
    enc_grad = None
    shard_grads = None
    weights = None
    enc_kv = None
    for micro_index in range(micro_count):
        weights = (
            lax.all_gather(w_qkv, "fsdp", axis=0, tiled=True),
            lax.all_gather(w_attn_out, "fsdp", axis=0, tiled=True),
            lax.all_gather(w_cross_q, "fsdp", axis=0, tiled=True),
            lax.all_gather(w_cross_kv, "fsdp", axis=0, tiled=True),
            lax.all_gather(w_cross_out, "fsdp", axis=0, tiled=True),
            lax.all_gather(w_ffn_in, "fsdp", axis=0, tiled=True),
            lax.all_gather(w_ffn_out, "fsdp", axis=0, tiled=True),
            lax.all_gather(norm_gain, "fsdp", axis=1, tiled=True),
            lax.all_gather(norm_bias, "fsdp", axis=1, tiled=True),
        )
        if micro_index == 0:
            enc_local = product(encoder, weights[3]).astype(jnp.bfloat16)
            enc_kv = lax.all_gather(enc_local, ("fsdp", "seq"), axis=0, tiled=True)
        prompt_cot = cot_prompt[0] if micro_index == 0 else jnp.zeros_like(cot_prompt[0])
        cot_rows = jnp.concatenate([prompt_cot, cot_cont[0, micro_index]], 0).astype(jnp.float32)
        third_out, grad_inputs, grad_encoder, gradients = micro_step(
            weights,
            prompt_x,
            cont_in[0, micro_index],
            encoder,
            enc_kv,
            prefix[0, micro_index],
            cot_rows,
        )
        if micro_index == 0:
            prompt_output = third_out[:prompt_rows]
            prompt_grad = grad_inputs[:prompt_rows]
            enc_grad = grad_encoder
        else:
            prompt_grad = prompt_grad + grad_inputs[:prompt_rows]
            enc_grad = enc_grad + grad_encoder
        outputs_cont.append(third_out[prompt_rows:])
        grads_cont.append(grad_inputs[prompt_rows:])
        reduced = (
            lax.psum_scatter(gradients[0], "fsdp", scatter_dimension=0, tiled=True),
            lax.psum_scatter(gradients[1], "fsdp", scatter_dimension=0, tiled=True),
            lax.psum_scatter(gradients[2], "fsdp", scatter_dimension=0, tiled=True),
            lax.psum_scatter(gradients[3], "fsdp", scatter_dimension=0, tiled=True),
            lax.psum_scatter(gradients[4], "fsdp", scatter_dimension=0, tiled=True),
            lax.psum_scatter(gradients[5], "fsdp", scatter_dimension=0, tiled=True),
            lax.psum_scatter(gradients[6], "fsdp", scatter_dimension=0, tiled=True),
            lax.psum_scatter(gradients[7], "fsdp", scatter_dimension=1, tiled=True),
            lax.psum_scatter(gradients[8], "fsdp", scatter_dimension=1, tiled=True),
        )
        shard_grads = (
            reduced if shard_grads is None else jax.tree.map(jnp.add, shard_grads, reduced)
        )
    totals = (
        lax.psum(shard_grads[0].astype(jnp.bfloat16), ("grp", "seq")).astype(jnp.float32),
        lax.psum(shard_grads[1].astype(jnp.bfloat16), ("grp", "seq")).astype(jnp.float32),
        lax.psum(shard_grads[2].astype(jnp.bfloat16), ("grp", "seq")).astype(jnp.float32),
        lax.psum(shard_grads[3].astype(jnp.bfloat16), ("grp", "seq")).astype(jnp.float32),
        lax.psum(shard_grads[4].astype(jnp.bfloat16), ("grp", "seq")).astype(jnp.float32),
        lax.psum(shard_grads[5].astype(jnp.bfloat16), ("grp", "seq")).astype(jnp.float32),
        lax.psum(shard_grads[6].astype(jnp.bfloat16), ("grp", "seq")).astype(jnp.float32),
        lax.psum(shard_grads[7].astype(jnp.bfloat16), ("grp", "seq")).astype(jnp.float32),
        lax.psum(shard_grads[8].astype(jnp.bfloat16), ("grp", "seq")).astype(jnp.float32),
    )
    return (
        prompt_output[None],
        jnp.stack(outputs_cont, 0)[None],
        prompt_grad[None],
        jnp.stack(grads_cont, 0)[None],
        enc_grad[None],
        totals[0],
        totals[1],
        totals[2],
        totals[3],
        totals[4],
        totals[5],
        totals[6],
        totals[7],
        totals[8],
    )


def solution(mesh):
    return jax.shard_map(
        on_device,
        mesh=mesh,
        in_specs=(
            P("grp", ("fsdp", "seq"), None),
            P("grp", "fsdp", "seq", None),
            P("grp", ("fsdp", "seq"), None),
            P("grp", "fsdp"),
            P("grp", ("fsdp", "seq"), None),
            P("grp", "fsdp", "seq", None),
            P("fsdp", None),
            P("fsdp", None),
            P("fsdp", None),
            P("fsdp", None),
            P("fsdp", None),
            P("fsdp", None),
            P("fsdp", None),
            P(None, "fsdp"),
            P(None, "fsdp"),
        ),
        out_specs=(
            P("grp", ("fsdp", "seq"), None),
            P("grp", "fsdp", "seq", None),
            P("grp", ("fsdp", "seq"), None),
            P("grp", "fsdp", "seq", None),
            P("grp", ("fsdp", "seq"), None),
            P("fsdp", None),
            P("fsdp", None),
            P("fsdp", None),
            P("fsdp", None),
            P("fsdp", None),
            P("fsdp", None),
            P("fsdp", None),
            P(None, "fsdp"),
            P(None, "fsdp"),
        ),
        check_vma=False,
    )
```

profile of v0, /device:TPU:0, one launch (start us, length us, event | category | flops | bytes accessed | tf_op | source)
XLA Modules:
  0.0 2061.6 jit_solution(17798676175585928813)
XLA Ops:
  10.1 54.7 %all-gather.19.cloned.1.call-done = bf16[768,1536]{1,0:T(8,128)(2,1)} async-done(((bf16[96,1536]{1,0:T(8,128)(2,1)}), bf16[768,1536]{1,0:T(8,128)(2,1)}) %all-gather.19.cloned.1.call-update) | async-done | bytes 2359312 | tf_op jit(solution)/shard_map/all_gather | solution.py:354
  71.7 18.8 all-gather.4
  90.5 16.8 all-gather.5
  115.5 14.8 all-gather.15.cloned.1.call-done
  220.1 36.1 %all-gather = bf16[1024,1,384]{2,0,1:T(8,128)(2,1)} all-gather(bf16[128,1,384]{2,0,1:T(8,128)(2,1)} %get-tuple-element.163), channel_id=2, replica_groups=mesh['grp'=2,'fsdp'=8,'seq'=2] {'fsdp'}, dimensions={0}, use_global_device_ids=true | all-gather | bytes 884736 | tf_op jit(solution)/shard_map/all_gather | solution.py:173
  263.2 34.9 %all-gather.1 = bf16[1024,1,384]{2,0,1:T(8,128)(2,1)} all-gather(bf16[128,1,384]{2,0,1:T(8,128)(2,1)} %get-tuple-element.164), channel_id=3, replica_groups=mesh['grp'=2,'fsdp'=8,'seq'=2] {'fsdp'}, dimensions={0}, use_global_device_ids=true | all-gather | bytes 884736 | tf_op jit(solution)/shard_map/all_gather | solution.py:174
  313.5 17.6 select_reduce_fusion.2
  343.6 19.1 fusion.16
  387.8 14.6 fusion.215
  407.5 37.2 %all-gather.2 = bf16[1024,1,384]{2,0,1:T(8,128)(2,1)} all-gather(bf16[128,1,384]{2,0,1:T(8,128)(2,1)S(1)} %copy-done.101), channel_id=4, replica_groups=mesh['grp'=2,'fsdp'=8,'seq'=2] {'fsdp'}, dimensions={0}, use_global_device_ids=true | all-gather | bytes 884736 | tf_op jit(solution)/shard_map/all_gather | solution.py:173
  446.1 36.5 %all-gather.3 = bf16[1024,1,384]{2,0,1:T(8,128)(2,1)} all-gather(bf16[128,1,384]{2,0,1:T(8,128)(2,1)S(1)} %get-tuple-element.162), channel_id=5, replica_groups=mesh['grp'=2,'fsdp'=8,'seq'=2] {'fsdp'}, dimensions={0}, use_global_device_ids=true | all-gather | bytes 884736 | tf_op jit(solution)/shard_map/all_gather | solution.py:174
  521.5 14.3 fusion.220
  572.5 14.4 fusion.222
  604.2 22.6 %multiply_convert_fusion.6 = (bf16[576,3072]{1,0:T(8,128)(2,1)}, f32[576,3072]{1,0:T(8,128)}, f32[576,3072]{1,0:T(8,128)}) fusion(bf16[768,3072]{1,0:T(8,128)(2,1)} %all-gather.27.cloned.1.call-done, f32[576,768]{1,0:T(8,128)} %copy-done.10, f32[576]{0:T(1024)S(1)} %fusion.155, f32[576]{0:T(1024)S(1)} %broadcast_multiply_fusion.1, f32[768]{0:T(1024)S(1)} %copy-done.98, ...), kind=kOutput, calls=%fused_computation.66 | convolution fusion | flops 2835136512 | bytes 24193536 | tf_op jit(solution)/shard_map/dot_general | solution.py:35
  634.3 14.3 fusion.217
  662.5 21.8 %multiply_convert_fusion.7 = (bf16[576,3072]{1,0:T(8,128)(2,1)S(1)}, f32[576,3072]{1,0:T(8,128)}, f32[576,3072]{1,0:T(8,128)}) fusion(bf16[768,3072]{1,0:T(8,128)(2,1)} %all-gather.27.cloned.1.call-done, f32[576,768]{1,0:T(8,128)S(1)} %get-tuple-element.208, f32[768]{0:T(1024)S(1)} %copy-done.98, f32[768]{0:T(1024)S(1)} %copy-done.96, ...), kind=kOutput, calls=%fused_computation.83 | convolution fusion | flops 2835136512 | bytes 24193536 | tf_op jit(solution)/shard_map/dot_general | solution.py:35
  748.5 21.0 %multiply_reduce_fusion.1 = (f32[12,576]{1,0:T(8,128)S(1)}, f32[12,576,1024]{2,1,0:T(8,128)}) fusion(f32[12,576,1024]{2,1,0:T(8,128)} %get-tuple-element.206, f32[12,576]{1,0:T(8,128)S(1)} %get-tuple-element.205, bf16[576,12,64]{0,2,1:T(8,128)(2,1)S(1)} %bitcast.451, bf16[1024,12,64]{0,2,1:T(8,128)(2,1)S(1)} %bitcast.440), kind=kOutput, calls=%fused_computation.9 | convolution fusion | flops 927196416 | bytes 59136000 | tf_op jit(solution)/shard_map/qhe,khe->hqk/dot_general | solution.py:222
  769.6 23.7 %multiply_convert_fusion.3 = bf16[12,576,1024]{2,1,0:T(8,128)(2,1)} fusion(f32[12,576,1024]{2,1,0:T(8,128)} %get-tuple-element.227, f32[12,576]{1,0:T(8,128)S(1)} %get-tuple-element.226, f32[12,576,1024]{2,1,0:T(8,128)} %get-tuple-element.206, f32[12,576]{1,0:T(8,128)S(1)} %get-tuple-element.205), kind=kLoop, calls=%fused_computation.8 | loop fusion | flops 28311552 | bytes 70834176 | tf_op jit(solution)/shard_map/convert_element_type | solution.py:228
  828.1 22.7 %multiply_reduce_fusion = (f32[12,576]{1,0:T(8,128)S(1)}, f32[12,576,1024]{2,1,0:T(8,128)}) fusion(f32[12,576,1024]{2,1,0:T(8,128)} %get-tuple-element.219, f32[12,576]{1,0:T(8,128)S(1)} %copy-done.133, bf16[576,12,64]{0,2,1:T(8,128)(2,1)S(1)} %bitcast.448, bf16[1024,12,64]{0,2,1:T(8,128)(2,1)S(1)} %bitcast.441), kind=kOutput, calls=%fused_computation.5 | convolution fusion | flops 927196416 | bytes 59136000 | tf_op jit(solution)/shard_map/qhe,khe->hqk/dot_general | solution.py:222
  850.9 24.4 %multiply_convert_fusion.1 = bf16[12,576,1024]{2,1,0:T(8,128)(2,1)} fusion(f32[12,576,1024]{2,1,0:T(8,128)} %get-tuple-element.229, f32[12,576]{1,0:T(8,128)S(1)} %get-tuple-element.228, f32[12,576,1024]{2,1,0:T(8,128)} %get-tuple-element.219, f32[12,576]{1,0:T(8,128)S(1)} %copy-done.133), kind=kLoop, calls=%fused_computation.4 | loop fusion | flops 28311552 | bytes 70834176 | tf_op jit(solution)/shard_map/convert_element_type | solution.py:228
  939.0 19.3 multiply_convert_fusion
  1008.0 16.2 multiply_convert_fusion.4
  1034.1 19.2 multiply_convert_fusion.2
  1104.6 16.3 multiply_convert_fusion.5
  1203.2 18.0 copy.333
  1236.8 18.0 copy.356
  1353.2 70.5 %reduce-scatter.24.cloned.1.call-done = f32[96,768]{1,0:T(8,128)} async-done(((f32[768,768]{1,0:T(8,128)}), f32[96,768]{1,0:T(8,128)}) %reduce-scatter.24.cloned.1.call-update) | async-done | bytes 294928 | tf_op jit(solution)/shard_map/reduce_scatter | solution.py:386
  1425.3 130.3 %reduce-scatter.22.cloned.1.call-done = f32[96,2304]{1,0:T(8,128)} async-done(((f32[768,2304]{1,0:T(8,128)}), f32[96,2304]{1,0:T(8,128)}) %reduce-scatter.22.cloned.1.call-update) | async-done | bytes 884752 | tf_op jit(solution)/shard_map/reduce_scatter | solution.py:385
  1557.6 162.8 %reduce-scatter.30.cloned.1.call-done = f32[96,3072]{1,0:T(8,128)} async-done(((f32[768,3072]{1,0:T(8,128)}), f32[96,3072]{1,0:T(8,128)}) %reduce-scatter.30.cloned.1.call-update) | async-done | bytes 1179664 | tf_op jit(solution)/shard_map/reduce_scatter | solution.py:390
  1722.5 162.5 %reduce-scatter.32.cloned.1.call-done = f32[384,768]{1,0:T(8,128)} async-done(((f32[3072,768]{1,0:T(8,128)}), f32[384,768]{1,0:T(8,128)}) %reduce-scatter.32.cloned.1.call-update) | async-done | bytes 1179664 | tf_op jit(solution)/shard_map/reduce_scatter | solution.py:391
  1887.2 96.3 %reduce-scatter.38.cloned.1.call-done = f32[96,1536]{1,0:T(8,128)} async-done(((f32[768,1536]{1,0:T(8,128)}), f32[96,1536]{1,0:T(8,128)}) %reduce-scatter.38.cloned.1.call-update) | async-done | bytes 589840
  1993.1 51.3 %all-reduce.15.cloned.1.call-done = (bf16[96,2304]{1,0:T(8,128)(2,1)}, bf16[96,768]{1,0:T(8,128)(2,1)}, bf16[96,768]{1,0:T(8,128)(2,1)}, bf16[96,1536]{0,1:T(8,1...) async-done(((bf16[96,2304]{1,0:T(8,128)(2,1)}, bf16[96,768]{1,0:T(8,128)(2,1)}, bf16[96,768]{1,0:T(8,128)(2,1)}, ...) | async-done | bytes 2359312 | tf_op jit(solution)/shard_map/psum | solution.py:399
  (744 shorter events, 783.2 us)
Async XLA Ops:
  7.2 57.6 %all-gather.19.cloned.1.call-start = ((), (), s32[]{:S(2)}) async-start(), calls=%async_computation.23 | async-start | bytes 2654208 | tf_op jit(solution)/shard_map/all_gather | solution.py:354
  7.9 122.3 %all-gather.15.cloned.1.call-start = ((), (), s32[]{:S(2)}) async-start(), calls=%async_computation.21 | async-start | bytes 3981312 | tf_op jit(solution)/shard_map/all_gather | solution.py:351
  8.7 536.1 %all-gather.17.cloned.1.call-start = ((), (), s32[]{:S(2)}) async-start(), calls=%async_computation.22 | async-start | bytes 1327104 | tf_op jit(solution)/shard_map/all_gather | solution.py:352
  9.4 538.3 %all-gather.23.cloned.1.call-start = ((), (), s32[]{:S(2)}) async-start(), calls=%async_computation.25 | async-start | bytes 1327104 | tf_op jit(solution)/shard_map/all_gather | solution.py:353
  10.0 80.5 %copy-start.179 = (bf16[3,96]{1,0:T(4,128)(2,1)S(1)}, bf16[3,96]{1,0:T(4,128)(2,1)}, u32[]{:S(2)}) copy-start(bf16[3,96]{1,0:T(4,128)(2,1)} %param.29) | copy-start | bytes 1732
  10.0 553.8 %all-gather.21.cloned.1.call-start = ((), (), s32[]{:S(2)}) async-start(), calls=%async_computation.24 | async-start | bytes 3342336 | tf_op jit(solution)/shard_map/all_gather | solution.py:363
  67.7 532.0 %all-gather.25.cloned.1.call-start = ((), (), s32[]{:S(2)}) async-start(), calls=%async_computation.26 | async-start | bytes 1327104 | tf_op jit(solution)/shard_map/all_gather | solution.py:355
  68.2 535.9 %all-gather.27.cloned.1.call-start = ((), (), s32[]{:S(2)}) async-start(), calls=%async_computation.27 | async-start | bytes 5308416 | tf_op jit(solution)/shard_map/all_gather | solution.py:356
  69.0 557.7 %all-gather.29.cloned.1.call-start = ((), (), s32[]{:S(2)}) async-start(), calls=%async_computation.28 | async-start | bytes 5308416 | tf_op jit(solution)/shard_map/all_gather | solution.py:357
  69.7 1237.7 %reduce-scatter.34.cloned.1.call-start = ((), (), s32[]{:S(2)}) async-start(), calls=%async_computation.35 | async-start | bytes 6684672
  109.7 411.8 %copy-start.6 = (pred[1152,1024]{0,1:T(8,128)(4,1)}, pred[1152,1024]{0,1:T(8,128)(4,1)S(1)}, u32[]{:S(2)}) copy-start(pred[1152,1024]{0,1:T(8,128)(4,1)S(1)} %iota_compare_fusion) | copy-start | bytes 3538948
  110.6 277.1 %copy-start.4 = (pred[1152,1024]{0,1:T(8,128)(4,1)}, pred[1152,1024]{0,1:T(8,128)(4,1)S(1)}, u32[]{:S(2)}) copy-start(pred[1152,1024]{0,1:T(8,128)(4,1)S(1)} %iota_compare_fusion.1) | copy-start | bytes 3538948
  217.4 113.7 %copy-start.22 = (bf16[1152,1,384]{0,2,1:T(8,128)(2,1)}, bf16[1152,1,384]{0,2,1:T(8,128)(2,1)S(1)}, u32[]{:S(2)}) copy-start(bf16[1152,1,384]{0,2,1:T(8,128)(2,1)S(1)} %copy.284) | copy-start | bytes 2654212
  387.7 148.8 %copy-start.113 = (f32[6,1152]{1,0:T(8,128)}, f32[6,1152]{1,0:T(8,128)S(1)}, u32[]{:S(2)}) copy-start(f32[6,1152]{1,0:T(8,128)S(1)} %get-tuple-element.169) | copy-start | bytes 82948
  404.9 80.1 %copy-start.24 = (bf16[1152,1,384]{0,2,1:T(8,128)(2,1)}, bf16[1152,1,384]{0,2,1:T(8,128)(2,1)S(1)}, u32[]{:S(2)}) copy-start(bf16[1152,1,384]{0,2,1:T(8,128)(2,1)S(1)} %copy.305) | copy-start | bytes 2654212
  602.5 128.2 %copy-start.119 = (f32[576]{0:T(1024)}, f32[576]{0:T(1024)S(1)}, u32[]{:S(2)}) copy-start(f32[576]{0:T(1024)S(1)} %broadcast_multiply_fusion.1) | copy-start | bytes 6916
  604.1 126.6 %copy-start.125 = (f32[576]{0:T(1024)}, f32[576]{0:T(1024)S(1)}, u32[]{:S(2)}) copy-start(f32[576]{0:T(1024)S(1)} %fusion.155) | copy-start | bytes 6916
  810.3 74.8 %copy-start.165 = (f32[576]{0:T(1024)}, f32[576]{0:T(1024)S(1)}, u32[]{:S(2)}) copy-start(f32[576]{0:T(1024)S(1)} %negate_multiply_fusion.3) | copy-start | bytes 6916
  928.3 41.1 %all-to-all-start.4 = ((bf16[576,2,384]{2,0,1:T(8,128)(2,1)}), bf16[576,2,384]{2,0,1:T(8,128)(2,1)}, u32[]{:S(2)}, u32[]{:S(2)}) async-start(bf16[576,2,384]{2,0,1:T(8,128)(2,1)} %bitcast.364), calls=%async_computation.4 | async-start | bytes 1769472 | tf_op jit(solution)/shard_map/all_to_all | solution.py:259
  932.6 376.1 %reduce-scatter.36.cloned.1.call-start = ((), (), s32[]{:S(2)}) async-start(), calls=%async_computation.36 | async-start | bytes 6684672
  996.4 155.5 %all-to-all-start.8 = ((bf16[8,128,768]{1,2,0:T(8,128)(2,1)}), bf16[8,128,768]{1,2,0:T(8,128)(2,1)}, u32[]{:S(2)}, u32[]{:S(2)}) async-start(bf16[8,128,768]{1,2,0:T(8,128)(2,1)} %pad_maximum_fusion.9), calls=%async_computation.8 | async-start | bytes 3145728 | tf_op jit(solution)/shard_map/all_to_all | solution.py:23
  1000.7 324.7 %reduce-scatter.40.cloned.1.call-start = ((), (), s32[]{:S(2)}) async-start(), calls=%async_computation.38 | async-start | bytes 442368
  1053.4 272.9 %reduce-scatter.42.cloned.1.call-start = ((), (), s32[]{:S(2)}) async-start(), calls=%async_computation.39 | async-start | bytes 442368
  1054.4 293.6 %reduce-scatter.28.cloned.1.call-start = ((), (), s32[]{:S(2)}) async-start(), calls=%async_computation.32 | async-start | bytes 2654208 | tf_op jit(solution)/shard_map/reduce_scatter | solution.py:389
  1059.1 292.5 %reduce-scatter.26.cloned.1.call-start = ((), (), s32[]{:S(2)}) async-start(), calls=%async_computation.31 | async-start | bytes 2654208 | tf_op jit(solution)/shard_map/reduce_scatter | solution.py:387
  1151.9 47.3 %all-to-all-start.5 = ((bf16[8,128,768]{1,2,0:T(8,128)(2,1)}), bf16[8,128,768]{1,2,0:T(8,128)(2,1)}, u32[]{:S(2)}, u32[]{:S(2)}) async-start(bf16[8,128,768]{1,2,0:T(8,128)(2,1)} %pad_maximum_fusion.8), calls=%async_computation.5 | async-start | bytes 3145728 | tf_op jit(solution)/shard_map/all_to_all | solution.py:23
  1157.6 266.1 %reduce-scatter.24.cloned.1.call-start = ((), (), s32[]{:S(2)}) async-start(), calls=%async_computation.30 | async-start | bytes 2654208 | tf_op jit(solution)/shard_map/reduce_scatter | solution.py:386
  1181.0 374.6 %reduce-scatter.22.cloned.1.call-start = ((), (), s32[]{:S(2)}) async-start(), calls=%async_computation.29 | async-start | bytes 7962624 | tf_op jit(solution)/shard_map/reduce_scatter | solution.py:385
  1278.0 442.4 %reduce-scatter.30.cloned.1.call-start = ((), (), s32[]{:S(2)}) async-start(), calls=%async_computation.33 | async-start | bytes 10616832 | tf_op jit(solution)/shard_map/reduce_scatter | solution.py:390
  1293.2 591.8 %reduce-scatter.32.cloned.1.call-start = ((), (), s32[]{:S(2)}) async-start(), calls=%async_computation.34 | async-start | bytes 10616832 | tf_op jit(solution)/shard_map/reduce_scatter | solution.py:391
  1307.4 676.1 %reduce-scatter.38.cloned.1.call-start = ((), (), s32[]{:S(2)}) async-start(), calls=%async_computation.37 | async-start | bytes 5308416
  1319.7 724.6 %all-reduce.15.cloned.1.call-start = ((), (), s32[]{:S(2)}) async-start(), calls=%async_computation.40 | async-start | bytes 4915200 | tf_op jit(solution)/shard_map/psum | solution.py:399
  (186 other events, 1893.8 us)
Sparse Core Ops, SparseCore 0:
  10.2 54.5 all-gather.18
  66.9 63.2 all-gather.14
  132.4 39.8 all-gather.16
  174.3 39.8 all-gather.22
  216.9 48.2 all-gather.20
  267.3 42.3 all-gather.24
  311.8 78.3 all-gather.26
  392.3 95.9 all-gather.28
  826.6 83.8 reduce-scatter.33
  958.5 108.4 reduce-scatter.35
  1070.8 61.3 reduce-scatter.39
  1135.3 71.9 reduce-scatter.41
  1210.7 68.5 reduce-scatter.27
  1282.7 68.8 reduce-scatter.25
  1354.9 68.7 reduce-scatter.23
  1427.2 128.3 reduce-scatter.21
  1559.0 161.2 reduce-scatter.29
  1723.8 161.1 reduce-scatter.31
  1888.7 94.7 reduce-scatter.37
  1987.3 56.9 all-reduce.14
where the time goes:
time: 2070 us; the launch traced here: 2060 us
  waiting for transfers between devices  750 us (36%)
  matrix products  651 us (31%)
  local copies, waits for them, and re-layouts  233 us (11%)
  blocking collectives  231 us (11%)
  other arithmetic  165 us (8%)
    reduce_scatter x1, waiting for transfers between devices, on_device(): lax.psum_scatter(gradients[5], 'fsdp', scatter_dimension=0, tiled=True)  163 us
    reduce_scatter x1, waiting for transfers between devices, on_device(): lax.psum_scatter(gradients[6], 'fsdp', scatter_dimension=0, tiled=True)  163 us
    reduce_scatter x1, waiting for transfers between devices, on_device(): lax.psum_scatter(gradients[0], 'fsdp', scatter_dimension=0, tiled=True)  130 us
    unnamed x25, waiting for transfers between devices  101 us
    dot_general x13, matrix products, product(): return jnp.dot(left, right, preferred_element_type=jnp.float32)  77.9 us
    all_gather x2, blocking collectives, micro_step(): lax.all_gather(prompt_keys, 'fsdp', axis=0, tiled=True)  73.3 us
    all_gather x2, blocking collectives, micro_step(): lax.all_gather(prompt_values, 'fsdp', axis=0, tiled=True)  71.4 us
    dot_general x4, matrix products, attention_grads(): jnp.einsum('qhe,khe->hqk', grad_heads, value_heads, preferred_element_typ...  71 us
  transfers between devices with their start and end apart: 23, of which 9 were waited for; matrix products, arithmetic and copies ran while one was open for 40% of the time, Pallas kernels for 0%

commit v1 on v0

v1 whole, which is shorter than its diff:
```python
import jax
import jax.numpy as jnp
from jax import lax
from jax.sharding import PartitionSpec as P

HEAD_DIM = 64
SCALE = 0.125
EPS = 1e-05
MASKED = -1e30
BF = jnp.bfloat16
F32 = jnp.float32


def mm(a, b):
    return jnp.dot(a, b, preferred_element_type=F32)


def mm_tn(a, b):
    return lax.dot_general(a, b, (((0,), (0,)), ((), ())), preferred_element_type=F32)


def mm_nt(a, b):
    return lax.dot_general(a, b, (((1,), (1,)), ((), ())), preferred_element_type=F32)


def swap(value, axis):
    return lax.ppermute(value, axis, [(0, 1), (1, 0)])


def half_rows(value):
    half = value.shape[0] // 2
    return lax.dynamic_slice_in_dim(value, lax.axis_index("seq") * half, half, 0)


def gather_rows(shard):
    return lax.all_gather(half_rows(shard), ("fsdp", "seq"), axis=0, tiled=True)


def both_halves(mine):
    other = swap(mine, "seq")
    first = lax.axis_index("seq") == 0
    low = jnp.where(first, mine, other)
    high = jnp.where(first, other, mine)
    return low, high


def reduce_rows(grad):
    part = lax.psum_scatter(grad.astype(BF), ("fsdp", "seq"), scatter_dimension=0, tiled=True)
    total = (part.astype(F32) + swap(part, "grp").astype(F32)).astype(BF)
    return jnp.concatenate(both_halves(total), 0).astype(F32)


def norm_stats(resid):
    average = jnp.mean(resid, axis=-1, keepdims=True)
    centred = resid - average
    variance = jnp.mean(centred * centred, axis=-1, keepdims=True)
    scale = lax.rsqrt(variance + EPS)
    return centred * scale, scale


def norm_back(grad, hat, scale, gain):
    weighted = grad * gain
    first = jnp.mean(weighted, axis=-1, keepdims=True)
    second = jnp.mean(weighted * hat, axis=-1, keepdims=True)
    back = scale * (weighted - first - hat * second)
    return back, jnp.sum(grad * hat, axis=0), jnp.sum(grad, axis=0)


def heads(value):
    return value.reshape(value.shape[0], -1, HEAD_DIM)


def attend(queries, keys, values, allowed):
    scores = jnp.einsum("qhe,khe->hqk", heads(queries), heads(keys), preferred_element_type=F32)
    scores = jnp.where(allowed, scores * SCALE, MASKED)
    top = jnp.max(scores, axis=-1, keepdims=True)
    raised = jnp.exp(scores - top)
    total = jnp.sum(raised, axis=-1, keepdims=True)
    out = jnp.einsum(
        "hqk,khe->qhe", raised.astype(BF), heads(values), preferred_element_type=F32
    )
    out = out / jnp.transpose(total, (1, 0, 2))
    return out.reshape(queries.shape).astype(BF), top + jnp.log(total)


def attend_back(queries, keys, values, allowed, out, grad, log_sum):
    scores = jnp.einsum("qhe,khe->hqk", heads(queries), heads(keys), preferred_element_type=F32)
    prob = jnp.exp(jnp.where(allowed, scores * SCALE, MASKED) - log_sum)
    grad_prob = jnp.einsum("qhe,khe->hqk", heads(grad), heads(values), preferred_element_type=F32)
    delta = jnp.sum(heads(grad).astype(F32) * heads(out).astype(F32), axis=-1).T[..., None]
    grad_score = (prob * (grad_prob - delta)).astype(BF)
    grad_q = jnp.einsum("hqk,khe->qhe", grad_score, heads(keys), preferred_element_type=F32)
    grad_k = jnp.einsum("hqk,qhe->khe", grad_score, heads(queries), preferred_element_type=F32)
    grad_v = jnp.einsum("hqk,qhe->khe", prob.astype(BF), heads(grad), preferred_element_type=F32)
    return (
        (grad_q * SCALE).reshape(queries.shape),
        (grad_k * SCALE).reshape(keys.shape),
        grad_v.reshape(values.shape),
    )


def self_masks(prompt_len, cont_len, reach):
    key = lax.iota(jnp.int32, prompt_len)[None, :]
    seen = jnp.broadcast_to(key < reach, (cont_len, prompt_len))
    own = lax.iota(jnp.int32, cont_len)
    return jnp.concatenate([seen, own[None, :] <= own[:, None]], 1)[None]


def self_forward(joined, prompt_kv, reach, place, conts):
    width = joined.shape[2] // 3
    cont_len = conts[2]
    half = cont_len // 2
    prompt_len = prompt_kv.shape[0]
    outs, sums = [], []
    for c in range(conts[1]):
        rows = joined[:, c * half : (c + 1) * half].reshape(cont_len, -1)
        keys = jnp.concatenate([prompt_kv[:, :width], rows[:, width : 2 * width]], 0)
        values = jnp.concatenate([prompt_kv[:, width:], rows[:, 2 * width :]], 0)
        out, log_sum = attend(rows[:, :width], keys, values, self_masks(prompt_len, cont_len, reach[c]))
        outs.append(out.reshape(2, half, width))
        sums.append(log_sum)
    rows = joined[:, conts[1] * half :].reshape(-1, 3 * width)
    allowed = lax.iota(jnp.int32, prompt_len)[None, None, :] <= place[None, :, None]
    out, log_sum = attend(rows[:, :width], prompt_kv[:, :width], prompt_kv[:, width:], allowed)
    outs.append(out.reshape(2, -1, width))
    sums.append(log_sum)
    return jnp.concatenate(outs, 1), tuple(sums)


def self_backward(joined, prompt_kv, reach, place, conts, out, grad, sums):
    width = joined.shape[2] // 3
    cont_len = conts[2]
    half = cont_len // 2
    prompt_len = prompt_kv.shape[0]
    pieces = []
    total_kv = 0.0
    for c in range(conts[1]):
        span = slice(c * half, (c + 1) * half)
        rows = joined[:, span].reshape(cont_len, -1)
        keys = jnp.concatenate([prompt_kv[:, :width], rows[:, width : 2 * width]], 0)
        values = jnp.concatenate([prompt_kv[:, width:], rows[:, 2 * width :]], 0)
        grad_q, grad_k, grad_v = attend_back(
            rows[:, :width],
            keys,
            values,
            self_masks(prompt_len, cont_len, reach[c]),
            out[:, span].reshape(cont_len, width),
            grad[:, span].reshape(cont_len, width),
            sums[c],
        )
        total_kv = total_kv + jnp.concatenate([grad_k[:prompt_len], grad_v[:prompt_len]], 1)
        piece = jnp.concatenate([grad_q, grad_k[prompt_len:], grad_v[prompt_len:]], 1)
        pieces.append(piece.astype(BF).reshape(2, half, 3 * width))
    start = conts[1] * half
    rows = joined[:, start:].reshape(-1, 3 * width)
    allowed = lax.iota(jnp.int32, prompt_len)[None, None, :] <= place[None, :, None]
    grad_q, grad_k, grad_v = attend_back(
        rows[:, :width],
        prompt_kv[:, :width],
        prompt_kv[:, width:],
        allowed,
        out[:, start:].reshape(-1, width),
        grad[:, start:].reshape(-1, width),
        sums[-1],
    )
    total_kv = total_kv + jnp.concatenate([grad_k, grad_v], 1)
    zero = jnp.zeros((2, rows.shape[0] // 2, 2 * width), BF)
    pieces.append(jnp.concatenate([grad_q.astype(BF).reshape(2, -1, width), zero], 2))
    return jnp.concatenate(pieces, 1), total_kv.astype(BF)


def cross_forward(queries, enc_kv):
    width = queries.shape[1]
    return attend(queries, enc_kv[:, :width], enc_kv[:, width:], True)


def cross_backward(queries, enc_kv, out, grad, log_sum):
    width = queries.shape[1]
    grad_q, grad_k, grad_v = attend_back(
        queries, enc_kv[:, :width], enc_kv[:, width:], True, out, grad, log_sum
    )
    return grad_q.astype(BF), jnp.concatenate([grad_k, grad_v], 1).astype(BF)


def exchange(value):
    return lax.all_to_all(value, "seq", split_axis=0, concat_axis=0, tiled=True)


def on_device(
    prompt_in,
    cont_in,
    enc_in,
    prefix,
    cot_prompt,
    cot_cont,
    w_qkv,
    w_attn_out,
    w_cross_q,
    w_cross_kv,
    w_cross_out,
    w_ffn_in,
    w_ffn_out,
    norm_gain,
    norm_bias,
):
    seq = lax.axis_index("seq")
    width = w_qkv.shape[1] // 3
    hg = width // 2
    shard = w_qkv.shape[0]
    rows_p = prompt_in.shape[1]
    count = cont_in.shape[1]
    half = cont_in.shape[2]
    rows_c = count * half
    conts = (rows_c, count, 2 * half)
    reach = prefix[0]

    own_cols = lax.dynamic_slice_in_dim(w_qkv.reshape(shard, 3, 2, hg), seq, 1, 2)
    wq = lax.all_gather(own_cols.reshape(shard, 3 * hg), "fsdp", axis=0, tiled=True)
    shared = lax.all_gather(
        jnp.concatenate([prompt_in[0], enc_in[0]], 0), ("fsdp", "seq"), axis=0
    )
    prompt_all = shared[:, :rows_p].reshape(-1, width)
    enc_all = shared[:, rows_p:].reshape(-1, width)
    norms = jnp.concatenate([norm_gain, norm_bias], 0).T
    norms = jnp.pad(norms, ((0, 0), (0, 128 - norms.shape[1])))
    mixed = gather_rows(jnp.concatenate([w_attn_out, w_cross_q, w_cross_out, w_cross_kv, norms], 1))
    wo = mixed[:, :width]
    wcq = mixed[:, width : 2 * width]
    wco = mixed[:, 2 * width : 3 * width]
    wckv = mixed[:, 3 * width : 5 * width]
    norms = mixed[:, 5 * width :].astype(F32).T
    w1 = gather_rows(w_ffn_in)
    w2 = gather_rows(w_ffn_out)

    mine = jnp.concatenate([cont_in[0].reshape(rows_c, width), prompt_in[0]], 0)
    x_low, x_high = both_halves(mine)
    x_all = jnp.stack([x_low, x_high], 0)
    joined = lax.dot_general(
        x_all, wq, (((2,), (0,)), ((), ())), preferred_element_type=F32
    ).astype(BF)
    prompt_kv = mm(prompt_all, wq[:, hg:]).astype(BF)
    place = lax.axis_index("fsdp") * (2 * rows_p) + lax.iota(jnp.int32, 2 * rows_p)
    att, sums = self_forward(joined, prompt_kv, reach, place, conts)
    att = att
    att_rows = exchange(att)
    proj = mm(att_rows[0], wo[:hg]) + mm(att_rows[1], wo[hg:])
    hat1, scale1 = norm_stats(mine.astype(F32) + proj)
    first = hat1 * norms[0] + norms[3]
    first_low = first.astype(BF)
    cq = mm(first_low, wcq).astype(BF)
    enc_kv = mm(enc_all, wckv).astype(BF)
    cross, cross_sum = cross_forward(cq, enc_kv)
    hat2, scale2 = norm_stats(first + mm(cross, wco))
    second = hat2 * norms[1] + norms[4]
    second_low = second.astype(BF)
    pre = mm(second_low, w1)
    gate = 0.5 * (1.0 + lax.erf(pre * 0.7071067811865476))
    act = (pre * gate).astype(BF)
    slope = (gate + pre * jnp.exp(-0.5 * pre * pre) * 0.3989422804014327).astype(BF)
    hat3, scale3 = norm_stats(second + mm(act, w2))
    third = (hat3 * norms[2] + norms[5]).astype(BF)

    cot = jnp.concatenate([cot_cont[0].reshape(rows_c, width), cot_prompt[0]], 0).astype(F32)
    grad3, gain3, bias3 = norm_back(cot, hat3, scale3, norms[2])
    low3 = grad3.astype(BF)
    g_w2 = reduce_rows(mm_tn(act, low3))
    grad_pre = (mm_nt(low3, w2) * slope.astype(F32)).astype(BF)
    g_w1 = reduce_rows(mm_tn(second_low, grad_pre))
    grad_second = grad3 + mm_nt(grad_pre, w1)
    grad2, gain2, bias2 = norm_back(grad_second, hat2, scale2, norms[1])
    low2 = grad2.astype(BF)
    g_wco = mm_tn(cross, low2)
    grad_cross = mm_nt(low2, wco).astype(BF)
    grad_cq, enc_terms = cross_backward(cq, enc_kv, cross, grad_cross, cross_sum)
    grad_ekv = lax.psum_scatter(enc_terms, ("fsdp", "seq"), scatter_dimension=0, tiled=True)
    g_wckv = mm_tn(enc_in[0], grad_ekv)
    grad_enc = mm_nt(grad_ekv, wckv)
    g_wcq = mm_tn(first_low, grad_cq)
    grad_first = grad2 + mm_nt(grad_cq, wcq)
    grad1, gain1, bias1 = norm_back(grad_first, hat1, scale1, norms[0])
    low1 = grad1.astype(BF)
    g_wo = jnp.concatenate([mm_tn(att_rows[0], low1), mm_tn(att_rows[1], low1)], 0)
    g_norms = jnp.stack([gain1, gain2, gain3, bias1, bias2, bias3], 1)
    g_norms = jnp.pad(g_norms, ((0, 0), (0, 122)))
    g_mixed = reduce_rows(jnp.concatenate([g_wo, g_wcq, g_wco, g_wckv, g_norms], 1))
    grad_att = jnp.stack([mm_nt(low1, wo[:hg]), mm_nt(low1, wo[hg:])], 0).astype(BF)
    grad_att = exchange(grad_att)
    grad_joined, grad_pkv = self_backward(
        joined, prompt_kv, reach, place, conts, att, grad_att, sums
    )
    g_wq = lax.dot_general(
        x_all, grad_joined, (((0, 1), (0, 1)), ((), ())), preferred_element_type=F32
    )
    g_wkv = mm_tn(prompt_all, grad_pkv)
    g_wq = g_wq + jnp.pad(g_wkv, ((0, 0), (hg, 0)))
    part = lax.psum_scatter(g_wq.astype(BF), "fsdp", scatter_dimension=0, tiled=True)
    part = (part.astype(F32) + swap(part, "grp").astype(F32)).astype(BF)
    q_low, q_high = both_halves(part)
    g_qkv = jnp.stack([q_low.reshape(shard, 3, hg), q_high.reshape(shard, 3, hg)], 2)
    g_qkv = g_qkv.reshape(shard, 3 * width).astype(F32)
    grad_x = lax.dot_general(
        grad_joined, wq, (((2,), (1,)), ((), ())), preferred_element_type=F32
    ).astype(BF)
    grad_x = exchange(grad_x)
    grad_in = grad1 + grad_x[0].astype(F32) + grad_x[1].astype(F32)
    grad_pr = lax.psum_scatter(
        mm_nt(grad_pkv, wq[:, hg:]).astype(BF), ("fsdp", "seq"), scatter_dimension=0, tiled=True
    )
    grad_prompt = grad_in[rows_c:] + grad_pr.astype(F32)

    g_norms = g_mixed[:, 5 * width :]
    return (
        third[rows_c:][None],
        third[:rows_c].reshape(cont_in.shape),
        grad_prompt[None],
        grad_in[:rows_c].reshape(cont_in.shape),
        grad_enc[None],
        g_qkv,
        g_mixed[:, :width],
        g_mixed[:, width : 2 * width],
        g_mixed[:, 3 * width : 5 * width],
        g_mixed[:, 2 * width : 3 * width],
        g_w1,
        g_w2,
        g_norms[:, :3].T,
        g_norms[:, 3:6].T,
    )


def solution(mesh):
    rows = P("grp", ("fsdp", "seq"), None)
    conts = P("grp", "fsdp", "seq", None)
    weight = P("fsdp", None)
    norm = P(None, "fsdp")
    return jax.shard_map(
        on_device,
        mesh=mesh,
        in_specs=(rows, conts, rows, P("grp", "fsdp"), rows, conts) + (weight,) * 7 + (norm,) * 2,
        out_specs=(rows, conts, rows, conts, rows) + (weight,) * 7 + (norm,) * 2,
        check_vma=False,
    )
```

time: 2070 us -> 1180 us (0.57)
  waiting for transfers between devices: 750 us -> 336 us
  blocking collectives: 231 us -> 12.4 us
  matrix products: 651 us -> 529 us
  local copies, waits for them, and re-layouts: 233 us -> 154 us
  other arithmetic: 165 us -> 118 us
    reduce_scatter x6 -> x5, waiting for transfers between devices: 528 us -> 268 us  [the longest x3 230 us: reduce_rows(): lax.psum_scatter(grad.astype(BF), ('fsdp', 'seq'), scatter_dimension=0, t...]
    all_gather x6 -> x0, blocking collectives: 180 us -> none  [the longest x2 73.3 us: micro_step(): lax.all_gather(prompt_keys, 'fsdp', axis=0, tiled=True)]
    unnamed x25 -> x12, waiting for transfers between devices: 101 us -> 0.18 us
    dot_general x75 -> x51, matrix products: 622 us -> 529 us  [the longest x4 91.2 us: attend_back(): jnp.einsum('qhe,khe->hqk', heads(grad), heads(values), preferred_element_...]
    convert_element_type x18 -> x10, other arithmetic: 71 us -> 8.94 us  [the longest x3 2.7 us: reduce_rows(): return jnp.concatenate(both_halves(total), 0).astype(F32)]
    reshape x30 -> x1, local copies, waits for them, and re-layouts: 61 us -> 1.27 us  [on_device(): w_qkv.reshape(shard, 3, 2, hg)]
    psum x1 -> x0, waiting for transfers between devices: 51.3 us -> none  [on_device(): lax.psum(shard_grads[0].astype(jnp.bfloat16), ('grp', 'seq'))]
    concatenate x5 -> x17, local copies, waits for them, and re-layouts: 2.87 us -> 35.3 us  [the longest x12 33.9 us: self_backward(): jnp.concatenate([grad_q, grad_k[prompt_len:], grad_v[prompt_len:]], 1)]
  transfers between devices with their start and end apart: 23 -> 21, of which waited for: 9 -> 9; matrix products, arithmetic and copies ran while one was open for 40% -> 39% of each run, Pallas kernels for 0% -> 0%
where the time goes in v1:
time: 1180 us
  matrix products  529 us (45%)
  waiting for transfers between devices  336 us (28%)
  local copies, waits for them, and re-layouts  154 us (13%)
  other arithmetic  118 us (10%)
  between operations  15.9 us (1%)
  starting transfers between devices  12.4 us (1%)
  blocking collectives  12.4 us (1%)
    reduce_scatter x3, waiting for transfers between devices, reduce_rows(): lax.psum_scatter(grad.astype(BF), ('fsdp', 'seq'), scatter_dimension=0, t...  230 us
    dot_general x4, matrix products, attend_back(): jnp.einsum('qhe,khe->hqk', heads(grad), heads(values), preferred_element_...  91.2 us
    reduce_sum x4, other arithmetic, attend(): total = jnp.sum(raised, axis=-1, keepdims=True)  68.6 us
    dot_general x4, matrix products, attend_back(): jnp.einsum('hqk,qhe->khe', prob.astype(BF), heads(grad), preferred_elemen...  68.2 us
    dot_general x4, matrix products, attend(): jnp.einsum('qhe,khe->hqk', heads(queries), heads(keys), preferred_element...  67 us
    dot_general x4, matrix products, attend(): jnp.einsum('hqk,khe->qhe', raised.astype(BF), heads(values), preferred_el...  62.2 us
    dot_general x8, matrix products, mm_nt(): lax.dot_general(a, b, (((1,), (1,)), ((), ())), preferred_element_type=F32)  52.7 us
    unnamed x248, local copies, waits for them, and re-layouts  50.9 us
  transfers between devices with their start and end apart: 21, of which 9 were waited for; matrix products, arithmetic and copies ran while one was open for 39% of the time, Pallas kernels for 0%

profile of v1, /device:TPU:0, one launch (start us, length us, event | category | flops | bytes accessed | tf_op | source)
XLA Modules:
  0.0 1177.6 jit_solution(16537911522550016725)
XLA Ops:
  29.9 29.6 %all-gather.7.cloned.1.call-done = bf16[768,1152]{1,0:T(8,128)(2,1)} async-done(((bf16[96,1152]{1,0:T(8,128)(2,1)}), bf16[768,1152]{1,0:T(8,128)(2,1)}) %all-gather.7.cloned.1.call-update) | async-done | bytes 1769488 | tf_op jit(solution)/shard_map/all_gather | solution.py:218
  83.0 23.5 %all-gather.15.cloned.1.call-done = bf16[2048,768]{1,0:T(8,128)(2,1)} async-done(((bf16[128,768]{1,0:T(8,128)(2,1)}), bf16[2048,768]{1,0:T(8,128)(2,1)}) %all-gather.15.cloned.1.call-update) | async-done | bytes 3145744 | tf_op jit(solution)/shard_map/all_gather | solution.py:219
  119.3 23.3 %fusion.14 = (f32[6,1024]{1,0:T(8,128)S(1)}, f32[6,1024,2048]{2,1,0:T(8,128)}) fusion(pred[1024,2048]{1,0:T(8,128)(4,1)} %get-tuple-element.130, bf16[1024,6,64]{0,2,1:T(8,128)(2,1)S(1)} %bitcast.296, bf16[2048,6,64]{0,2,1:T(8,128)(2,1)} %bitcast.288), kind=kOutput, calls=%fused_computation.24 | convolution fusion | flops 1648355328 | bytes 54812672 | tf_op jit(solution)/shard_map/qhe,khe->hqk/dot_general | solution.py:74
  142.6 23.0 %fusion.5 = f32[6,1024]{1,0:T(8,128)S(1)} fusion(f32[6,1024,2048]{2,1,0:T(8,128)} %get-tuple-element.146, f32[6,1024]{1,0:T(8,128)S(1)} %get-tuple-element.145, pred[1024,2048]{1,0:T(8,128)(4,1)S(1)} %copy-done.22), kind=kLoop, calls=%fused_computation.16 | loop fusion | flops 50325504 | bytes 52477952 | tf_op jit(solution)/shard_map/reduce_sum | solution.py:78
  166.2 20.2 %fusion.80 = bf16[1024,6,64]{0,2,1:T(8,128)(2,1)S(1)} fusion(bf16[2048,6,64]{0,2,1:T(8,128)(2,1)} %bitcast.310, f32[6,1024,2048]{2,1,0:T(8,128)} %get-tuple-element.146, f32[6,1024]{1,0:T(8,128)S(1)} %get-tuple-element.145, pred[1024,2048]{1,0:T(8,128)(4,1)} %get-tuple-element.130, f32[1024,6]{0,1:T(8,128)S(1)} %bitcast.325), kind=kOutput, calls=%fused_computation.152 | convolution fusion | flops 1661730816 | bytes 54837248 | tf_op jit(solution)/shard_map/hqk,khe->qhe/dot_general | solution.py:79
  190.9 22.6 %fusion.13 = (f32[6,1024]{1,0:T(8,128)S(1)}, f32[6,1024,2048]{2,1,0:T(8,128)}) fusion(pred[1024,2048]{1,0:T(8,128)(4,1)S(1)} %copy-done.20, bf16[1024,6,64]{0,2,1:T(8,128)(2,1)} %bitcast.294, bf16[2048,6,64]{0,2,1:T(8,128)(2,1)} %bitcast.286), kind=kOutput, calls=%fused_computation.23 | convolution fusion | flops 1648355328 | bytes 54812672 | tf_op jit(solution)/shard_map/qhe,khe->hqk/dot_general | solution.py:74
  213.5 22.9 %fusion.3 = f32[6,1024]{1,0:T(8,128)S(1)} fusion(f32[6,1024,2048]{2,1,0:T(8,128)} %get-tuple-element.148, f32[6,1024]{1,0:T(8,128)S(1)} %get-tuple-element.147, pred[1024,2048]{1,0:T(8,128)(4,1)S(1)} %copy-done.20), kind=kLoop, calls=%fused_computation.14 | loop fusion | flops 50325504 | bytes 52477952 | tf_op jit(solution)/shard_map/reduce_sum | solution.py:78
  237.0 20.1 %fusion.81 = bf16[1024,6,64]{0,2,1:T(8,128)(2,1)S(1)} fusion(bf16[2048,6,64]{0,2,1:T(8,128)(2,1)} %bitcast.308, f32[6,1024,2048]{2,1,0:T(8,128)} %get-tuple-element.148, f32[6,1024]{1,0:T(8,128)S(1)} %get-tuple-element.147, pred[1024,2048]{1,0:T(8,128)(4,1)S(1)} %copy-done.20, f32[1024,6]{0,1:T(8,128)S(1)} %bitcast.324), kind=kOutput, calls=%fused_computation.154 | convolution fusion | flops 1661730816 | bytes 54837248 | tf_op jit(solution)/shard_map/hqk,khe->qhe/dot_general | solution.py:79
  295.7 20.3 %multiply_reduce_fusion = (f32[12,1088]{1,0:T(8,128)S(1)}, f32[12,1088,1024]{2,1,0:T(8,128)}) fusion(bf16[1088,12,64]{0,2,1:T(8,128)(2,1)} %bitcast.261, bf16[1024,12,64]{0,2,1:T(8,128)(2,1)S(1)} %bitcast.259), kind=kOutput, calls=%fused_computation.20 | convolution fusion | flops 1738001664 | bytes 56773632 | tf_op jit(solution)/shard_map/qhe,khe->hqk/dot_general | solution.py:74
  316.0 21.9 %fusion = f32[12,1088]{1,0:T(8,128)S(1)} fusion(f32[12,1088,1024]{2,1,0:T(8,128)} %get-tuple-element.152, f32[12,1088]{1,0:T(8,128)S(1)} %get-tuple-element.151), kind=kLoop, calls=%fused_computation.11 | loop fusion | flops 40094976 | bytes 53581824 | tf_op jit(solution)/shard_map/reduce_sum | solution.py:78
  337.9 21.1 %divide_convert_fusion = bf16[1088,12,64]{0,2,1:T(8,128)(2,1)} fusion(bf16[1024,12,64]{0,2,1:T(8,128)(2,1)S(1)} %bitcast.285, f32[12,1088,1024]{2,1,0:T(8,128)} %get-tuple-element.152, f32[12,1088]{1,0:T(8,128)S(1)} %get-tuple-element.151, f32[1088,12]{0,1:T(8,128)S(1)} %bitcast.323), kind=kOutput, calls=%fused_computation.70 | convolution fusion | flops 1753055232 | bytes 56825856 | tf_op jit(solution)/shard_map/hqk,khe->qhe/dot_general | solution.py:79
  366.3 12.4 %multiply_convert_fusion.3 = (bf16[1088,3072]{1,0:T(8,128)(2,1)}, f32[1088,3072]{1,0:T(8,128)}) fusion(bf16[768,3072]{1,0:T(8,128)(2,1)} %all-gather.11.cloned.1.call-done, f32[1088,768]{1,0:T(8,128)} %copy-done.11, f32[768]{0:T(1024)S(1)} %get-tuple-element.97, f32[768]{0:T(1024)S(1)} %get-tuple-element.98, f32[1088]{0:T(1024)S(1)} %add_rsqrt_fusion.1, ...), kind=kOutput, calls=%fused_computation.40 | convolution fusion | flops 5154717696 | bytes 28129792 | tf_op jit(solution)/shard_map/dot_general | solution.py:15
  378.7 11.1 fusion.157
  396.8 17.8 %fusion.32 = bf16[1088,3072]{1,0:T(8,128)(2,1)} fusion(bf16[3072,768]{1,0:T(8,128)(2,1)S(1)} %copy-done.112, f32[1088,3072]{1,0:T(8,128)} %get-tuple-element.156, f32[1088,768]{1,0:T(8,128)S(1)} %get-tuple-element.158, f32[1088]{0:T(1024)S(1)} %broadcast_multiply_fusion.4, f32[1088]{0:T(1024)S(1)} %broadcast_multiply_fusion.5, ...), kind=kOutput, calls=%fused_computation.42 | convolution fusion | flops 5183963136 | bytes 29806592 | tf_op jit(solution)/shard_map/dot_general | solution.py:23
  414.6 11.8 %multiply_reduce_fusion.2 = (bf16[768]{0:T(1024)(128)(2,1)}, f32[1088]{0:T(1024)S(1)}, f32[1088]{0:T(1024)S(1)}, bf16[768]{0:T(1024)(128)(2,1)}, f32[1088,768]{1,0:T(8,128)S(1)}) fusion(f32[1088,768]{1,0:T(8,128)S(1)} %copy-done.12, f32[1088]{0:T(1024)S(1)} %add_rsqrt_fusion.1, f32[1088]{0:T(1024)S(1)} %broadcast_multiply_fusion.7, ...), kind=kOutput, calls=%fused_computation.83 | convolution fusion | flops 5151371264 | bytes 23145472 | tf_op jit(solution)/shard_map/dot_general | solution.py:23
  438.1 21.8 %fusion.73 = bf16[12,64,1024]{2,1,0:T(8,128)(2,1)} fusion(bf16[1088,12,64]{0,2,1:T(8,128)(2,1)S(1)} %bitcast.257, f32[12,1088,1024]{2,1,0:T(8,128)} %get-tuple-element.152, f32[12,1088]{1,0:T(8,128)S(1)} %log_add_fusion), kind=kOutput, calls=%fused_computation.134 | convolution fusion | flops 1752170496 | bytes 56773632 | tf_op jit(solution)/shard_map/hqk,qhe->khe/dot_general | solution.py:94
  459.8 28.3 %multiply_convert_fusion = bf16[12,1088,1024]{2,1,0:T(8,128)(2,1)} fusion(f32[12,1088,1024]{2,1,0:T(8,128)} %get-tuple-element.152, bf16[1088,12,64]{0,2,1:T(8,128)(2,1)S(1)} %bitcast.258, bf16[1024,12,64]{0,2,1:T(8,128)(2,1)} %bitcast.284, f32[12,1088]{1,0:T(8,128)S(1)} %bitcast.316, f32[12,1088]{1,0:T(8,128)S(1)} %log_add_fusion), kind=kOutput, calls=%fused_computation | convolution fusion | flops 1778122752 | bytes 83564544 | tf_op jit(solution)/shard_map/qhe,khe->hqk/dot_general | solution.py:89
  488.2 15.5 %multiply_convert_fusion.4 = bf16[12,64,1024]{2,1,0:T(8,128)(2,1)} fusion(bf16[1088,12,64]{0,2,1:T(8,128)(2,1)} %bitcast.262, bf16[12,1088,1024]{2,1,0:T(8,128)(2,1)} %multiply_convert_fusion), kind=kOutput, calls=%fused_computation.99 | convolution fusion | flops 1712848896 | bytes 29982720 | tf_op jit(solution)/shard_map/hqk,qhe->khe/dot_general | solution.py:93
  503.6 14.5 %fusion.43 = bf16[12,64,1088]{2,1,0:T(8,128)(2,1)} fusion(bf16[1024,12,64]{0,2,1:T(8,128)(2,1)S(1)} %bitcast.260, bf16[12,1088,1024]{2,1,0:T(8,128)(2,1)} %multiply_convert_fusion), kind=kOutput, calls=%fused_computation.71 | convolution fusion | flops 1712947200 | bytes 29982720 | tf_op jit(solution)/shard_map/hqk,khe->qhe/dot_general | solution.py:92
  548.6 21.7 %fusion.56 = f32[2048,6,64]{0,2,1:T(8,128)} fusion(bf16[1024,6,64]{0,2,1:T(8,128)(2,1)} %reshape_reshape.7, f32[6,1024,2048]{2,1,0:T(8,128)} %get-tuple-element.146, f32[6,1024]{1,0:T(8,128)S(1)} %copy-done.89, pred[1024,2048]{1,0:T(8,128)(4,1)S(1)} %copy-done.23), kind=kOutput, calls=%fused_computation.110 | convolution fusion | flops 1660944384 | bytes 56385536 | tf_op jit(solution)/shard_map/hqk,qhe->khe/dot_general | solution.py:94
  570.3 30.0 %multiply_convert_fusion.1 = bf16[6,1024,2048]{2,1,0:T(8,128)(2,1)} fusion(f32[6,1024,2048]{2,1,0:T(8,128)} %get-tuple-element.146, f32[6,1024]{1,0:T(8,128)S(1)} %bitcast.327, f32[6,1024]{1,0:T(8,128)S(1)} %copy-done.89, pred[1024,2048]{1,0:T(8,128)(4,1)S(1)} %copy-done.23, bf16[1024,6,64]{0,2,1:T(8,128)(2,1)S(1)} %copy-done.43, ...), kind=kOutput, calls=%fused_computation.3 | convolution fusion | flops 1686110208 | bytes 80003072 | tf_op jit(solution)/shard_map/qhe,khe->hqk/dot_general | solution.py:89
  600.2 10.7 multiply_bitcast_fusion
  623.7 21.6 %fusion.53 = f32[2048,6,64]{0,2,1:T(8,128)} fusion(bf16[1024,6,64]{0,2,1:T(8,128)(2,1)} %reshape_reshape.6, f32[6,1024,2048]{2,1,0:T(8,128)} %get-tuple-element.148, f32[6,1024]{1,0:T(8,128)S(1)} %copy-done.88, pred[1024,2048]{1,0:T(8,128)(4,1)S(1)} %copy-done.21), kind=kOutput, calls=%fused_computation.109 | convolution fusion | flops 1660944384 | bytes 56385536 | tf_op jit(solution)/shard_map/hqk,qhe->khe/dot_general | solution.py:94
  645.2 29.9 %multiply_convert_fusion.2 = bf16[6,1024,2048]{2,1,0:T(8,128)(2,1)} fusion(f32[6,1024,2048]{2,1,0:T(8,128)} %get-tuple-element.148, f32[6,1024]{1,0:T(8,128)S(1)} %bitcast.328, f32[6,1024]{1,0:T(8,128)S(1)} %copy-done.88, pred[1024,2048]{1,0:T(8,128)(4,1)S(1)} %copy-done.21, bf16[1024,6,64]{0,2,1:T(8,128)(2,1)S(1)} %copy-done.44, ...), kind=kOutput, calls=%fused_computation.5 | convolution fusion | flops 1686110208 | bytes 80003072 | tf_op jit(solution)/shard_map/qhe,khe->hqk/dot_general | solution.py:89
  701.8 14.6 %fusion.91 = bf16[1024,6,64]{0,2,1:T(8,128)(2,1)} fusion(bf16[2048,6,64]{0,2,1:T(8,128)(2,1)} %bitcast.289, bf16[6,1024,2048]{2,1,0:T(8,128)(2,1)} %multiply_convert_fusion.1), kind=kOutput, calls=%fused_computation.169 | convolution fusion | flops 1611399168 | bytes 27525120 | tf_op jit(solution)/shard_map/hqk,khe->qhe/dot_general | solution.py:92
  733.5 13.8 %fusion.90 = bf16[1024,6,64]{0,2,1:T(8,128)(2,1)} fusion(bf16[2048,6,64]{0,2,1:T(8,128)(2,1)} %bitcast.287, bf16[6,1024,2048]{2,1,0:T(8,128)(2,1)} %multiply_convert_fusion.2), kind=kOutput, calls=%fused_computation.168 | convolution fusion | flops 1611399168 | bytes 27525120 | tf_op jit(solution)/shard_map/hqk,khe->qhe/dot_general | solution.py:92
  783.3 12.0 %convolution_convert_fusion.2 = bf16[768,3072]{1,0:T(8,128)(2,1)} fusion(bf16[1088,3072]{1,0:T(8,128)(2,1)} %fusion.32, f32[1088,768]{1,0:T(8,128)} %copy-done.11, f32[768]{0:T(1024)S(1)} %copy-done.106, f32[768]{0:T(1024)S(1)} %copy-done.97, f32[1088]{0:T(1024)S(1)} %copy-done.85, f32[1088]{0:T(1024)S(1)} %copy-done.78), kind=kOutput, calls=%fused_computation.49 | convolution fusion | flops 5140365312 | bytes 14760448 | tf_op jit(solution)/shard_map/dot_general | solution.py:19
  796.8 13.3 %convolution_convert_fusion.1 = bf16[3072,768]{1,0:T(8,128)(2,1)} fusion(bf16[1088,3072]{1,0:T(8,128)(2,1)} %get-tuple-element.155, f32[1088,768]{1,0:T(8,128)} %copy-done.13, f32[1088]{0:T(1024)S(1)} %copy-done.100, f32[1088]{0:T(1024)S(1)} %copy-done.102, f32[768]{0:T(1024)S(1)} %copy-done.95, f32[1088]{0:T(1024)S(1)} %copy-done.87, ...), kind=kOutput, calls=%fused_computation.48 | convolution fusion | flops 5146214400 | bytes 16437248 | tf_op jit(solution)/shard_map/dot_general | solution.py:19
  868.3 38.2 %reduce-scatter.11.cloned.1.call-done = bf16[64,768]{1,0:T(8,128)(2,1)} async-done(((bf16[1024,768]{1,0:T(8,128)(2,1)}), bf16[64,768]{1,0:T(8,128)(2,1)}) %reduce-scatter.11.cloned.1.call-update) | async-done | bytes 98320 | tf_op jit(solution)/shard_map/reduce_scatter | solution.py:306
  908.2 76.8 %reduce-scatter.15.cloned.1.call-done = bf16[48,3072]{1,0:T(8,128)(2,1)} async-done(((bf16[768,3072]{1,0:T(8,128)(2,1)}), bf16[48,3072]{1,0:T(8,128)(2,1)}) %reduce-scatter.15.cloned.1.call-update) | async-done | bytes 294928 | tf_op jit(solution)/shard_map/reduce_scatter | solution.py:48
  989.1 74.4 %reduce-scatter.17.cloned.1.call-done = bf16[192,768]{1,0:T(8,128)(2,1)} async-done(((bf16[3072,768]{1,0:T(8,128)(2,1)}), bf16[192,768]{1,0:T(8,128)(2,1)}) %reduce-scatter.17.cloned.1.call-update) | async-done | bytes 294928 | tf_op jit(solution)/shard_map/reduce_scatter | solution.py:48
  1070.9 78.7 %reduce-scatter.21.cloned.1.call-done = bf16[48,3968]{1,0:T(8,128)(2,1)} async-done(((bf16[768,3968]{1,0:T(8,128)(2,1)}), bf16[48,3968]{1,0:T(8,128)(2,1)}) %reduce-scatter.21.cloned.1.call-update) | async-done | bytes 380944 | tf_op jit(solution)/shard_map/reduce_scatter | solution.py:48
  (474 shorter events, 344.5 us)
Async XLA Ops:
  7.3 52.3 %all-gather.7.cloned.1.call-start = ((), (), s32[]{:S(2)}) async-start(), calls=%async_computation.9 | async-start | bytes 1990656 | tf_op jit(solution)/shard_map/all_gather | solution.py:218
  10.8 95.7 %all-gather.15.cloned.1.call-start = ((), (), s32[]{:S(2)}) async-start(), calls=%async_computation.17 | async-start | bytes 3342336 | tf_op jit(solution)/shard_map/all_gather | solution.py:219
  12.5 254.5 %all-gather.9.cloned.1.call-start = ((), (), s32[]{:S(2)}) async-start(), calls=%async_computation.10 | async-start | bytes 6475776 | tf_op jit(solution)/shard_map/all_gather | solution.py:36
  15.2 351.1 %all-gather.11.cloned.1.call-start = ((), (), s32[]{:S(2)}) async-start(), calls=%async_computation.11 | async-start | bytes 5013504 | tf_op jit(solution)/shard_map/all_gather | solution.py:36
  16.0 362.6 %all-gather.13.cloned.1.call-start = ((), (), s32[]{:S(2)}) async-start(), calls=%async_computation.12 | async-start | bytes 5013504 | tf_op jit(solution)/shard_map/all_gather | solution.py:36
  17.4 8.7 collective-permute-start
  262.1 18.8 %all-to-all-start = ((bf16[2,1088,384]{2,1,0:T(8,128)(2,1)}), bf16[2,1088,384]{2,1,0:T(8,128)(2,1)}, u32[]{:S(2)}, u32[]{:S(2)}) async-start(bf16[2,1088,384]{2,1,0:T(8,128)(2,1)} %pad_maximum_fusion.9), calls=%async_computation | async-start | bytes 3342336 | tf_op jit(solution)/shard_map/all_to_all | solution.py:186
  266.9 559.3 %reduce-scatter.19.cloned.1.call-start = ((), (), s32[]{:S(2)}) async-start(), calls=%async_computation.18 | async-start | bytes 3342336
  269.1 89.8 %copy-start.103 = (f32[768]{0:T(1024)}, f32[768]{0:T(1024)S(1)}, u32[]{:S(2)}) copy-start(f32[768]{0:T(1024)S(1)} %get-tuple-element.99) | copy-start | bytes 9220
  269.1 109.5 %copy-start.105 = (f32[768]{0:T(1024)}, f32[768]{0:T(1024)S(1)}, u32[]{:S(2)}) copy-start(f32[768]{0:T(1024)S(1)} %get-tuple-element.97) | copy-start | bytes 9220
  269.1 145.4 %copy-start.94 = (f32[768]{0:T(1024)}, f32[768]{0:T(1024)S(1)}, u32[]{:S(2)}) copy-start(f32[768]{0:T(1024)S(1)} %get-tuple-element.95) | copy-start | bytes 9220
  269.2 157.2 %copy-start.96 = (f32[768]{0:T(1024)}, f32[768]{0:T(1024)S(1)}, u32[]{:S(2)}) copy-start(f32[768]{0:T(1024)S(1)} %get-tuple-element.98) | copy-start | bytes 9220
  269.2 256.5 %copy-start.92 = (f32[768]{0:T(1024)}, f32[768]{0:T(1024)S(1)}, u32[]{:S(2)}) copy-start(f32[768]{0:T(1024)S(1)} %get-tuple-element.100) | copy-start | bytes 9220
  285.9 239.7 %copy-start.81 = (f32[1088]{0:T(1024)}, f32[1088]{0:T(1024)S(1)}, u32[]{:S(2)}) copy-start(f32[1088]{0:T(1024)S(1)} %broadcast_multiply_fusion.8) | copy-start | bytes 13060
  286.5 239.2 %copy-start.90 = (f32[1088]{0:T(1024)}, f32[1088]{0:T(1024)S(1)}, u32[]{:S(2)}) copy-start(f32[1088]{0:T(1024)S(1)} %add_rsqrt_fusion.2) | copy-start | bytes 13060
  363.8 62.6 %copy-start.77 = (f32[1088]{0:T(1024)}, f32[1088]{0:T(1024)S(1)}, u32[]{:S(2)}) copy-start(f32[1088]{0:T(1024)S(1)} %broadcast_multiply_fusion.7) | copy-start | bytes 13060
  366.2 60.2 %copy-start.84 = (f32[1088]{0:T(1024)}, f32[1088]{0:T(1024)S(1)}, u32[]{:S(2)}) copy-start(f32[1088]{0:T(1024)S(1)} %add_rsqrt_fusion.1) | copy-start | bytes 13060
  696.9 162.6 %reduce-scatter.13.cloned.1.call-start = ((), (), s32[]{:S(2)}) async-start(), calls=%async_computation.14 | async-start | bytes 1990656 | tf_op jit(solution)/shard_map/reduce_scatter | solution.py:296
  778.9 127.6 %reduce-scatter.11.cloned.1.call-start = ((), (), s32[]{:S(2)}) async-start(), calls=%async_computation.13 | async-start | bytes 1671168 | tf_op jit(solution)/shard_map/reduce_scatter | solution.py:306
  783.3 201.7 %reduce-scatter.15.cloned.1.call-start = ((), (), s32[]{:S(2)}) async-start(), calls=%async_computation.15 | async-start | bytes 5013504 | tf_op jit(solution)/shard_map/reduce_scatter | solution.py:48
  795.4 268.1 %reduce-scatter.17.cloned.1.call-start = ((), (), s32[]{:S(2)}) async-start(), calls=%async_computation.16 | async-start | bytes 5013504 | tf_op jit(solution)/shard_map/reduce_scatter | solution.py:48
  810.1 339.5 %reduce-scatter.21.cloned.1.call-start = ((), (), s32[]{:S(2)}) async-start(), calls=%async_computation.19 | async-start | bytes 6475776 | tf_op jit(solution)/shard_map/reduce_scatter | solution.py:48
  859.6 7.7 collective-permute-start.1
  868.2 118.2 %collective-permute-start.2 = (bf16[96,1152]{1,0:T(8,128)(2,1)S(1)}, bf16[96,1152]{1,0:T(8,128)(2,1)S(1)}, u32[]{:S(2)}, u32[]{:S(2)}) collective-permute-start(bf16[96,1152]{1,0:T(8,128)(2,1)S(1)} %add_convert_fusion.4), channel_id=1, source_target_pairs={{0,1},{1,0},{2,3},{3,2},{4,5},{5,4},{6,7},{7,6},{8,9},{9,8},{10,11... | collective-permute-start | bytes 663560 | tf_op jit(solution)/shard_map/ppermute | solution.py:27
  984.9 80.0 %collective-permute-start.5 = (bf16[48,3072]{1,0:T(8,128)(2,1)}, bf16[48,3072]{1,0:T(8,128)(2,1)S(1)}, u32[]{:S(2)}, u32[]{:S(2)}) collective-permute-start(bf16[48,3072]{1,0:T(8,128)(2,1)} %reduce-scatter.15.cloned.1.call-done), channel_id=1, source_target_pairs={{0,16},{16,0},{1,17},{17,1},{2,18},{18,2},{3,19},{19,3},{4,20},{20... | collective-permute-start | bytes 884744 | tf_op jit(solution)/shard_map/ppermute | solution.py:27
  986.5 78.5 %copy-start.71 = (bf16[48,3072]{1,0:T(8,128)(2,1)S(1)}, bf16[48,3072]{1,0:T(8,128)(2,1)}, u32[]{:S(2)}) copy-start(bf16[48,3072]{1,0:T(8,128)(2,1)} %reduce-scatter.15.cloned.1.call-done) | copy-start | bytes 884740
  986.6 78.5 %copy-start.74 = (bf16[64,1536]{1,0:T(8,128)(2,1)S(1)}, bf16[64,1536]{1,0:T(8,128)(2,1)}, u32[]{:S(2)}) copy-start(bf16[64,1536]{1,0:T(8,128)(2,1)} %reduce-scatter.19.cloned.1.call-done) | copy-start | bytes 589828
  1063.5 7.2 collective-permute-start.7
  1065.0 85.9 %collective-permute-start.6 = (bf16[48,3072]{1,0:T(8,128)(2,1)S(1)}, bf16[48,3072]{1,0:T(8,128)(2,1)S(1)}, u32[]{:S(2)}, u32[]{:S(2)}) collective-permute-start(bf16[48,3072]{1,0:T(8,128)(2,1)S(1)} %add_convert_fusion.3), channel_id=1, source_target_pairs={{0,1},{1,0},{2,3},{3,2},{4,5},{5,4},{6,7},{7,6},{8,9},{9,8},{10,11... | collective-permute-start | bytes 884744 | tf_op jit(solution)/shard_map/ppermute | solution.py:27
  1070.8 80.2 %collective-permute-start.8 = (bf16[192,768]{1,0:T(8,128)(2,1)S(1)}, bf16[192,768]{1,0:T(8,128)(2,1)S(1)}, u32[]{:S(2)}, u32[]{:S(2)}) collective-permute-start(bf16[192,768]{1,0:T(8,128)(2,1)S(1)} %add_convert_fusion.2), channel_id=1, source_target_pairs={{0,1},{1,0},{2,3},{3,2},{4,5},{5,4},{6,7},{7,6},{8,9},{9,8},{10,11... | collective-permute-start | bytes 884744 | tf_op jit(solution)/shard_map/ppermute | solution.py:27
  1149.6 9.2 collective-permute-start.3
  1161.9 2.3 collective-permute-start.4
  (108 other events, 778.2 us)
Sparse Core Ops, SparseCore 0:
  10.9 48.6 all-gather.6
  62.4 44.0 all-gather.14
  109.3 58.8 all-gather.8
  170.8 51.7 all-gather.10
  225.3 51.6 all-gather.12
  697.0 65.1 reduce-scatter.18
  779.0 65.1 reduce-scatter.12
  847.9 58.5 reduce-scatter.10
  910.4 74.5 reduce-scatter.14
  988.6 74.7 reduce-scatter.16
  1067.6 81.9 reduce-scatter.20

commit v2 on v1

v2 whole, which is shorter than its diff:
```python
import functools

import jax
import jax.numpy as jnp
from jax import lax
from jax.experimental import pallas as pl
from jax.experimental.pallas import tpu as pltpu
from jax.sharding import PartitionSpec as P

HEAD_DIM = 64
SCALE = 0.125
EPS = 1e-05
MASKED = -1e30
BF = jnp.bfloat16
F32 = jnp.float32


def mm(a, b):
    return jnp.dot(a, b, preferred_element_type=F32)


def mm_tn(a, b):
    return lax.dot_general(a, b, (((0,), (0,)), ((), ())), preferred_element_type=F32)


def mm_nt(a, b):
    return lax.dot_general(a, b, (((1,), (1,)), ((), ())), preferred_element_type=F32)


def swap(value, axis):
    return lax.ppermute(value, axis, [(0, 1), (1, 0)])


def half_rows(value):
    half = value.shape[0] // 2
    return lax.dynamic_slice_in_dim(value, lax.axis_index("seq") * half, half, 0)


def gather_rows(shard):
    return lax.all_gather(half_rows(shard), ("fsdp", "seq"), axis=0, tiled=True)


def both_halves(mine):
    other = swap(mine, "seq")
    first = lax.axis_index("seq") == 0
    low = jnp.where(first, mine, other)
    high = jnp.where(first, other, mine)
    return low, high


def scatter_sum(value):
    return lax.psum_scatter(value, ("fsdp", "seq"), scatter_dimension=0, tiled=True)


def per_owner(values):
    owners = 2 * lax.axis_size("fsdp")
    width = values[0].shape[-1]
    pieces = [v.reshape(owners, -1, width) for v in values]
    return jnp.concatenate(pieces, 1).reshape(-1, width)


def over_groups(part):
    return (part.astype(F32) + swap(part, "grp").astype(F32)).astype(BF)


def norm_stats(resid):
    average = jnp.mean(resid, axis=-1, keepdims=True)
    centred = resid - average
    variance = jnp.mean(centred * centred, axis=-1, keepdims=True)
    scale = lax.rsqrt(variance + EPS)
    return centred * scale, scale


def norm_back(grad, hat, scale, gain):
    weighted = grad * gain
    first = jnp.mean(weighted, axis=-1, keepdims=True)
    second = jnp.mean(weighted * hat, axis=-1, keepdims=True)
    back = scale * (weighted - first - hat * second)
    return back, jnp.sum(grad * hat, axis=0), jnp.sum(grad, axis=0)


def dot_nn(a, b):
    return lax.dot_general(a, b, (((1,), (0,)), ((), ())), preferred_element_type=F32)


def dot_nt(a, b):
    return lax.dot_general(a, b, (((1,), (1,)), ((), ())), preferred_element_type=F32)


def lane_masks():
    lane = lax.broadcasted_iota(jnp.int32, (1, 2 * HEAD_DIM), 1)
    low = lane < HEAD_DIM
    return low, jnp.where(low, 1.0, 0.0).astype(BF), jnp.where(low, 0.0, 1.0).astype(BF)


def forward_block(queries, segments):
    low, *masks = lane_masks()
    scaled = queries * BF(SCALE)
    outs, sums = [], []
    for mask in masks:
        own = scaled * mask
        scores = []
        for keys, _, hide in segments:
            part = dot_nt(own, keys)
            scores.append(part if hide is None else hide(part, 1))
        top = scores[0].max(axis=-1, keepdims=True)
        for part in scores[1:]:
            top = jnp.maximum(top, part.max(axis=-1, keepdims=True))
        total, out = 0.0, 0.0
        for part, (_, values, _) in zip(scores, segments):
            raised = jnp.exp(part - top)
            total = total + raised.sum(axis=-1, keepdims=True)
            out = out + dot_nn(raised.astype(BF), values)
        outs.append(out / total)
        sums.append(top + jnp.log(total))
    out = jnp.where(low, outs[0], outs[1]).astype(BF)
    return out, jnp.where(low, sums[0], sums[1])


def backward_block(queries, grad, out, log_sum, segments):
    _, *masks = lane_masks()
    scaled = queries * BF(SCALE)
    delta = (grad.astype(F32) * out.astype(F32)).T
    owns = [scaled * mask for mask in masks]
    grads = [grad * mask for mask in masks]
    own_pair = jnp.concatenate(owns, 0)
    grad_pair = jnp.concatenate(grads, 0)
    grad_q = [0.0, 0.0]
    grad_kv = []
    for keys, turned, values, hide in segments:
        probs, slopes = [], []
        for h in range(2):
            span = slice(h * HEAD_DIM, (h + 1) * HEAD_DIM)
            scores = dot_nt(keys, owns[h])
            if hide is not None:
                scores = hide(scores, 0)
            prob = jnp.exp(scores - log_sum[h : h + 1])
            grad_prob = dot_nt(values, grads[h])
            slope = prob * (grad_prob - delta[span].sum(axis=0, keepdims=True))
            slope = slope.astype(BF)
            grad_q[h] = grad_q[h] + dot_nn(turned[span], slope)
            probs.append(prob.astype(BF))
            slopes.append(slope)
        grad_kv.append(
            (
                dot_nn(jnp.concatenate(slopes, 1), own_pair),
                dot_nn(jnp.concatenate(probs, 1), grad_pair),
            )
        )
    grad_q = jnp.concatenate(grad_q, 0).T * SCALE
    return grad_q.astype(BF), grad_kv


def hide_after(limit):
    def hide(scores, axis):
        key = lax.broadcasted_iota(jnp.int32, scores.shape, axis)
        return jnp.where(key < limit, scores, MASKED)

    return hide


def hide_future(start):
    def hide(scores, axis):
        key = lax.broadcasted_iota(jnp.int32, scores.shape, axis)
        query = lax.broadcasted_iota(jnp.int32, scores.shape, 1 - axis)
        return jnp.where(key <= query + start, scores, MASKED)

    return hide


def store_sums(ref, log_sum):
    turned = log_sum.T
    ref[0, 0, 0:1, : turned.shape[1]] = turned[0:1]
    ref[0, 0, 1:2, : turned.shape[1]] = turned[HEAD_DIM : HEAD_DIM + 1]


def own_spans(pos, block, half):
    spans = []
    for j in range(pos + 1):
        spans.append((j * block // half, j * block % half, block, j == pos))
    merged = []
    for span in spans:
        if merged and not span[3] and merged[-1][0] == span[0]:
            last = merged.pop()
            span = (last[0], last[1], last[2] + span[2], False)
        merged.append(span)
    return merged


def self_forward_kernel(
    info, q_ref, k_ref, v_ref, pk_ref, pv_ref, out_ref, sum_ref, *, half, count, rows_p, block
):
    step = pl.program_id(1)
    per = 2 * half // block
    for pos in range(per):

        @pl.when((step < count * per) & (lax.rem(step, per) == pos))
        def _():
            c = lax.div(step, per)
            base = pl.multiple_of(c * half, half)
            segments = [(pk_ref[...], pv_ref[...], hide_after(info[c]))]
            for source, offset, size, last in own_spans(pos, block, half):
                rows = pl.ds(base + offset, size)
                segments.append(
                    (k_ref[source, rows, :], v_ref[source, rows, :], hide_future(0) if last else None)
                )
            rows = pl.ds(base + pos * block % half, block)
            source = pos * block // half
            out, log_sum = forward_block(q_ref[source, rows, :], segments)
            out_ref[source, rows, :] = out
            store_sums(sum_ref, log_sum)

    @pl.when(step == count * per)
    def _():
        rows = slice(count * half, count * half + rows_p)
        queries = jnp.concatenate([q_ref[0, rows, :], q_ref[1, rows, :]], 0)
        out, log_sum = forward_block(queries, [(pk_ref[...], pv_ref[...], hide_future(info[count]))])
        out_ref[0, rows, :] = out[:rows_p]
        out_ref[1, rows, :] = out[rows_p:]
        store_sums(sum_ref, log_sum)


def self_backward_kernel(
    info,
    q_ref,
    k_ref,
    v_ref,
    pk_ref,
    pv_ref,
    out_ref,
    grad_ref,
    sum_ref,
    joined_ref,
    prompt_ref,
    acc_pk,
    acc_pv,
    acc_k,
    acc_v,
    turned_p,
    turned,
    *,
    half,
    count,
    rows_p,
    block,
):
    step = pl.program_id(1)
    per = 2 * half // block

    @pl.when(step == 0)
    def _():
        acc_pk[...] = jnp.zeros_like(acc_pk)
        acc_pv[...] = jnp.zeros_like(acc_pv)
        turned_p[...] = pk_ref[...].T

    for pos in range(per):

        @pl.when((step < count * per) & (lax.rem(step, per) == pos))
        def _():
            c = lax.div(step, per)
            base = pl.multiple_of(c * half, half)
            if pos == 0:
                for source in range(2):
                    turned[:, source * half : (source + 1) * half] = k_ref[
                        source, pl.ds(base, half), :
                    ].T
            spans = own_spans(pos, block, half)
            segments = [(pk_ref[...], turned_p[...], pv_ref[...], hide_after(info[c]))]
            for source, offset, size, last in spans:
                rows = pl.ds(base + offset, size)
                at = source * half + offset
                segments.append(
                    (
                        k_ref[source, rows, :],
                        turned[:, at : at + size],
                        v_ref[source, rows, :],
                        hide_future(0) if last else None,
                    )
                )
            rows = pl.ds(base + pos * block % half, block)
            source = pos * block // half
            grad_q, grad_kv = backward_block(
                q_ref[source, rows, :],
                grad_ref[source, rows, :],
                out_ref[source, rows, :],
                sum_ref[0, 0],
                segments,
            )
            joined_ref[0, source, rows, :] = grad_q
            acc_pk[...] += grad_kv[0][0]
            acc_pv[...] += grad_kv[0][1]
            for (source, offset, size, last), (grad_k, grad_v) in zip(spans, grad_kv[1:]):
                at = source * half + offset
                if last:
                    acc_k[at : at + size] = grad_k
                    acc_v[at : at + size] = grad_v
                else:
                    acc_k[at : at + size] += grad_k
                    acc_v[at : at + size] += grad_v
            if pos == per - 1:
                for source in range(2):
                    rows = pl.ds(base, half)
                    span = slice(source * half, (source + 1) * half)
                    joined_ref[1, source, rows, :] = acc_k[span].astype(BF)
                    joined_ref[2, source, rows, :] = acc_v[span].astype(BF)

    @pl.when(step == count * per)
    def _():
        rows = slice(count * half, count * half + rows_p)
        both = [jnp.concatenate([r[0, rows, :], r[1, rows, :]], 0) for r in (q_ref, grad_ref, out_ref)]
        grad_q, grad_kv = backward_block(
            *both,
            sum_ref[0, 0][:, : 2 * rows_p],
            [(pk_ref[...], turned_p[...], pv_ref[...], hide_future(info[count]))],
        )
        for source in range(2):
            joined_ref[0, source, rows, :] = grad_q[source * rows_p : (source + 1) * rows_p]
            zero = jnp.zeros((rows_p, grad_q.shape[1]), BF)
            joined_ref[1, source, rows, :] = zero
            joined_ref[2, source, rows, :] = zero
        prompt_ref[0] = (acc_pk[...] + grad_kv[0][0]).astype(BF)
        prompt_ref[1] = (acc_pv[...] + grad_kv[0][1]).astype(BF)


PAIR = 2 * HEAD_DIM
BLOCK = 256


def wide(rows, at, lead=()):
    shape = lead + (rows, PAIR)
    zeros = (0,) * (len(lead) + 1)
    return pl.BlockSpec(shape, lambda pair, step, *_: zeros + (at + pair,))


def sums_spec(block):
    return pl.BlockSpec((1, 1, 8, block), lambda pair, step, *_: (pair, step, 0, 0))


def cost(flops, exps, *arrays):
    return pl.CostEstimate(
        flops=flops,
        transcendentals=exps,
        bytes_accessed=sum(a.size * a.dtype.itemsize for a in arrays),
    )


def self_forward(joined, prompt_kv, info, half, count, rows_p):
    rows, width = joined.shape[1], joined.shape[2] // 3
    keys = prompt_kv.shape[0]
    pairs = width // PAIR
    block = min(BLOCK, half)
    steps = count * 2 * half // block + 1
    scores = 2 * pairs * (count * 2 * half * (keys + half) + 2 * rows_p * keys)
    return pl.pallas_call(
        functools.partial(self_forward_kernel, half=half, count=count, rows_p=rows_p, block=block),
        out_shape=(
            jax.ShapeDtypeStruct((2, rows, width), BF),
            jax.ShapeDtypeStruct((pairs, steps, 8, block), F32),
        ),
        grid_spec=pltpu.PrefetchScalarGridSpec(
            num_scalar_prefetch=1,
            grid=(pairs, steps),
            in_specs=[
                wide(rows, 0, (2,)),
                wide(rows, pairs, (2,)),
                wide(rows, 2 * pairs, (2,)),
                wide(keys, 0),
                wide(keys, pairs),
            ],
            out_specs=[wide(rows, 0, (2,)), sums_spec(block)],
        ),
        cost_estimate=cost(scores * 512, scores, joined, prompt_kv),
        name="self_forward",
    )(info, joined, joined, joined, prompt_kv, prompt_kv)


def self_backward(joined, prompt_kv, info, out, grad, sums, half, count, rows_p):
    rows, width = joined.shape[1], joined.shape[2] // 3
    keys = prompt_kv.shape[0]
    pairs = width // PAIR
    block = min(BLOCK, half)
    steps = count * 2 * half // block + 1
    scores = 2 * pairs * (count * 2 * half * (keys + half) + 2 * rows_p * keys)
    return pl.pallas_call(
        functools.partial(self_backward_kernel, half=half, count=count, rows_p=rows_p, block=block),
        out_shape=(
            jax.ShapeDtypeStruct((3, 2, rows, width), BF),
            jax.ShapeDtypeStruct((2, keys, width), BF),
        ),
        grid_spec=pltpu.PrefetchScalarGridSpec(
            num_scalar_prefetch=1,
            grid=(pairs, steps),
            in_specs=[
                wide(rows, 0, (2,)),
                wide(rows, pairs, (2,)),
                wide(rows, 2 * pairs, (2,)),
                wide(keys, 0),
                wide(keys, pairs),
                wide(rows, 0, (2,)),
                wide(rows, 0, (2,)),
                sums_spec(block),
            ],
            out_specs=[wide(rows, 0, (3, 2)), wide(keys, 0, (2,))],
            scratch_shapes=[pltpu.VMEM((keys, PAIR), F32)] * 2
            + [pltpu.VMEM((2 * half, PAIR), F32)] * 2
            + [pltpu.VMEM((PAIR, keys), BF), pltpu.VMEM((PAIR, 2 * half), BF)],
        ),
        cost_estimate=cost(scores * 1280, scores, joined, prompt_kv, out, grad, joined),
        name="self_backward",
    )(info, joined, joined, joined, prompt_kv, prompt_kv, out, grad, sums)


def cross_forward_kernel(q_ref, k_ref, v_ref, out_ref, sum_ref, *, full, rest, block):
    step = pl.program_id(1)

    @pl.when(step < full)
    def _():
        rows = pl.ds(pl.multiple_of(step * block, block), block)
        out, log_sum = forward_block(q_ref[rows, :], [(k_ref[...], v_ref[...], None)])
        out_ref[rows, :] = out
        store_sums(sum_ref, log_sum)

    @pl.when(step == full)
    def _():
        rows = slice(full * block, full * block + rest)
        out, log_sum = forward_block(q_ref[rows, :], [(k_ref[...], v_ref[...], None)])
        out_ref[rows, :] = out
        store_sums(sum_ref, log_sum)


def cross_backward_kernel(
    q_ref, k_ref, v_ref, out_ref, grad_ref, sum_ref, gq_ref, gk_ref, gv_ref, acc_k, acc_v, turned, *, full, rest, block
):
    step = pl.program_id(1)

    @pl.when(step == 0)
    def _():
        acc_k[...] = jnp.zeros_like(acc_k)
        acc_v[...] = jnp.zeros_like(acc_v)
        turned[...] = k_ref[...].T

    def piece(rows, size):
        grad_q, grad_kv = backward_block(
            q_ref[rows, :],
            grad_ref[rows, :],
            out_ref[rows, :],
            sum_ref[0, 0][:, :size],
            [(k_ref[...], turned[...], v_ref[...], None)],
        )
        gq_ref[rows, :] = grad_q
        return grad_kv[0]

    @pl.when(step < full)
    def _():
        grad_k, grad_v = piece(pl.ds(pl.multiple_of(step * block, block), block), block)
        acc_k[...] += grad_k
        acc_v[...] += grad_v

    @pl.when(step == full)
    def _():
        grad_k, grad_v = piece(slice(full * block, full * block + rest), rest)
        gk_ref[...] = (acc_k[...] + grad_k).astype(BF)
        gv_ref[...] = (acc_v[...] + grad_v).astype(BF)


def cross_forward(queries, enc_kv, rows_c):
    rows, width = queries.shape
    keys = enc_kv.shape[0]
    pairs = width // PAIR
    full = rows_c // BLOCK
    scores = 2 * pairs * rows * keys
    return pl.pallas_call(
        functools.partial(cross_forward_kernel, full=full, rest=rows - rows_c, block=BLOCK),
        out_shape=(
            jax.ShapeDtypeStruct((rows, width), BF),
            jax.ShapeDtypeStruct((pairs, full + 1, 8, BLOCK), F32),
        ),
        grid=(pairs, full + 1),
        in_specs=[wide(rows, 0), wide(keys, 0), wide(keys, pairs)],
        out_specs=[wide(rows, 0), sums_spec(BLOCK)],
        cost_estimate=cost(scores * 512, scores, queries, enc_kv),
        name="cross_forward",
    )(queries, enc_kv, enc_kv)


def cross_backward(queries, enc_kv, out, grad, sums, rows_c):
    rows, width = queries.shape
    keys = enc_kv.shape[0]
    pairs = width // PAIR
    full = rows_c // BLOCK
    scores = 2 * pairs * rows * keys
    return pl.pallas_call(
        functools.partial(cross_backward_kernel, full=full, rest=rows - rows_c, block=BLOCK),
        out_shape=(
            jax.ShapeDtypeStruct((rows, width), BF),
            jax.ShapeDtypeStruct((keys, width), BF),
            jax.ShapeDtypeStruct((keys, width), BF),
        ),
        grid=(pairs, full + 1),
        in_specs=[
            wide(rows, 0),
            wide(keys, 0),
            wide(keys, pairs),
            wide(rows, 0),
            wide(rows, 0),
            sums_spec(BLOCK),
        ],
        out_specs=[wide(rows, 0), wide(keys, 0), wide(keys, 0)],
        scratch_shapes=[pltpu.VMEM((keys, PAIR), F32)] * 2 + [pltpu.VMEM((PAIR, keys), BF)],
        cost_estimate=cost(scores * 1280, scores, queries, enc_kv, out, grad),
        name="cross_backward",
    )(queries, enc_kv, enc_kv, out, grad, sums)


def exchange(value):
    return lax.all_to_all(value, "seq", split_axis=0, concat_axis=0, tiled=True)


def on_device(
    prompt_in,
    cont_in,
    enc_in,
    prefix,
    cot_prompt,
    cot_cont,
    w_qkv,
    w_attn_out,
    w_cross_q,
    w_cross_kv,
    w_cross_out,
    w_ffn_in,
    w_ffn_out,
    norm_gain,
    norm_bias,
):
    seq = lax.axis_index("seq")
    width = w_qkv.shape[1] // 3
    hg = width // 2
    shard = w_qkv.shape[0]
    rows_p = prompt_in.shape[1]
    count = cont_in.shape[1]
    half = cont_in.shape[2]
    rows_c = count * half
    reach = prefix[0]

    own_cols = lax.dynamic_slice_in_dim(w_qkv.reshape(shard, 3, 2, hg), seq, 1, 2)
    wq = lax.all_gather(own_cols.reshape(shard, 3 * hg), "fsdp", axis=0, tiled=True)
    shared = lax.all_gather(
        jnp.concatenate([prompt_in[0], enc_in[0]], 0), ("fsdp", "seq"), axis=0
    )
    prompt_all = shared[:, :rows_p].reshape(-1, width)
    enc_all = shared[:, rows_p:].reshape(-1, width)
    norms = jnp.concatenate([norm_gain, norm_bias], 0).T
    norms = jnp.pad(norms, ((0, 0), (0, 128 - norms.shape[1])))
    mixed = gather_rows(jnp.concatenate([w_attn_out, w_cross_q, w_cross_out, w_cross_kv, norms], 1))
    wo = mixed[:, :width]
    wcq = mixed[:, width : 2 * width]
    wco = mixed[:, 2 * width : 3 * width]
    wckv = mixed[:, 3 * width : 5 * width]
    norms = mixed[:, 5 * width :].astype(F32).T
    w1 = gather_rows(w_ffn_in)
    w2 = gather_rows(w_ffn_out)

    mine = jnp.concatenate([cont_in[0].reshape(rows_c, width), prompt_in[0]], 0)
    x_low, x_high = both_halves(mine)
    x_all = jnp.stack([x_low, x_high], 0)
    joined = lax.dot_general(
        x_all, wq, (((2,), (0,)), ((), ())), preferred_element_type=F32
    ).astype(BF)
    prompt_kv = mm(prompt_all, wq[:, hg:]).astype(BF)
    info = jnp.concatenate([reach, lax.axis_index("fsdp")[None] * (2 * rows_p)])
    att, sums = self_forward(joined, prompt_kv, info, half, count, rows_p)
    att_rows = exchange(att)
    proj = mm(att_rows[0], wo[:hg]) + mm(att_rows[1], wo[hg:])
    hat1, scale1 = norm_stats(mine.astype(F32) + proj)
    first = hat1 * norms[0] + norms[3]
    first_low = first.astype(BF)
    cq = mm(first_low, wcq).astype(BF)
    enc_kv = mm(enc_all, wckv).astype(BF)
    cross, cross_sum = cross_forward(cq, enc_kv, rows_c)
    hat2, scale2 = norm_stats(first + mm(cross, wco))
    second = hat2 * norms[1] + norms[4]
    second_low = second.astype(BF)
    pre = mm(second_low, w1)
    gate = 0.5 * (1.0 + lax.erf(pre * 0.7071067811865476))
    act = (pre * gate).astype(BF)
    slope = (gate + pre * jnp.exp(-0.5 * pre * pre) * 0.3989422804014327).astype(BF)
    hat3, scale3 = norm_stats(second + mm(act, w2))
    third = (hat3 * norms[2] + norms[5]).astype(BF)

    cot = jnp.concatenate([cot_cont[0].reshape(rows_c, width), cot_prompt[0]], 0).astype(F32)
    grad3, gain3, bias3 = norm_back(cot, hat3, scale3, norms[2])
    low3 = grad3.astype(BF)
    g_w2 = mm_tn(act, low3).astype(BF)
    grad_pre = (mm_nt(low3, w2) * slope.astype(F32)).astype(BF)
    g_w1 = mm_tn(second_low, grad_pre).astype(BF)
    owners = 2 * lax.axis_size("fsdp")
    columns = [slice(i, i + width) for i in range(0, g_w1.shape[1], width)]
    g_ffn = per_owner([g_w2] + [g_w1[:, cols] for cols in columns])
    grad_second = grad3 + mm_nt(grad_pre, w1)
    grad2, gain2, bias2 = norm_back(grad_second, hat2, scale2, norms[1])
    low2, g_ffn = lax.optimization_barrier((grad2.astype(BF), g_ffn))
    g_ffn = scatter_sum(g_ffn)
    g_wco = mm_tn(cross, low2)
    grad_cross = mm_nt(low2, wco).astype(BF)
    grad_cq, grad_ck, grad_cv = cross_backward(cq, enc_kv, cross, grad_cross, cross_sum, rows_c)
    g_wckv = [mm_tn(enc_all, grad_ck), mm_tn(enc_all, grad_cv)]
    grad_enc = (mm_nt(grad_ck, wckv[:, :width]) + mm_nt(grad_cv, wckv[:, width:])).astype(BF)
    g_wcq = mm_tn(first_low, grad_cq)
    grad_first = grad2 + mm_nt(grad_cq, wcq)
    grad1, gain1, bias1 = norm_back(grad_first, hat1, scale1, norms[0])
    low1 = grad1.astype(BF)
    g_wo = jnp.concatenate([mm_tn(att_rows[0], low1), mm_tn(att_rows[1], low1)], 0)
    g_norms = jnp.stack([gain1, gain2, gain3, bias1, bias2, bias3], 0).astype(BF)
    g_norms = g_norms.reshape(6, owners, shard // 2).swapaxes(0, 1)
    g_norms = jnp.pad(g_norms, ((0, 0), (0, 10), (0, width - shard // 2))).reshape(-1, width)
    g_mixed = [g.astype(BF) for g in (g_wo, g_wcq, g_wco, *g_wckv, grad_enc, g_norms)]
    g_mixed = per_owner(g_mixed)
    grad_att = jnp.stack([mm_nt(low1, wo[:hg]), mm_nt(low1, wo[hg:])], 0).astype(BF)
    grad_att, g_mixed, g_ffn = lax.optimization_barrier((exchange(grad_att), g_mixed, g_ffn))
    g_mixed = scatter_sum(g_mixed)
    grad_joined, grad_pkv = self_backward(
        joined, prompt_kv, info, att, grad_att, sums, half, count, rows_p
    )
    grad_joined, g_mixed = lax.optimization_barrier((grad_joined, g_mixed))
    flat = x_all.reshape(-1, width)
    g_q, g_k, g_v = (mm_tn(flat, grad_joined[i].reshape(-1, hg)) for i in range(3))
    g_k = g_k + mm_tn(prompt_all, grad_pkv[0])
    g_v = g_v + mm_tn(prompt_all, grad_pkv[1])
    grad_pr = mm_nt(grad_pkv[0], wq[:, hg : 2 * hg]) + mm_nt(grad_pkv[1], wq[:, 2 * hg :])
    chips = lax.axis_size("fsdp")
    last = [g_q, g_k, g_v, grad_pr[:, :hg], grad_pr[:, hg:]]
    last = jnp.concatenate([v.astype(BF).reshape(chips, -1, hg) for v in last], 1)
    last = lax.psum_scatter(
        last.reshape(-1, hg), "fsdp", scatter_dimension=0, tiled=True
    )
    q_low, q_high = both_halves(over_groups(last[: 3 * shard]))
    g_qkv = [v.reshape(3, shard, hg) for v in (q_low, q_high)]
    g_qkv = jnp.concatenate([g_qkv[i % 2][i // 2] for i in range(6)], 1).astype(F32)
    grad_x = sum(
        mm_nt(grad_joined[i].reshape(-1, hg), wq[:, i * hg : (i + 1) * hg]) for i in range(3)
    )
    grad_x = grad_x.astype(BF).reshape(x_all.shape)
    cont_x = exchange(grad_x[:, :rows_c])
    grad_in = grad1[:rows_c] + cont_x[0].astype(F32) + cont_x[1].astype(F32)
    grad_pr = last[3 * shard :].reshape(2, 2 * rows_p, hg)
    grad_pr = jnp.concatenate([grad_pr[0], grad_pr[1]], 1).reshape(2, rows_p, width)
    prompt_x = exchange((grad_x[:, rows_c:].astype(F32) + grad_pr.astype(F32)).astype(BF))
    grad_prompt = grad1[rows_c:] + prompt_x[0].astype(F32) + prompt_x[1].astype(F32)

    both = both_halves(over_groups(g_ffn))
    g_w2 = jnp.concatenate([v[: 2 * shard] for v in both], 0).astype(F32)
    mine = shard // 2
    g_w1 = [
        jnp.concatenate([v[2 * shard + i * mine :][:mine] for i in range(len(columns))], 1)
        for v in both
    ]
    g_w1 = jnp.concatenate(g_w1, 0).astype(F32)
    used = 5 * mine
    grad_enc = g_mixed[used : used + rows_p].astype(F32)
    g_mixed = jnp.concatenate([g_mixed[:used], g_mixed[used + rows_p :]], 0)
    both = both_halves(over_groups(g_mixed))
    g_wo, g_wcq, g_wco, g_wck, g_wcv = (
        jnp.concatenate([v[i * mine : (i + 1) * mine] for v in both], 0).astype(F32)
        for i in range(5)
    )
    g_norms = jnp.concatenate([v[used : used + 6, :mine] for v in both], 1).astype(F32)
    return (
        third[rows_c:][None],
        third[:rows_c].reshape(cont_in.shape),
        grad_prompt[None],
        grad_in.reshape(cont_in.shape),
        grad_enc[None],
        g_qkv,
        g_wo,
        g_wcq,
        jnp.concatenate([g_wck, g_wcv], 1),
        g_wco,
        g_w1,
        g_w2,
        g_norms[:3],
        g_norms[3:],
    )


def solution(mesh):
    rows = P("grp", ("fsdp", "seq"), None)
    conts = P("grp", "fsdp", "seq", None)
    weight = P("fsdp", None)
    norm = P(None, "fsdp")
    return jax.shard_map(
        on_device,
        mesh=mesh,
        in_specs=(rows, conts, rows, P("grp", "fsdp"), rows, conts) + (weight,) * 7 + (norm,) * 2,
        out_specs=(rows, conts, rows, conts, rows) + (weight,) * 7 + (norm,) * 2,
        check_vma=False,
    )
```

time: 1180 us -> 690 us (0.58)
  matrix products: 529 us -> 160 us
  Pallas kernels: 0 us -> 210 us
  waiting for transfers between devices: 336 us -> 166 us
  local copies, waits for them, and re-layouts: 154 us -> 52.7 us
  other arithmetic: 118 us -> 54.1 us
  blocking collectives: 12.4 us -> 0 us
  starting transfers between devices: 12.4 us -> 24.4 us
    dot_general x26 -> x0, matrix products: 383 us -> none  [the longest x4 91.2 us: attend_back(): jnp.einsum('qhe,khe->hqk', heads(grad), heads(values), preferred_element_...]
    reduce_scatter x5 -> x3, waiting for transfers between devices: 268 us -> 55.6 us  [the longest x1 38.9 us: on_device(): lax.psum_scatter(last.reshape(-1, hg), 'fsdp', scatter_dimension=0, tiled...]
    pallas_call x0 -> x4, Pallas kernels: none -> 210 us  [the longest x1 73.5 us: self_backward(): pl.pallas_call(functools.partial(self_backward_kernel, half=half, count=c...]
    reduce_sum x8 -> x0, other arithmetic: 73.5 us -> none  [the longest x4 68.6 us: attend(): total = jnp.sum(raised, axis=-1, keepdims=True)]
    all_gather x3, waiting for transfers between devices: 0.04 us -> 38.4 us  [gather_rows(): return lax.all_gather(half_rows(shard), ('fsdp', 'seq'), axis=0, tiled=True)]
    concatenate x16 -> x4, local copies, waits for them, and re-layouts: 35.3 us -> 1.9 us  [the longest x1 0.97 us: on_device(): jnp.concatenate([v.astype(BF).reshape(chips, -1, hg) for v in last], 1)]
    unnamed x248 -> x129, local copies, waits for them, and re-layouts: 50.9 us -> 25.2 us
    convert_element_type x13 -> x0, local copies, waits for them, and re-layouts: 16.6 us -> none  [the longest x6 7.14 us: attend(): return (out.reshape(queries.shape).astype(BF), top + jnp.log(total))]
  transfers between devices with their start and end apart: 21 -> 19, of which waited for: 9 -> 9; matrix products, arithmetic and copies ran while one was open for 39% -> 25% of each run, Pallas kernels for 0% -> 31%
where the time goes in v2:
time: 690 us; the launch traced here: 683 us
  Pallas kernels  210 us (30%)
  waiting for transfers between devices  166 us (24%)
  matrix products  160 us (23%)
  other arithmetic  54.1 us (8%)
  local copies, waits for them, and re-layouts  52.7 us (8%)
  starting transfers between devices  24.4 us (4%)
  between operations  15.6 us (2%)
    pallas_call x1, Pallas kernels, self_backward(): pl.pallas_call(functools.partial(self_backward_kernel, half=half, count=c...  73.5 us
    dot_general x13, matrix products, mm_nt(): lax.dot_general(a, b, (((1,), (1,)), ((), ())), preferred_element_type=F32)  64.9 us
    pallas_call x1, Pallas kernels, cross_backward(): pl.pallas_call(functools.partial(cross_backward_kernel, full=full, rest=r...  51.4 us
    pallas_call x1, Pallas kernels, self_forward(): pl.pallas_call(functools.partial(self_forward_kernel, half=half, count=co...  48.8 us
    dot_general x8, matrix products, mm(): return jnp.dot(a, b, preferred_element_type=F32)  43.1 us
    dot_general x13, matrix products, mm_tn(): lax.dot_general(a, b, (((0,), (0,)), ((), ())), preferred_element_type=F32)  42.7 us
    reduce_scatter x1, waiting for transfers between devices, on_device(): lax.psum_scatter(last.reshape(-1, hg), 'fsdp', scatter_dimension=0, tiled...  38.9 us
    all_gather x3, waiting for transfers between devices, gather_rows(): return lax.all_gather(half_rows(shard), ('fsdp', 'seq'), axis=0, tiled=True)  38.4 us
  transfers between devices with their start and end apart: 19, of which 9 were waited for; matrix products, arithmetic and copies ran while one was open for 25% of the time, Pallas kernels for 31%

profile of v2, /device:TPU:0, one launch (start us, length us, event | category | flops | bytes accessed | tf_op | source)
XLA Modules:
  0.0 682.6 jit_solution(7148779472837224397)
XLA Ops:
  23.2 3.9 select_bitcast_fusion.1
  27.0 32.5 %all-gather.7.cloned.1.call-done = bf16[768,1152]{1,0:T(8,128)(2,1)} async-done(((bf16[96,1152]{1,0:T(8,128)(2,1)}), bf16[768,1152]{1,0:T(8,128)(2,1)}) %all-gather.7.cloned.1.call-update) | async-done | bytes 1769488 | tf_op jit(solution)/shard_map/all_gather | solution.py:547
  59.5 9.3 %convolution_convert_fusion.q_ref.k_ref.v_ref = bf16[2,1088,1152]{2,1,0:T(8,128)(2,1)} fusion(bf16[768,1152]{1,0:T(8,128)(2,1)} %all-gather.7.cloned.1.call-done, bf16[1,1088,768]{2,1,0:T(8,128)(2,1)} %get-tuple-element.76, bf16[1,1088,768]{2,1,0:T(8,128)(2,1)} %get-tuple-element.75), kind=kOutput, calls=%fused_computation.10 | convolution fusion | flops 3854548992 | bytes 10125312 | tf_op jit(solution)/shard_map/dot_general | solution.py:567
  68.8 37.6 %all-gather.15.cloned.1.call-done = bf16[2048,768]{1,0:T(8,128)(2,1)} async-done(((bf16[128,768]{1,0:T(8,128)(2,1)}), bf16[2048,768]{1,0:T(8,128)(2,1)}) %all-gather.15.cloned.1.call-update) | async-done | bytes 3145744 | tf_op jit(solution)/shard_map/all_gather | solution.py:548
  112.4 48.8 %self_forward.1 = (bf16[2,1088,384]{2,1,0:T(8,128)(2,1)}, f32[3,9,8,256]{3,2,1,0:T(8,128)}) custom-call(s32[3]{0:T(128)} %pad_add_fusion.info, bf16[2,1088,1152]{2,1,0:T(8,128)(2,1)} %convolution_convert_fusion.q_ref.k_ref.v_ref, bf16[2,1088,1152]{2,1,0:T(8,128)(2,1)} %convolution_convert_fusion.q_ref.k_ref.v_ref, ...), custom_call_target="tpu_custom_call" | custom-call | flops 10066329600 | bytes 6586368 | tf_op jit(solution)/shard_map/self_forward/pallas_call | solution.py:354
  161.2 3.7 all-to-all-start
  180.9 4.2 convolution_convert_fusion.3.k_ref.v_ref
  185.0 36.6 %cross_forward.1 = (bf16[1088,768]{1,0:T(8,128)(2,1)}, f32[6,5,8,256]{3,2,1,0:T(8,128)}) custom-call(bf16[1088,768]{1,0:T(8,128)(2,1)} %convolution_convert_fusion.5.q_ref, bf16[1024,1536]{1,0:T(8,128)(2,1)} %convolution_convert_fusion.3.k_ref.v_ref, bf16[1024,1536]{1,0:T(8,128)(2,1)} %convolution_convert_fusion.3.k_ref.v_ref), custom_call_target="tpu_custom_call" | custom-call | flops 6845104128 | bytes 4816896 | tf_op jit(solution)/shard_map/cross_forward/pallas_call | solution.py:472
  221.7 5.1 fusion.78
  229.3 12.5 %multiply_convert_fusion = (bf16[1088,3072]{1,0:T(8,128)(2,1)}, f32[1088,3072]{1,0:T(8,128)}) fusion(bf16[768,3072]{1,0:T(8,128)(2,1)} %all-gather.11.cloned.1.call-done, f32[1088,768]{1,0:T(8,128)} %get-tuple-element.112, f32[768]{0:T(1024)S(1)} %get-tuple-element.59, f32[768]{0:T(1024)S(1)} %get-tuple-element.60, f32[1088]{0:T(1024)S(1)} %add_rsqrt_fusion.1, ...), kind=kOutput, calls=%fused_computation.7 | convolution fusion | flops 5154717696 | bytes 28129792 | tf_op jit(solution)/shard_map/dot_general | solution.py:19
  241.8 35.2 %all-gather.13.cloned.1.call-done = bf16[3072,768]{1,0:T(8,128)(2,1)} async-done(((bf16[192,768]{1,0:T(8,128)(2,1)}), bf16[3072,768]{1,0:T(8,128)(2,1)}) %all-gather.13.cloned.1.call-update) | async-done | bytes 4718608 | tf_op jit(solution)/shard_map/all_gather | solution.py:40
  277.0 11.1 %fusion.79 = (f32[1088]{0:T(1024)S(1)}, f32[1088,768]{1,0:T(8,128)S(1)}) fusion(bf16[1088,3072]{1,0:T(8,128)(2,1)} %get-tuple-element.113, bf16[3072,768]{1,0:T(8,128)(2,1)} %all-gather.13.cloned.1.call-done, f32[768]{0:T(1024)S(1)} %get-tuple-element.59, f32[768]{0:T(1024)S(1)} %get-tuple-element.60, f32[1088]{0:T(1024)S(1)} %add_rsqrt_fusion.1, ...), kind=kOutput, calls=%fused_computation.217 | convolution fusion | flops 5138840576 | bytes 18107136 | tf_op jit(solution)/shard_map/dot_general | solution.py:19
  290.7 3.9 fusion.13
  294.7 9.7 %convolution_convert_fusion.2 = bf16[3072,768]{1,0:T(8,128)(2,1)} fusion(bf16[1088,3072]{1,0:T(8,128)(2,1)S(1)} %copy-done.46, f32[1088,768]{1,0:T(8,128)S(1)} %get-tuple-element.116, f32[1088]{0:T(1024)S(1)} %get-tuple-element.119, f32[1088]{0:T(1024)S(1)} %get-tuple-element.120, f32[768]{0:T(1024)S(1)} %get-tuple-element.57, f32[1088]{0:T(1024)S(1)} %add_rsqrt_fusion, ...), kind=kOutput, calls=%fused_computation.13 | convolution fusion | flops 5146214400 | bytes 16437248 | tf_op jit(solution)/shard_map/dot_general | solution.py:23
  304.4 16.6 %fusion.5 = bf16[1088,3072]{1,0:T(8,128)(2,1)S(1)} fusion(bf16[3072,768]{1,0:T(8,128)(2,1)S(1)} %bitcast.197, f32[1088,3072]{1,0:T(8,128)} %get-tuple-element.114, f32[1088,768]{1,0:T(8,128)S(1)} %get-tuple-element.116, f32[1088]{0:T(1024)S(1)} %get-tuple-element.119, f32[1088]{0:T(1024)S(1)} %get-tuple-element.120, f32[768]{0:T(1024)S(1)} %get-tuple-element.57, ...), kind=kOutput, calls=%fused_computation.9 | convolution fusion | flops 5183963136 | bytes 29806592 | tf_op jit(solution)/shard_map/dot_general | solution.py:27
  321.1 12.1 %convolution_convert_fusion.1 = bf16[768,3072]{1,0:T(8,128)(2,1)S(1)} fusion(bf16[1088,3072]{1,0:T(8,128)(2,1)S(1)} %fusion.5, f32[1088,768]{1,0:T(8,128)} %get-tuple-element.112, f32[768]{0:T(1024)S(1)} %get-tuple-element.59, f32[768]{0:T(1024)S(1)} %get-tuple-element.60, f32[1088]{0:T(1024)S(1)} %add_rsqrt_fusion.1, f32[1088]{0:T(1024)S(1)} %broadcast_multiply_fusion.7), kind=kOutput, calls=%fused_computation.12 | convolution fusion | flops 5140365312 | bytes 14760448 | tf_op jit(solution)/shard_map/dot_general | solution.py:23
  337.1 14.5 %multiply_reduce_fusion = (bf16[768]{0:T(1024)(128)(2,1)S(1)}, f32[1088]{0:T(1024)S(1)}, f32[1088]{0:T(1024)S(1)}, bf16[768]{0:T(1024)(128)(2,1)S(1)}, f32[1088,768]{1,0:T(8,128)}) fusion(f32[1088,768]{1,0:T(8,128)} %get-tuple-element.112, f32[1088]{0:T(1024)S(1)} %add_rsqrt_fusion.1, f32[1088]{0:T(1024)S(1)} %broadcast_multiply_fusion.7, ...), kind=kOutput, calls=%fused_computation.33 | convolution fusion | flops 5151371264 | bytes 23145472 | tf_op jit(solution)/shard_map/dot_general | solution.py:27
  355.5 6.7 fusion.66
  364.0 4.5 convolution_convert_fusion.4.grad_ref
  368.5 51.4 %cross_backward.1 = (bf16[1088,768]{1,0:T(8,128)(2,1)}, bf16[1024,768]{1,0:T(8,128)(2,1)}, bf16[1024,768]{1,0:T(8,128)(2,1)}) custom-call(bf16[1088,768]{1,0:T(8,128)(2,1)} %convolution_convert_fusion.5.q_ref, bf16[1024,1536]{1,0:T(8,128)(2,1)} %convolution_convert_fusion.3.k_ref.v_ref, bf16[1024,1536]{1,0:T(8,128)(2,1)} %convolution_convert_fusion.3.k_ref.v_ref, ...), custom_call_target="tpu_custom_call" | custom-call | flops 17112760320 | bytes 8159232 | tf_op jit(solution)/shard_map/cross_backward/pallas_call | solution.py:492
  419.9 6.7 multiply_reduce_fusion.1
  427.2 3.7 fusion.65
  436.9 4.7 all-to-all-start.1
  466.8 5.3 reduce-scatter.4.cloned.1.call-done
  476.2 73.5 %self_backward.1 = (bf16[3,2,1088,384]{3,2,1,0:T(8,128)(2,1)}, bf16[2,1024,384]{2,1,0:T(8,128)(2,1)}) custom-call(s32[3]{0:T(128)} %pad_add_fusion.info, bf16[2,1088,1152]{2,1,0:T(8,128)(2,1)} %convolution_convert_fusion.q_ref.k_ref.v_ref, bf16[2,1088,1152]{2,1,0:T(8,128)(2,1)} %convolution_convert_fusion.q_ref.k_ref.v_ref, ...), custom_call_target="tpu_custom_call" | custom-call | flops 25165824000 | bytes 14942208 | tf_op jit(solution)/shard_map/self_backward/pallas_call | solution.py:384
  559.7 11.4 %reduce-scatter.6.cloned.1.call-done = bf16[320,768]{1,0:T(8,128)(2,1)} async-done(((bf16[5120,768]{1,0:T(8,128)(2,1)}), bf16[320,768]{1,0:T(8,128)(2,1)}) %reduce-scatter.6.cloned.1.call-update) | async-done | bytes 491536 | tf_op jit(solution)/shard_map/reduce_scatter | solution.py:52
  597.3 3.8 add_convert_fusion
  601.1 3.8 slice.397
  604.9 5.5 all-to-all-start.3
  614.4 4.0 fusion.14
  623.4 38.9 %reduce-scatter.8.cloned.1.call-done = bf16[544,384]{1,0:T(8,128)(2,1)} async-done(((bf16[4352,384]{1,0:T(8,128)(2,1)}), bf16[544,384]{1,0:T(8,128)(2,1)}) %reduce-scatter.8.cloned.1.call-update) | async-done | bytes 417808 | tf_op jit(solution)/shard_map/reduce_scatter | solution.py:634
  667.5 3.4 all-to-all-start.2
  (269 shorter events, 142.3 us)
Async XLA Ops:
  7.2 9.9 %copy-start = (bf16[96,3072]{1,0:T(8,128)(2,1)S(1)}, bf16[96,3072]{1,0:T(8,128)(2,1)}, u32[]{:S(2)}) copy-start(bf16[96,3072]{1,0:T(8,128)(2,1)} %param.26) | copy-start | bytes 1769476
  7.2 10.7 %copy-start.28 = (bf16[1,64,768]{2,1,0:T(8,128)(2,1)S(1)}, bf16[1,64,768]{2,1,0:T(8,128)(2,1)}, u32[]{:S(2)}) copy-start(bf16[1,64,768]{2,1,0:T(8,128)(2,1)} %param.15) | copy-start | bytes 294916
  7.2 8.9 %copy-start.39 = (bf16[96,1536]{1,0:T(8,128)(2,1)S(1)}, bf16[96,1536]{1,0:T(8,128)(2,1)}, u32[]{:S(2)}) copy-start(bf16[96,1536]{1,0:T(8,128)(2,1)} %param.24) | copy-start | bytes 884740
  7.2 10.7 %copy-start.9 = (bf16[1,2,512,768]{3,2,1,0:T(8,128)(2,1)S(1)}, bf16[1,2,512,768]{3,2,1,0:T(8,128)(2,1)}, u32[]{:S(2)}) copy-start(bf16[1,2,512,768]{3,2,1,0:T(8,128)(2,1)} %param.16) | copy-start | bytes 4718596
  7.2 52.3 %all-gather.7.cloned.1.call-start = ((), (), s32[]{:S(2)}) async-start(), calls=%async_computation.7 | async-start | bytes 1990656 | tf_op jit(solution)/shard_map/all_gather | solution.py:547
  10.7 95.7 %all-gather.15.cloned.1.call-start = ((), (), s32[]{:S(2)}) async-start(), calls=%async_computation.14 | async-start | bytes 3342336 | tf_op jit(solution)/shard_map/all_gather | solution.py:548
  12.4 155.7 %all-gather.9.cloned.1.call-start = ((), (), s32[]{:S(2)}) async-start(), calls=%async_computation.8 | async-start | bytes 6475776 | tf_op jit(solution)/shard_map/all_gather | solution.py:40
  17.0 212.3 %all-gather.11.cloned.1.call-start = ((), (), s32[]{:S(2)}) async-start(), calls=%async_computation.9 | async-start | bytes 5013504 | tf_op jit(solution)/shard_map/all_gather | solution.py:40
  17.8 259.2 %all-gather.13.cloned.1.call-start = ((), (), s32[]{:S(2)}) async-start(), calls=%async_computation.10 | async-start | bytes 5013504 | tf_op jit(solution)/shard_map/all_gather | solution.py:40
  19.2 4.0 collective-permute-start
  68.8 41.0 %copy-start.17 = (bf16[768,1152]{1,0:T(8,128)(2,1)S(1)}, bf16[768,1152]{1,0:T(8,128)(2,1)}, u32[]{:S(2)}) copy-start(bf16[768,1152]{1,0:T(8,128)(2,1)} %all-gather.7.cloned.1.call-done) | copy-start | bytes 5308420
  161.2 9.1 %all-to-all-start = ((bf16[2,1088,384]{2,1,0:T(8,128)(2,1)}), bf16[2,1088,384]{2,1,0:T(8,128)(2,1)S(1)}, u32[]{:S(2)}, u32[]{:S(2)}) async-start(bf16[2,1088,384]{2,1,0:T(8,128)(2,1)} %get-tuple-element.30.out_ref), calls=%async_computation | async-start | bytes 3342336 | tf_op jit(solution)/shard_map/all_to_all | solution.py:516
  164.9 307.3 %reduce-scatter.4.cloned.1.call-start = ((), (), s32[]{:S(2)}) async-start(), calls=%async_computation.11 | async-start | bytes 10027008 | tf_op jit(solution)/shard_map/reduce_scatter | solution.py:52
  288.1 16.3 %copy-start.12 = (f32[1088,768]{1,0:T(8,128)}, f32[1088,768]{1,0:T(8,128)S(1)}, u32[]{:S(2)}) copy-start(f32[1088,768]{1,0:T(8,128)S(1)} %get-tuple-element.116) | copy-start | bytes 10027012
  288.2 6.5 copy-start.46
  290.7 13.7 %slice-start = ((s8[4718592]{0:T(1024)(128)(4,1)}), s8[4194304]{0:T(1024)(128)(4,1)S(1)}, s32[]{:S(2)}) async-start(s8[4718592]{0:T(1024)(128)(4,1)} %bitcast.196), calls=%async_computation.15 | async-start | bytes 8388608
  294.7 9.7 %slice-start.1 = ((s8[4718592]{0:T(1024)(128)(4,1)}), s8[524288]{0:T(1024)(128)(4,1)S(1)}, s32[]{:S(2)}) async-start(s8[4718592]{0:T(1024)(128)(4,1)} %bitcast.196), calls=%async_computation.16 | async-start | bytes 1048576
  321.1 12.1 %copy-start.43 = (bf16[1088,3072]{1,0:T(8,128)(2,1)}, bf16[1088,3072]{1,0:T(8,128)(2,1)S(1)}, u32[]{:S(2)}) copy-start(bf16[1088,3072]{1,0:T(8,128)(2,1)S(1)} %fusion.5) | copy-start | bytes 20054020
  355.0 7.2 %copy-start.2 = (bf16[16,384,768]{2,1,0:T(8,128)(2,1)}, bf16[16,384,768]{2,1,0:T(8,128)(2,1)S(1)}, u32[]{:S(2)}) copy-start(bf16[16,384,768]{2,1,0:T(8,128)(2,1)S(1)} %constant_dynamic-update-slice_fusion.5) | copy-start | bytes 28311556
  436.9 29.9 %all-to-all-start.1 = ((bf16[2,1088,384]{2,1,0:T(8,128)(2,1)}), bf16[2,1088,384]{2,1,0:T(8,128)(2,1)}, u32[]{:S(2)}, u32[]{:S(2)}) async-start(bf16[2,1088,384]{2,1,0:T(8,128)(2,1)} %pad_maximum_fusion.3), calls=%async_computation.1 | async-start | bytes 3342336 | tf_op jit(solution)/shard_map/all_to_all | solution.py:516
  441.6 129.4 %reduce-scatter.6.cloned.1.call-start = ((), (), s32[]{:S(2)}) async-start(), calls=%async_computation.12 | async-start | bytes 8355840 | tf_op jit(solution)/shard_map/reduce_scatter | solution.py:52
  472.2 190.2 %reduce-scatter.8.cloned.1.call-start = ((), (), s32[]{:S(2)}) async-start(), calls=%async_computation.13 | async-start | bytes 3760128 | tf_op jit(solution)/shard_map/reduce_scatter | solution.py:634
  474.7 110.2 %collective-permute-start.5 = (bf16[384,768]{1,0:T(8,128)(2,1)}, bf16[384,768]{1,0:T(8,128)(2,1)}, u32[]{:S(2)}, u32[]{:S(2)}) collective-permute-start(bf16[384,768]{1,0:T(8,128)(2,1)} %reduce-scatter.4.cloned.1.call-done), channel_id=1, source_target_pairs={{0,16},{16,0},{1,17},{17,1},{2,18},{18,2},{3,19},{19,3},{4,20},{20... | collective-permute-start | bytes 1769480 | tf_op jit(solution)/shard_map/ppermute | solution.py:31
  586.2 2.1 collective-permute-start.6
  591.6 20.4 %collective-permute-start.3 = (bf16[256,768]{1,0:T(8,128)(2,1)}, bf16[256,768]{1,0:T(8,128)(2,1)}, u32[]{:S(2)}, u32[]{:S(2)}) collective-permute-start(bf16[256,768]{1,0:T(8,128)(2,1)} %pad_maximum_fusion.5), channel_id=1, source_target_pairs={{0,16},{16,0},{1,17},{17,1},{2,18},{18,2},{3,19},{19,3},{4,20},{20... | collective-permute-start | bytes 1179656 | tf_op jit(solution)/shard_map/ppermute | solution.py:31
  604.9 9.6 %copy-start.11 = (f32[1088,768]{1,0:T(8,128)S(1)}, f32[1088,768]{1,0:T(8,128)}, u32[]{:S(2)}) copy-start(f32[1088,768]{1,0:T(8,128)} %get-tuple-element.64) | copy-start | bytes 10027012
  604.9 9.6 %all-to-all-start.3 = ((bf16[2,1024,768]{2,1,0:T(8,128)(2,1)}), bf16[2,1024,768]{2,1,0:T(8,128)(2,1)}, u32[]{:S(2)}, u32[]{:S(2)}) async-start(bf16[2,1024,768]{2,1,0:T(8,128)(2,1)} %slice.397), calls=%async_computation.6 | async-start | bytes 6291456 | tf_op jit(solution)/shard_map/all_to_all | solution.py:516
  614.0 4.5 collective-permute-start.4
  622.6 52.7 %copy-start.1 = (bf16[96,3072]{1,0:T(8,128)(2,1)S(1)}, bf16[96,3072]{1,0:T(8,128)(2,1)}, u32[]{:S(2)}) copy-start(bf16[96,3072]{1,0:T(8,128)(2,1)} %param.26) | copy-start | bytes 1769476
  663.3 7.6 %collective-permute-start.1 = (bf16[288,384]{1,0:T(8,128)(2,1)S(1)}, bf16[288,384]{1,0:T(8,128)(2,1)S(1)}, u32[]{:S(2)}, u32[]{:S(2)}) collective-permute-start(bf16[288,384]{1,0:T(8,128)(2,1)S(1)} %slice.400), channel_id=1, source_target_pairs={{0,16},{16,0},{1,17},{17,1},{2,18},{18,2},{3,19},{19,3},{4,20},{20... | collective-permute-start | bytes 663560 | tf_op jit(solution)/shard_map/ppermute | solution.py:31
  667.5 5.0 all-to-all-start.2
  672.0 2.2 collective-permute-start.2
  (36 other events, 108.6 us)
Sparse Core Ops, SparseCore 0:
  10.9 48.5 all-gather.6
  62.4 44.0 all-gather.14
  109.2 58.8 all-gather.8
  170.8 51.7 all-gather.10
  225.3 51.6 all-gather.12
  362.3 109.7 reduce-scatter.3
  476.2 94.8 reduce-scatter.5
  585.0 77.3 reduce-scatter.7

commit v3 on v2

--- a/solution.py
+++ b/solution.py
@@ -12,6 +12,9 @@
 EPS = 1e-05
 MASKED = -1e30
 BF = jnp.bfloat16
+PAIR = 2 * HEAD_DIM
+FLAGS = object()
+MESH = pl.DeviceIdType.MESH
 F32 = jnp.float32
 
 
@@ -93,15 +96,32 @@
     return low, jnp.where(low, 1.0, 0.0).astype(BF), jnp.where(low, 0.0, 1.0).astype(BF)
 
 
+def with_flags(queries):
+    lane = lax.broadcasted_iota(jnp.int32, (1, PAIR), 1)
+    _, *masks = lane_masks()
+    flags = [jnp.where(lane == at, 1.0, 0.0).astype(BF) for at in (HEAD_DIM, 0)]
+    return [queries * mask + flag for mask, flag in zip(masks, flags)]
+
+
+def flag_keys(flagged, keys, limit):
+    lane = lax.broadcasted_iota(jnp.int32, keys.shape, 1)
+    key = lax.broadcasted_iota(jnp.int32, keys.shape, 0)
+    bias = jnp.where(key < limit, 0.0, MASKED)
+    for h, at in enumerate((HEAD_DIM, 0)):
+        flagged[h] = jnp.where(lane == at, bias, keys.astype(F32)).astype(BF)
+
+
 def forward_block(queries, segments):
     low, *masks = lane_masks()
     scaled = queries * BF(SCALE)
     outs, sums = [], []
-    for mask in masks:
+    flagged = with_flags(scaled)
+    for h, mask in enumerate(masks):
         own = scaled * mask
         scores = []
         for keys, _, hide in segments:
-            part = dot_nt(own, keys)
+            part = dot_nt(flagged[h], keys[h]) if hide is FLAGS else dot_nt(own, keys)
+            hide = None if hide is FLAGS else hide
             scores.append(part if hide is None else hide(part, 1))
         top = scores[0].max(axis=-1, keepdims=True)
         for part in scores[1:]:
@@ -124,6 +144,7 @@
     owns = [scaled * mask for mask in masks]
     grads = [grad * mask for mask in masks]
     own_pair = jnp.concatenate(owns, 0)
+    flagged = with_flags(scaled)
     grad_pair = jnp.concatenate(grads, 0)
     grad_q = [0.0, 0.0]
     grad_kv = []
@@ -131,8 +152,8 @@
         probs, slopes = [], []
         for h in range(2):
             span = slice(h * HEAD_DIM, (h + 1) * HEAD_DIM)
-            scores = dot_nt(keys, owns[h])
-            if hide is not None:
+            scores = dot_nt(keys[h], flagged[h]) if hide is FLAGS else dot_nt(keys, owns[h])
+            if hide is not None and hide is not FLAGS:
                 scores = hide(scores, 0)
             prob = jnp.exp(scores - log_sum[h : h + 1])
             grad_prob = dot_nt(values, grads[h])
@@ -151,14 +172,6 @@
     return grad_q.astype(BF), grad_kv
 
 
-def hide_after(limit):
-    def hide(scores, axis):
-        key = lax.broadcasted_iota(jnp.int32, scores.shape, axis)
-        return jnp.where(key < limit, scores, MASKED)
-
-    return hide
-
-
 def hide_future(start):
     def hide(scores, axis):
         key = lax.broadcasted_iota(jnp.int32, scores.shape, axis)
@@ -188,7 +201,7 @@
 
 
 def self_forward_kernel(
-    info, q_ref, k_ref, v_ref, pk_ref, pv_ref, out_ref, sum_ref, *, half, count, rows_p, block
+    info, q_ref, k_ref, v_ref, pk_ref, pv_ref, out_ref, sum_ref, flagged, *, half, count, rows_p, block
 ):
     step = pl.program_id(1)
     per = 2 * half // block
@@ -198,7 +211,9 @@
         def _():
             c = lax.div(step, per)
             base = pl.multiple_of(c * half, half)
-            segments = [(pk_ref[...], pv_ref[...], hide_after(info[c]))]
+            if pos == 0:
+                flag_keys(flagged, pk_ref[...], info[c])
+            segments = [((flagged[0], flagged[1]), pv_ref[...], FLAGS)]
             for source, offset, size, last in own_spans(pos, block, half):
                 rows = pl.ds(base + offset, size)
                 segments.append(
@@ -238,6 +253,7 @@
     acc_v,
     turned_p,
     turned,
+    flagged,
     *,
     half,
     count,
@@ -260,12 +276,13 @@
             c = lax.div(step, per)
             base = pl.multiple_of(c * half, half)
             if pos == 0:
+                flag_keys(flagged, pk_ref[...], info[c])
                 for source in range(2):
                     turned[:, source * half : (source + 1) * half] = k_ref[
                         source, pl.ds(base, half), :
                     ].T
             spans = own_spans(pos, block, half)
-            segments = [(pk_ref[...], turned_p[...], pv_ref[...], hide_after(info[c]))]
+            segments = [((flagged[0], flagged[1]), turned_p[...], pv_ref[...], FLAGS)]
             for source, offset, size, last in spans:
                 rows = pl.ds(base + offset, size)
                 at = source * half + offset
@@ -322,8 +339,7 @@
         prompt_ref[1] = (acc_pv[...] + grad_kv[0][1]).astype(BF)
 
 
-PAIR = 2 * HEAD_DIM
-BLOCK = 256
+BLOCK = 512
 
 
 def wide(rows, at, lead=()):
@@ -345,8 +361,8 @@
 
 
 def self_forward(joined, prompt_kv, info, half, count, rows_p):
-    rows, width = joined.shape[1], joined.shape[2] // 3
-    keys = prompt_kv.shape[0]
+    rows, width = joined[0].shape[1:]
+    keys = prompt_kv[0].shape[0]
     pairs = width // PAIR
     block = min(BLOCK, half)
     steps = count * 2 * half // block + 1
@@ -362,21 +378,22 @@
             grid=(pairs, steps),
             in_specs=[
                 wide(rows, 0, (2,)),
-                wide(rows, pairs, (2,)),
-                wide(rows, 2 * pairs, (2,)),
+                wide(rows, 0, (2,)),
+                wide(rows, 0, (2,)),
                 wide(keys, 0),
-                wide(keys, pairs),
+                wide(keys, 0),
             ],
             out_specs=[wide(rows, 0, (2,)), sums_spec(block)],
+            scratch_shapes=[pltpu.VMEM((2, keys, PAIR), BF)],
         ),
-        cost_estimate=cost(scores * 512, scores, joined, prompt_kv),
+        cost_estimate=cost(scores * 512, scores, *joined, *prompt_kv),
         name="self_forward",
-    )(info, joined, joined, joined, prompt_kv, prompt_kv)
+    )(info, *joined, *prompt_kv)
 
 
 def self_backward(joined, prompt_kv, info, out, grad, sums, half, count, rows_p):
-    rows, width = joined.shape[1], joined.shape[2] // 3
-    keys = prompt_kv.shape[0]
+    rows, width = joined[0].shape[1:]
+    keys = prompt_kv[0].shape[0]
     pairs = width // PAIR
     block = min(BLOCK, half)
     steps = count * 2 * half // block + 1
@@ -392,10 +409,10 @@
             grid=(pairs, steps),
             in_specs=[
                 wide(rows, 0, (2,)),
-                wide(rows, pairs, (2,)),
-                wide(rows, 2 * pairs, (2,)),
+                wide(rows, 0, (2,)),
+                wide(rows, 0, (2,)),
                 wide(keys, 0),
-                wide(keys, pairs),
+                wide(keys, 0),
                 wide(rows, 0, (2,)),
                 wide(rows, 0, (2,)),
                 sums_spec(block),
@@ -403,11 +420,12 @@
             out_specs=[wide(rows, 0, (3, 2)), wide(keys, 0, (2,))],
             scratch_shapes=[pltpu.VMEM((keys, PAIR), F32)] * 2
             + [pltpu.VMEM((2 * half, PAIR), F32)] * 2
-            + [pltpu.VMEM((PAIR, keys), BF), pltpu.VMEM((PAIR, 2 * half), BF)],
+            + [pltpu.VMEM((PAIR, keys), BF), pltpu.VMEM((PAIR, 2 * half), BF)]
+            + [pltpu.VMEM((2, keys, PAIR), BF)],
         ),
-        cost_estimate=cost(scores * 1280, scores, joined, prompt_kv, out, grad, joined),
+        cost_estimate=cost(scores * 1280, scores, *joined, *prompt_kv, out, grad, *joined),
         name="self_backward",
-    )(info, joined, joined, joined, prompt_kv, prompt_kv, out, grad, sums)
+    )(info, *joined, *prompt_kv, out, grad, sums)
 
 
 def cross_forward_kernel(q_ref, k_ref, v_ref, out_ref, sum_ref, *, full, rest, block):
@@ -512,6 +530,198 @@
     )(queries, enc_kv, enc_kv, out, grad, sums)
 
 
+def line_events(count):
+    return [None] + [(d, k) for k in range(count - 1) for d in (0, 1)]
+
+
+def gather_kernel(
+    w_ref, s_ref, c_ref, p_ref, w_out, s_out, x_out, own, x_sem, z_send, z_recv, p_send, p_recv, c_send, c_recv
+):
+    f, seq = lax.axis_index("fsdp"), lax.axis_index("seq")
+    count = w_out.shape[1] // 2
+    high, low = lax.div(f, 2), lax.rem(f, 2)
+    pair = {"fsdp": f + 1 - 2 * low}
+    core = {"seq": 1 - seq}
+    signs = (1, -1)
+
+    def inside(place):
+        return (place >= 0) & (place < count)
+
+    barrier = pltpu.get_barrier_semaphore()
+    for where in (pair, core):
+        pl.semaphore_signal(barrier, inc=1, device_id=where, device_id_type=MESH)
+    for sign in signs:
+
+        @pl.when(inside(high + sign))
+        def _():
+            pl.semaphore_signal(
+                barrier, inc=1, device_id={"fsdp": f + 2 * sign}, device_id_type=MESH
+            )
+
+    edges = jnp.where(high > 0, 1, 0) + jnp.where(high < count - 1, 1, 0)
+    pl.semaphore_wait(barrier, 2 + edges)
+
+    def remote(src, dst, send, recv, where):
+        return pltpu.make_async_remote_copy(
+            src_ref=src, dst_ref=dst, send_sem=send, recv_sem=recv, device_id=where, device_id_type=MESH
+        )
+
+    rows_c = c_ref.shape[0]
+    rows_p = p_ref.shape[0]
+    places = [x_out.at[seq, pl.ds(0, rows_c)], x_out.at[seq, pl.ds(rows_c, rows_p)]]
+    across = [
+        remote(src, dst, x_sem.at[0, i], x_sem.at[1, i], core)
+        for i, (src, dst) in enumerate(zip((c_ref, p_ref), places))
+    ]
+    local = [
+        pltpu.make_async_copy(w_ref, w_out.at[:, f], own.at[0]),
+        pltpu.make_async_copy(s_ref, s_out.at[:, f, seq], own.at[1]),
+        pltpu.make_async_copy(c_ref, places[0], own.at[2]),
+        pltpu.make_async_copy(p_ref, places[1], own.at[3]),
+    ]
+
+    def block(origin, side, first):
+        index = 2 * origin + side
+        held = (w_out.at[:, index], s_out.at[:, index, seq])
+        return held, ((w_ref, s_ref) if first else held)
+
+    def line_copies(d, k):
+        held, source = block(high - signs[d] * k, low, k == 0)
+        where = {"fsdp": f + 2 * signs[d]}
+        return [
+            remote(src, dst, z_send.at[d, k, i], z_recv.at[d, k, i], where)
+            for i, (src, dst) in enumerate(zip(source, held))
+        ]
+
+    def pair_copies(event, origin, first):
+        held, source = block(origin, low, first)
+        return [
+            remote(src, dst, p_send.at[event, i], p_recv.at[event, i], pair)
+            for i, (src, dst) in enumerate(zip(source, held))
+        ]
+
+    def core_copy(event, origin, side, first):
+        held, source = block(origin, side, first)
+        return remote(source[1], held[1], c_send.at[event], c_recv.at[event], core)
+
+    events = line_events(count)
+
+    def origin_of(event):
+        return high if event is None else high - signs[event[0]] * (event[1] + 1)
+
+    def sends_on(d, k):
+        return inside(high - signs[d] * k) & inside(high + signs[d])
+
+    def gets(event):
+        d, k = event
+        return inside(high - signs[d]) & inside(high - signs[d] * (k + 1))
+
+    def start_line(d, k):
+        @pl.when(sends_on(d, k))
+        def _():
+            for copy in line_copies(d, k):
+                copy.start()
+
+    for d in (0, 1):
+        start_line(d, 0)
+    for copy in pair_copies(0, high, True):
+        copy.start()
+    for copy in across:
+        copy.start()
+    core_copy(0, high, low, True).start()
+    for copy in local:
+        copy.start()
+    for number, event in enumerate(events[1:], 1):
+        d, k = event
+
+        @pl.when(gets(event))
+        def _():
+            origin = origin_of(event)
+            held, _ = block(origin, low, False)
+            for i, ref in enumerate(held):
+                remote(ref, ref, z_send.at[d, k, i], z_recv.at[d, k, i], pair).wait_recv()
+            if k + 1 < count - 1:
+
+                @pl.when(inside(high + signs[d]))
+                def _():
+                    for copy in line_copies(d, k + 1):
+                        copy.start()
+
+            for copy in pair_copies(number, origin, False):
+                copy.start()
+            core_copy(number, origin, low, False).start()
+
+    def finish(number, event):
+        origin = origin_of(event)
+        held, _ = block(origin, 1 - low, False)
+        for i, ref in enumerate(held):
+            remote(ref, ref, p_send.at[number, i], p_recv.at[number, i], pair).wait_recv()
+        core_copy(len(events) + number, origin, 1 - low, False).start()
+
+    def drain(number, event):
+        origin = origin_of(event)
+        for copy in pair_copies(number, origin, event is None):
+            copy.wait_send()
+        for place, side in ((number, low), (len(events) + number, 1 - low)):
+            copy = core_copy(place, origin, side, event is None and side is low)
+            copy.wait_send()
+            theirs = s_out.at[:, 2 * origin + side, 1 - seq]
+            remote(theirs, theirs, c_send.at[place], c_recv.at[place], core).wait_recv()
+
+    for act in (finish, drain):
+        for number, event in enumerate(events):
+            if event is None:
+                act(number, event)
+            else:
+                pl.when(gets(event))(functools.partial(act, number, event))
+    for d in (0, 1):
+        for k in range(count - 1):
+
+            @pl.when(sends_on(d, k))
+            def _():
+                for copy in line_copies(d, k):
+                    copy.wait_send()
+
+    for i, copy in enumerate(across):
+        copy.wait_send()
+        theirs = x_out.at[1 - seq, pl.ds(0, rows_c) if i == 0 else pl.ds(rows_c, rows_p)]
+        remote(theirs, theirs, x_sem.at[0, i], x_sem.at[1, i], core).wait_recv()
+    for copy in local:
+        copy.wait()
+
+
+def gather_start(w_own, s_own, cont_rows, prompt_rows):
+    chips = lax.axis_size("fsdp")
+    count = chips // 2
+    events = len(line_events(count))
+    rows = cont_rows.shape[0] + prompt_rows.shape[0]
+    dma = pltpu.SemaphoreType.DMA
+    vmem = pl.BlockSpec(memory_space=pltpu.VMEM)
+    kinds, depth, width = w_own.shape
+    return pl.pallas_call(
+        gather_kernel,
+        out_shape=(
+            jax.ShapeDtypeStruct((kinds, chips, depth, width), BF),
+            jax.ShapeDtypeStruct((2, chips, 2) + s_own.shape[1:], BF),
+            jax.ShapeDtypeStruct((2, rows, cont_rows.shape[1]), BF),
+        ),
+        in_specs=[vmem] * 4,
+        out_specs=[vmem] * 3,
+        scratch_shapes=[
+            dma((4,)),
+            dma((2, 2)),
+            dma((2, count - 1, 2)),
+            dma((2, count - 1, 2)),
+            dma((events, 2)),
+            dma((events, 2)),
+            dma((2 * events,)),
+            dma((2 * events,)),
+        ],
+        compiler_params=pltpu.CompilerParams(collective_id=0, has_side_effects=True),
+        name="gather_start",
+    )(w_own, s_own, cont_rows, prompt_rows)
+
+
 def exchange(value):
     return lax.all_to_all(value, "seq", split_axis=0, concat_axis=0, tiled=True)
 
@@ -543,31 +753,30 @@
     rows_c = count * half
     reach = prefix[0]
 
-    own_cols = lax.dynamic_slice_in_dim(w_qkv.reshape(shard, 3, 2, hg), seq, 1, 2)
-    wq = lax.all_gather(own_cols.reshape(shard, 3 * hg), "fsdp", axis=0, tiled=True)
-    shared = lax.all_gather(
-        jnp.concatenate([prompt_in[0], enc_in[0]], 0), ("fsdp", "seq"), axis=0
-    )
-    prompt_all = shared[:, :rows_p].reshape(-1, width)
-    enc_all = shared[:, rows_p:].reshape(-1, width)
+    own = lax.dynamic_index_in_dim(w_qkv.reshape(shard, 3, 2, hg), seq, 2, False).swapaxes(0, 1)
+    pair = jnp.stack([prompt_in[0], enc_in[0]], 0)
+    wq, shared, x_all = gather_start(own, pair, cont_in[0].reshape(rows_c, width), prompt_in[0])
+    wq = wq.reshape(3, -1, hg)
+    prompt_all = shared[0].reshape(-1, width)
+    enc_all = shared[1].reshape(-1, width)
     norms = jnp.concatenate([norm_gain, norm_bias], 0).T
     norms = jnp.pad(norms, ((0, 0), (0, 128 - norms.shape[1])))
-    mixed = gather_rows(jnp.concatenate([w_attn_out, w_cross_q, w_cross_out, w_cross_kv, norms], 1))
+    mixed = jnp.concatenate([w_attn_out, w_cross_q, w_cross_out, w_cross_kv, norms], 1)
+    mixed, x_all = lax.optimization_barrier((mixed, x_all))
+    mixed = gather_rows(mixed)
     wo = mixed[:, :width]
     wcq = mixed[:, width : 2 * width]
     wco = mixed[:, 2 * width : 3 * width]
     wckv = mixed[:, 3 * width : 5 * width]
     norms = mixed[:, 5 * width :].astype(F32).T
+    w_ffn_in, w_ffn_out, x_all = lax.optimization_barrier((w_ffn_in, w_ffn_out, x_all))
     w1 = gather_rows(w_ffn_in)
     w2 = gather_rows(w_ffn_out)
 
     mine = jnp.concatenate([cont_in[0].reshape(rows_c, width), prompt_in[0]], 0)
-    x_low, x_high = both_halves(mine)
-    x_all = jnp.stack([x_low, x_high], 0)
-    joined = lax.dot_general(
-        x_all, wq, (((2,), (0,)), ((), ())), preferred_element_type=F32
-    ).astype(BF)
-    prompt_kv = mm(prompt_all, wq[:, hg:]).astype(BF)
+    flat = x_all.reshape(-1, width)
+    joined = tuple(mm(flat, w).astype(BF).reshape(2, -1, hg) for w in wq)
+    prompt_kv = (mm(prompt_all, wq[1]).astype(BF), mm(prompt_all, wq[2]).astype(BF))
     info = jnp.concatenate([reach, lax.axis_index("fsdp")[None] * (2 * rows_p)])
     att, sums = self_forward(joined, prompt_kv, info, half, count, rows_p)
     att_rows = exchange(att)
@@ -622,23 +831,20 @@
     grad_joined, grad_pkv = self_backward(
         joined, prompt_kv, info, att, grad_att, sums, half, count, rows_p
     )
-    grad_joined, g_mixed = lax.optimization_barrier((grad_joined, g_mixed))
-    flat = x_all.reshape(-1, width)
     g_q, g_k, g_v = (mm_tn(flat, grad_joined[i].reshape(-1, hg)) for i in range(3))
     g_k = g_k + mm_tn(prompt_all, grad_pkv[0])
     g_v = g_v + mm_tn(prompt_all, grad_pkv[1])
-    grad_pr = mm_nt(grad_pkv[0], wq[:, hg : 2 * hg]) + mm_nt(grad_pkv[1], wq[:, 2 * hg :])
+    grad_pr = mm_nt(grad_pkv[0], wq[1]) + mm_nt(grad_pkv[1], wq[2])
     chips = lax.axis_size("fsdp")
     last = [g_q, g_k, g_v, grad_pr[:, :hg], grad_pr[:, hg:]]
     last = jnp.concatenate([v.astype(BF).reshape(chips, -1, hg) for v in last], 1)
-    last = lax.psum_scatter(
-        last.reshape(-1, hg), "fsdp", scatter_dimension=0, tiled=True
-    )
+    last, g_mixed = lax.optimization_barrier((last.reshape(-1, hg), g_mixed))
+    last = lax.psum_scatter(last, "fsdp", scatter_dimension=0, tiled=True)
     q_low, q_high = both_halves(over_groups(last[: 3 * shard]))
     g_qkv = [v.reshape(3, shard, hg) for v in (q_low, q_high)]
     g_qkv = jnp.concatenate([g_qkv[i % 2][i // 2] for i in range(6)], 1).astype(F32)
     grad_x = sum(
-        mm_nt(grad_joined[i].reshape(-1, hg), wq[:, i * hg : (i + 1) * hg]) for i in range(3)
+        mm_nt(grad_joined[i].reshape(-1, hg), wq[i]) for i in range(3)
     )
     grad_x = grad_x.astype(BF).reshape(x_all.shape)
     cont_x = exchange(grad_x[:, :rows_c])

time: 690 us -> 638 us (0.925)
  waiting for transfers between devices: 166 us -> 95.2 us
  Pallas kernels: 210 us -> 249 us
  other arithmetic: 54.1 us -> 36.2 us
    all_gather x2 -> x0, waiting for transfers between devices: 70.1 us -> none  [the longest x1 37.6 us: on_device(): lax.all_gather(jnp.concatenate([prompt_in[0], enc_in[0]], 0), ('fsdp', 's...]
    pallas_call x0 -> x1, Pallas kernels: none -> 50.7 us  [gather_start(): pl.pallas_call(gather_kernel, out_shape=(jax.ShapeDtypeStruct((kinds, chi...]
    ppermute x7 -> x6, waiting for transfers between devices: 1.29 us -> 18.9 us  [swap(): return lax.ppermute(value, axis, [(0, 1), (1, 0)])]
    all_gather x3, waiting for transfers between devices: 38.4 us -> 23.6 us  [gather_rows(): return lax.all_gather(half_rows(shard), ('fsdp', 'seq'), axis=0, tiled=True)]
    dot_general x8 -> x12, matrix products: 43.1 us -> 53.3 us  [mm(): return jnp.dot(a, b, preferred_element_type=F32)]
    dot_general x1 -> x0, matrix products: 9.31 us -> none  [on_device(): lax.dot_general(x_all, wq, (((2,), (0,)), ((), ())), preferred_element_ty...]
    reduce_scatter x1, waiting for transfers between devices: 38.9 us -> 32 us  [on_device(): last = lax.psum_scatter(last, 'fsdp', scatter_dimension=0, tiled=True)]
    all_to_all x4 -> x3, starting transfers between devices: 17.3 us -> 11.8 us  [exchange(): return lax.all_to_all(value, 'seq', split_axis=0, concat_axis=0, tiled=True)]
  transfers between devices with their start and end apart: 19 -> 15, of which waited for: 9 -> 7; matrix products, arithmetic and copies ran while one was open for 25% -> 23% of each run, Pallas kernels for 31% -> 31%
where the time goes in v3:
time: 638 us; the launch traced here: 630 us
  Pallas kernels  249 us (39%)
  matrix products  156 us (24%)
  waiting for transfers between devices  95.2 us (15%)
  local copies, waits for them, and re-layouts  54.1 us (8%)
  other arithmetic  36.2 us (6%)
  starting transfers between devices  17.9 us (3%)
  between operations  15.5 us (2%)
  blocking collectives  6.66 us (1%)
    pallas_call x1, Pallas kernels, self_backward(): pl.pallas_call(functools.partial(self_backward_kernel, half=half, count=c...  70.9 us
    dot_general x13, matrix products, mm_nt(): lax.dot_general(a, b, (((1,), (1,)), ((), ())), preferred_element_type=F32)  61.6 us
    dot_general x12, matrix products, mm(): return jnp.dot(a, b, preferred_element_type=F32)  53.3 us
    pallas_call x1, Pallas kernels, gather_start(): pl.pallas_call(gather_kernel, out_shape=(jax.ShapeDtypeStruct((kinds, chi...  50.7 us
    pallas_call x1, Pallas kernels, self_forward(): pl.pallas_call(functools.partial(self_forward_kernel, half=half, count=co...  47.5 us
    pallas_call x1, Pallas kernels, cross_backward(): pl.pallas_call(functools.partial(cross_backward_kernel, full=full, rest=r...  45.2 us
    dot_general x13, matrix products, mm_tn(): lax.dot_general(a, b, (((0,), (0,)), ((), ())), preferred_element_type=F32)  41 us
    pallas_call x1, Pallas kernels, cross_forward(): pl.pallas_call(functools.partial(cross_forward_kernel, full=full, rest=ro...  34.1 us
  transfers between devices with their start and end apart: 15, of which 7 were waited for; matrix products, arithmetic and copies ran while one was open for 23% of the time, Pallas kernels for 31%

profile of v3, /device:TPU:0, one launch (start us, length us, event | category | flops | bytes accessed | tf_op | source)
XLA Modules:
  0.0 630.2 jit_solution(9001415005834559068)
XLA Ops:
  14.1 50.7 %gather_start.1 = (bf16[3,8,96,384]{3,2,1,0:T(8,128)(2,1)}, bf16[2,8,2,64,768]{4,3,2,1,0:T(8,128)(2,1)}, bf16[2,1088,768]{2,1,0:T(8,128)(2,1)}) custom-call(bf16[3,96,384]{2,1,0:T(8,128)(2,1)} %bitcast.210, bf16[2,64,768]{2,1,0:T(8,128)(2,1)} %pad_maximum_fusion.4.s_ref, bf16[1024,768]{1,0:T(8,128)(2,1)} %bitcast.173, bf16[64,768]{1,0:T(8,128)(2,1)} %bitcast.208), custom_call_target="tpu_custom_call" | custom-call | tf_op jit(solution)/shard_map/gather_start/pallas_call | solution.py:701
  73.9 3.1 convolution_convert_fusion.3
  82.2 3.4 convolution_convert_fusion.15.pk_ref
  85.6 3.1 convolution_convert_fusion.4
  88.7 47.5 %self_forward.1 = (bf16[2,1088,384]{2,1,0:T(8,128)(2,1)}, f32[3,5,8,512]{3,2,1,0:T(8,128)}) custom-call(s32[3]{0:T(128)} %pad_add_fusion.info, bf16[2,1088,384]{2,1,0:T(8,128)(2,1)} %bitcast.227, bf16[2,1088,384]{2,1,0:T(8,128)(2,1)} %bitcast.225, bf16[2,1088,384]{2,1,0:T(8,128)(2,1)} %bitcast.223, bf16[1024,384]{1,0:T(8,128)(2,1)} %convolution_convert_fusion.15.pk_ref, ...), custom_call_target="tpu_custom_call" | custom-call | flops 10066329600 | bytes 6586368 | tf_op jit(solution)/shard_map/self_forward/pallas_call | solution.py:370
  136.2 3.7 all-to-all-start
  153.0 4.2 convolution_convert_fusion.5.k_ref.v_ref
  157.1 34.1 %cross_forward.1 = (bf16[1088,768]{1,0:T(8,128)(2,1)}, f32[6,3,8,512]{3,2,1,0:T(8,128)}) custom-call(bf16[1088,768]{1,0:T(8,128)(2,1)} %convolution_convert_fusion.7.q_ref, bf16[1024,1536]{1,0:T(8,128)(2,1)} %convolution_convert_fusion.5.k_ref.v_ref, bf16[1024,1536]{1,0:T(8,128)(2,1)} %convolution_convert_fusion.5.k_ref.v_ref), custom_call_target="tpu_custom_call" | custom-call | flops 6845104128 | bytes 4816896 | tf_op jit(solution)/shard_map/cross_forward/pallas_call | solution.py:490
  191.3 3.5 fusion.68
  197.2 12.3 %multiply_convert_fusion = (bf16[1088,3072]{1,0:T(8,128)(2,1)}, f32[1088,3072]{1,0:T(8,128)}) fusion(bf16[768,3072]{1,0:T(8,128)(2,1)} %all-gather.6.cloned.1.call-done, f32[1088,768]{1,0:T(8,128)} %copy-done.8, f32[768]{0:T(1024)S(1)} %get-tuple-element.75, f32[768]{0:T(1024)S(1)} %get-tuple-element.76, f32[1088]{0:T(1024)S(1)} %add_rsqrt_fusion.1, ...), kind=kOutput, calls=%fused_computation.7 | convolution fusion | flops 5154717696 | bytes 28129792 | tf_op jit(solution)/shard_map/dot_general | solution.py:22
  209.5 23.6 %all-gather.8.cloned.1.call-done = bf16[3072,768]{1,0:T(8,128)(2,1)} async-done(((bf16[192,768]{1,0:T(8,128)(2,1)}), bf16[3072,768]{1,0:T(8,128)(2,1)}) %all-gather.8.cloned.1.call-update) | async-done | bytes 4718608 | tf_op jit(solution)/shard_map/all_gather | solution.py:43
  233.0 11.1 %fusion.69 = (f32[1088]{0:T(1024)S(1)}, f32[1088,768]{1,0:T(8,128)S(1)}) fusion(bf16[1088,3072]{1,0:T(8,128)(2,1)} %get-tuple-element.130, bf16[3072,768]{1,0:T(8,128)(2,1)} %all-gather.8.cloned.1.call-done, f32[768]{0:T(1024)S(1)} %get-tuple-element.75, f32[768]{0:T(1024)S(1)} %get-tuple-element.76, f32[1088]{0:T(1024)S(1)} %add_rsqrt_fusion.1, ...), kind=kOutput, calls=%fused_computation.207 | convolution fusion | flops 5138840576 | bytes 18107136 | tf_op jit(solution)/shard_map/dot_general | solution.py:22
  246.7 4.6 fusion.13
  251.3 12.3 %convolution_convert_fusion.1 = bf16[3072,768]{1,0:T(8,128)(2,1)} fusion(bf16[1088,3072]{1,0:T(8,128)(2,1)} %get-tuple-element.130, f32[1088,768]{1,0:T(8,128)S(1)} %get-tuple-element.133, f32[1088]{0:T(1024)S(1)} %get-tuple-element.136, f32[1088]{0:T(1024)S(1)} %get-tuple-element.137, f32[768]{0:T(1024)S(1)} %copy-done.52, f32[1088]{0:T(1024)S(1)} %add_rsqrt_fusion, ...), kind=kOutput, calls=%fused_computation.12 | convolution fusion | flops 5146214400 | bytes 16437248 | tf_op jit(solution)/shard_map/dot_general | solution.py:26
  263.7 17.7 %fusion.5 = bf16[1088,3072]{1,0:T(8,128)(2,1)} fusion(bf16[3072,768]{1,0:T(8,128)(2,1)S(1)} %bitcast.221, f32[1088,3072]{1,0:T(8,128)} %get-tuple-element.131, f32[1088,768]{1,0:T(8,128)S(1)} %get-tuple-element.133, f32[1088]{0:T(1024)S(1)} %get-tuple-element.136, f32[1088]{0:T(1024)S(1)} %get-tuple-element.137, f32[768]{0:T(1024)S(1)} %copy-done.52, ...), kind=kOutput, calls=%fused_computation.9 | convolution fusion | flops 5183963136 | bytes 29806592 | tf_op jit(solution)/shard_map/dot_general | solution.py:30
  281.5 10.0 %convolution_convert_fusion = bf16[768,3072]{1,0:T(8,128)(2,1)S(1)} fusion(bf16[1088,3072]{1,0:T(8,128)(2,1)} %fusion.5, f32[1088,768]{1,0:T(8,128)S(1)} %copy-done.9, f32[768]{0:T(1024)S(1)} %copy-done.60, f32[768]{0:T(1024)S(1)} %copy-done.50, f32[1088]{0:T(1024)S(1)} %add_rsqrt_fusion.1, f32[1088]{0:T(1024)S(1)} %broadcast_multiply_fusion.7), kind=kOutput, calls=%fused_computation.11 | convolution fusion | flops 5140365312 | bytes 14760448 | tf_op jit(solution)/shard_map/dot_general | solution.py:26
  295.8 14.8 %multiply_reduce_fusion = (bf16[768]{0:T(1024)(128)(2,1)}, f32[1088]{0:T(1024)}, f32[1088]{0:T(1024)}, bf16[768]{0:T(1024)(128)(2,1)}, f32[1088,768]{1,0:T(8,128)}) fusion(f32[1088,768]{1,0:T(8,128)S(1)} %copy-done.9, f32[1088]{0:T(1024)} %copy-done.47, f32[1088]{0:T(1024)S(1)} %broadcast_multiply_fusion.7, f32[768]{0:T(1024)} %copy-done.49, ...), kind=kOutput, calls=%fused_computation.34 | convolution fusion | flops 5151371264 | bytes 23145472 | tf_op jit(solution)/shard_map/dot_general | solution.py:30
  316.0 3.4 fusion.55
  322.4 4.5 convolution_convert_fusion.6.grad_ref
  326.9 45.2 %cross_backward.1 = (bf16[1088,768]{1,0:T(8,128)(2,1)}, bf16[1024,768]{1,0:T(8,128)(2,1)}, bf16[1024,768]{1,0:T(8,128)(2,1)}) custom-call(bf16[1088,768]{1,0:T(8,128)(2,1)} %convolution_convert_fusion.7.q_ref, bf16[1024,1536]{1,0:T(8,128)(2,1)} %convolution_convert_fusion.5.k_ref.v_ref, bf16[1024,1536]{1,0:T(8,128)(2,1)} %convolution_convert_fusion.5.k_ref.v_ref, ...), custom_call_target="tpu_custom_call" | custom-call | flops 17112760320 | bytes 8159232 | tf_op jit(solution)/shard_map/cross_backward/pallas_call | solution.py:510
  372.1 6.6 %multiply_reduce_fusion.1 = (bf16[768]{0:T(1024)(128)(2,1)S(1)}, f32[1088]{0:T(1024)S(1)}, f32[1088]{0:T(1024)S(1)}, bf16[768]{0:T(1024)(128)(2,1)S(1)}, f32[1088,768]{1,0:T(8,128)}) fusion(f32[1088,768]{1,0:T(8,128)S(1)} %get-tuple-element.127, f32[1088]{0:T(1024)S(1)} %copy-done.46, f32[1088]{0:T(1024)S(1)} %broadcast_multiply_fusion.8, ...), kind=kOutput, calls=%fused_computation.35 | convolution fusion | flops 1291809280 | bytes 12901376 | tf_op jit(solution)/shard_map/dot_general | solution.py:30
  379.3 3.9 fusion.54
  389.2 4.7 all-to-all-start.1
  419.0 11.5 %reduce-scatter.4.cloned.1.call-done = bf16[384,768]{1,0:T(8,128)(2,1)} async-done(((bf16[6144,768]{1,0:T(8,128)(2,1)}), bf16[384,768]{1,0:T(8,128)(2,1)}) %reduce-scatter.4.cloned.1.call-update) | async-done | bytes 589840 | tf_op jit(solution)/shard_map/reduce_scatter | solution.py:55
  430.7 70.9 %self_backward.1 = (bf16[3,2,1088,384]{3,2,1,0:T(8,128)(2,1)}, bf16[2,1024,384]{2,1,0:T(8,128)(2,1)}) custom-call(s32[3]{0:T(128)} %pad_add_fusion.info, bf16[2,1088,384]{2,1,0:T(8,128)(2,1)} %bitcast.228, bf16[2,1088,384]{2,1,0:T(8,128)(2,1)} %bitcast.226, bf16[2,1088,384]{2,1,0:T(8,128)(2,1)} %bitcast.224, ...), custom_call_target="tpu_custom_call" | custom-call | flops 25165824000 | bytes 14942208 | tf_op jit(solution)/shard_map/self_backward/pallas_call | solution.py:401
  501.7 3.1 fusion.56
  520.2 9.0 %reduce-scatter.6.cloned.1.call-done = bf16[320,768]{1,0:T(8,128)(2,1)} async-done(((bf16[5120,768]{1,0:T(8,128)(2,1)}), bf16[320,768]{1,0:T(8,128)(2,1)}) %reduce-scatter.6.cloned.1.call-update) | async-done | bytes 491536 | tf_op jit(solution)/shard_map/reduce_scatter | solution.py:55
  538.9 9.3 %collective-permute-done.4 = bf16[384,768]{1,0:T(8,128)(2,1)S(1)} collective-permute-done((bf16[384,768]{1,0:T(8,128)(2,1)S(1)}, bf16[384,768]{1,0:T(8,128)(2,1)S(1)}, u32[]{:S(2)}, u32[]{:S(2)}) %collective-permute-start.4) | collective-permute-done | bytes 589856 | tf_op jit(solution)/shard_map/ppermute | solution.py:34
  551.0 6.7 %all_to_all.20 = bf16[2,1024,768]{2,1,0:T(8,128)(2,1)S(1)} all-to-all(bf16[2,1024,768]{2,1,0:T(8,128)(2,1)S(1)} %slice.383), channel_id=1, replica_groups=mesh['grp'=2,'fsdp'=8,'seq'=2] {'seq'}, dimensions={0} | all-to-all | bytes 6291456 | tf_op jit(solution)/shard_map/all_to_all | solution.py:726
  561.5 9.6 %collective-permute-done.2 = bf16[256,768]{1,0:T(8,128)(2,1)S(1)} collective-permute-done((bf16[256,768]{1,0:T(8,128)(2,1)S(1)}, bf16[256,768]{1,0:T(8,128)(2,1)S(1)}, u32[]{:S(2)}, u32[]{:S(2)}) %collective-permute-start.2) | collective-permute-done | bytes 393248 | tf_op jit(solution)/shard_map/ppermute | solution.py:34
  578.2 32.0 %reduce-scatter.8.cloned.1.call-done = bf16[544,384]{1,0:T(8,128)(2,1)} async-done(((bf16[4352,384]{1,0:T(8,128)(2,1)}), bf16[544,384]{1,0:T(8,128)(2,1)}) %reduce-scatter.8.cloned.1.call-update) | async-done | bytes 417808 | tf_op jit(solution)/shard_map/reduce_scatter | solution.py:842
  615.3 3.4 all-to-all-start.2
  (304 shorter events, 130.9 us)
Async XLA Ops:
  7.2 58.5 %copy-start = (bf16[96,3072]{1,0:T(8,128)(2,1)S(1)}, bf16[96,3072]{1,0:T(8,128)(2,1)}, u32[]{:S(2)}) copy-start(bf16[96,3072]{1,0:T(8,128)(2,1)} %param.26) | copy-start | bytes 1769476
  7.2 132.8 %all-gather.4.cloned.1.call-start = ((), (), s32[]{:S(2)}) async-start(), calls=%async_computation.7 | async-start | bytes 6475776 | tf_op jit(solution)/shard_map/all_gather | solution.py:43
  65.6 131.6 %all-gather.6.cloned.1.call-start = ((), (), s32[]{:S(2)}) async-start(), calls=%async_computation.8 | async-start | bytes 5013504 | tf_op jit(solution)/shard_map/all_gather | solution.py:43
  66.4 166.6 %all-gather.8.cloned.1.call-start = ((), (), s32[]{:S(2)}) async-start(), calls=%async_computation.9 | async-start | bytes 5013504 | tf_op jit(solution)/shard_map/all_gather | solution.py:43
  136.2 6.2 all-to-all-start
  139.9 290.6 %reduce-scatter.4.cloned.1.call-start = ((), (), s32[]{:S(2)}) async-start(), calls=%async_computation.10 | async-start | bytes 10027008 | tf_op jit(solution)/shard_map/reduce_scatter | solution.py:55
  142.4 48.9 %copy-start.57 = (f32[768]{0:T(1024)}, f32[768]{0:T(1024)S(1)}, u32[]{:S(2)}) copy-start(f32[768]{0:T(1024)S(1)} %get-tuple-element.77) | copy-start | bytes 9220
  142.4 90.7 %copy-start.49 = (f32[768]{0:T(1024)}, f32[768]{0:T(1024)S(1)}, u32[]{:S(2)}) copy-start(f32[768]{0:T(1024)S(1)} %get-tuple-element.76) | copy-start | bytes 9220
  142.4 90.7 %copy-start.59 = (f32[768]{0:T(1024)}, f32[768]{0:T(1024)S(1)}, u32[]{:S(2)}) copy-start(f32[768]{0:T(1024)S(1)} %get-tuple-element.75) | copy-start | bytes 9220
  150.0 41.3 %copy-start.45 = (f32[1088]{0:T(1024)}, f32[1088]{0:T(1024)S(1)}, u32[]{:S(2)}) copy-start(f32[1088]{0:T(1024)S(1)} %add_rsqrt_fusion.2) | copy-start | bytes 13060
  197.1 84.3 %copy-start.47 = (f32[1088]{0:T(1024)}, f32[1088]{0:T(1024)S(1)}, u32[]{:S(2)}) copy-start(f32[1088]{0:T(1024)S(1)} %add_rsqrt_fusion.1) | copy-start | bytes 13060
  244.1 19.5 %copy-start.11 = (f32[1088,768]{1,0:T(8,128)}, f32[1088,768]{1,0:T(8,128)S(1)}, u32[]{:S(2)}) copy-start(f32[1088,768]{1,0:T(8,128)S(1)} %get-tuple-element.133) | copy-start | bytes 10027012
  244.7 18.9 %copy-start.44 = (f32[1088]{0:T(1024)}, f32[1088]{0:T(1024)S(1)}, u32[]{:S(2)}) copy-start(f32[1088]{0:T(1024)S(1)} %add_rsqrt_fusion) | copy-start | bytes 13060
  246.7 17.0 %slice-start = ((s8[4718592]{0:T(1024)(128)(4,1)}), s8[4194304]{0:T(1024)(128)(4,1)S(1)}, s32[]{:S(2)}) async-start(s8[4718592]{0:T(1024)(128)(4,1)} %bitcast.220), calls=%async_computation.13 | async-start | bytes 8388608
  251.3 12.4 %copy-start.55 = (f32[1088]{0:T(1024)}, f32[1088]{0:T(1024)S(1)}, u32[]{:S(2)}) copy-start(f32[1088]{0:T(1024)S(1)} %get-tuple-element.136) | copy-start | bytes 13060
  251.3 12.4 %copy-start.56 = (f32[1088]{0:T(1024)}, f32[1088]{0:T(1024)S(1)}, u32[]{:S(2)}) copy-start(f32[1088]{0:T(1024)S(1)} %get-tuple-element.137) | copy-start | bytes 13060
  251.3 12.4 %slice-start.1 = ((s8[4718592]{0:T(1024)(128)(4,1)}), s8[524288]{0:T(1024)(128)(4,1)S(1)}, s32[]{:S(2)}) async-start(s8[4718592]{0:T(1024)(128)(4,1)} %bitcast.220), calls=%async_computation.14 | async-start | bytes 1048576
  263.7 17.7 %copy-start.9 = (f32[1088,768]{1,0:T(8,128)S(1)}, f32[1088,768]{1,0:T(8,128)}, u32[]{:S(2)}) copy-start(f32[1088,768]{1,0:T(8,128)} %copy-done.8) | copy-start | bytes 10027012
  263.7 17.7 %copy-start.50 = (f32[768]{0:T(1024)S(1)}, f32[768]{0:T(1024)}, u32[]{:S(2)}) copy-start(f32[768]{0:T(1024)} %copy-done.49) | copy-start | bytes 9220
  263.7 17.7 %copy-start.60 = (f32[768]{0:T(1024)S(1)}, f32[768]{0:T(1024)}, u32[]{:S(2)}) copy-start(f32[768]{0:T(1024)} %copy-done.59) | copy-start | bytes 9220
  326.8 45.2 %copy-start.46 = (f32[1088]{0:T(1024)S(1)}, f32[1088]{0:T(1024)}, u32[]{:S(2)}) copy-start(f32[1088]{0:T(1024)} %copy-done.45) | copy-start | bytes 13060
  389.2 29.8 %all-to-all-start.1 = ((bf16[2,1088,384]{2,1,0:T(8,128)(2,1)}), bf16[2,1088,384]{2,1,0:T(8,128)(2,1)}, u32[]{:S(2)}, u32[]{:S(2)}) async-start(bf16[2,1088,384]{2,1,0:T(8,128)(2,1)} %pad_maximum_fusion.1), calls=%async_computation.1 | async-start | bytes 3342336 | tf_op jit(solution)/shard_map/all_to_all | solution.py:726
  393.9 135.3 %reduce-scatter.6.cloned.1.call-start = ((), (), s32[]{:S(2)}) async-start(), calls=%async_computation.11 | async-start | bytes 8355840 | tf_op jit(solution)/shard_map/reduce_scatter | solution.py:55
  430.5 179.6 %reduce-scatter.8.cloned.1.call-start = ((), (), s32[]{:S(2)}) async-start(), calls=%async_computation.12 | async-start | bytes 3760128 | tf_op jit(solution)/shard_map/reduce_scatter | solution.py:842
  533.5 14.7 %collective-permute-start.4 = (bf16[384,768]{1,0:T(8,128)(2,1)S(1)}, bf16[384,768]{1,0:T(8,128)(2,1)S(1)}, u32[]{:S(2)}, u32[]{:S(2)}) collective-permute-start(bf16[384,768]{1,0:T(8,128)(2,1)S(1)} %copy-done.38), channel_id=1, source_target_pairs={{0,16},{16,0},{1,17},{17,1},{2,18},{18,2},{3,19},{19,3},{4,20},{20... | collective-permute-start | bytes 1769480 | tf_op jit(solution)/shard_map/ppermute | solution.py:34
  548.6 11.1 %collective-permute-start.5 = (bf16[384,768]{1,0:T(8,128)(2,1)S(1)}, bf16[384,768]{1,0:T(8,128)(2,1)S(1)}, u32[]{:S(2)}, u32[]{:S(2)}) collective-permute-start(bf16[384,768]{1,0:T(8,128)(2,1)S(1)} %add_convert_fusion.4), channel_id=1, source_target_pairs={{0,1},{1,0},{2,3},{3,2},{4,5},{5,4},{6,7},{7,6},{8,9},{9,8},{10,11... | collective-permute-start | bytes 1769480 | tf_op jit(solution)/shard_map/ppermute | solution.py:34
  559.9 11.2 %collective-permute-start.2 = (bf16[256,768]{1,0:T(8,128)(2,1)S(1)}, bf16[256,768]{1,0:T(8,128)(2,1)S(1)}, u32[]{:S(2)}, u32[]{:S(2)}) collective-permute-start(bf16[256,768]{1,0:T(8,128)(2,1)S(1)} %pad_maximum_fusion.3), channel_id=1, source_target_pairs={{0,16},{16,0},{1,17},{17,1},{2,18},{18,2},{3,19},{19,3},{4,20},{20... | collective-permute-start | bytes 1179656 | tf_op jit(solution)/shard_map/ppermute | solution.py:34
  571.3 3.0 collective-permute-start.3
  577.3 45.8 %copy-start.1 = (bf16[96,3072]{1,0:T(8,128)(2,1)S(1)}, bf16[96,3072]{1,0:T(8,128)(2,1)}, u32[]{:S(2)}) copy-start(bf16[96,3072]{1,0:T(8,128)(2,1)} %param.26) | copy-start | bytes 1769476
  611.1 7.6 %collective-permute-start = (bf16[288,384]{1,0:T(8,128)(2,1)S(1)}, bf16[288,384]{1,0:T(8,128)(2,1)S(1)}, u32[]{:S(2)}, u32[]{:S(2)}) collective-permute-start(bf16[288,384]{1,0:T(8,128)(2,1)S(1)} %slice.386), channel_id=1, source_target_pairs={{0,16},{16,0},{1,17},{17,1},{2,18},{18,2},{3,19},{19,3},{4,20},{20... | collective-permute-start | bytes 663560 | tf_op jit(solution)/shard_map/ppermute | solution.py:34
  615.3 5.0 all-to-all-start.2
  619.7 2.2 collective-permute-start.1
  (53 other events, 209.6 us)
Sparse Core Ops, SparseCore 0:
  65.7 57.9 all-gather.3
  126.6 51.7 all-gather.5
  181.3 51.6 all-gather.7
  320.7 109.7 reduce-scatter.3
  434.4 94.7 reduce-scatter.5
  532.7 77.4 reduce-scatter.7

commit v4 on v3

--- a/solution.py
+++ b/solution.py
@@ -43,14 +43,6 @@
     return lax.all_gather(half_rows(shard), ("fsdp", "seq"), axis=0, tiled=True)
 
 
-def both_halves(mine):
-    other = swap(mine, "seq")
-    first = lax.axis_index("seq") == 0
-    low = jnp.where(first, mine, other)
-    high = jnp.where(first, other, mine)
-    return low, high
-
-
 def scatter_sum(value):
     return lax.psum_scatter(value, ("fsdp", "seq"), scatter_dimension=0, tiled=True)
 
@@ -62,8 +54,12 @@
     return jnp.concatenate(pieces, 1).reshape(-1, width)
 
 
-def over_groups(part):
-    return (part.astype(F32) + swap(part, "grp").astype(F32)).astype(BF)
+def total_halves(part):
+    across = [(i, 3 - i) for i in range(4)]
+    terms = (part, swap(part, "grp")), (swap(part, "seq"), lax.ppermute(part, ("grp", "seq"), across))
+    mine, other = ((a.astype(F32) + b.astype(F32)).astype(BF) for a, b in terms)
+    first = lax.axis_index("seq") == 0
+    return jnp.where(first, mine, other), jnp.where(first, other, mine)
 
 
 def norm_stats(resid):
@@ -535,20 +531,22 @@
 
 
 def gather_kernel(
-    w_ref, s_ref, c_ref, p_ref, w_out, s_out, x_out, own, x_sem, z_send, z_recv, p_send, p_recv, c_send, c_recv
+    w_ref, s_ref, c_ref, p_ref, w_out, s_out, x_out, own, x_sem, z_send, z_recv, p_send, p_recv, g_send, g_recv, c_send, c_recv
 ):
     f, seq = lax.axis_index("fsdp"), lax.axis_index("seq")
     count = w_out.shape[1] // 2
     high, low = lax.div(f, 2), lax.rem(f, 2)
     pair = {"fsdp": f + 1 - 2 * low}
     core = {"seq": 1 - seq}
+    group = lax.axis_index("grp")
+    twin = {"grp": 1 - group}
     signs = (1, -1)
 
     def inside(place):
         return (place >= 0) & (place < count)
 
     barrier = pltpu.get_barrier_semaphore()
-    for where in (pair, core):
+    for where in (pair, core, twin):
         pl.semaphore_signal(barrier, inc=1, device_id=where, device_id_type=MESH)
     for sign in signs:
 
@@ -559,7 +557,7 @@
             )
 
     edges = jnp.where(high > 0, 1, 0) + jnp.where(high < count - 1, 1, 0)
-    pl.semaphore_wait(barrier, 2 + edges)
+    pl.semaphore_wait(barrier, 3 + edges)
 
     def remote(src, dst, send, recv, where):
         return pltpu.make_async_remote_copy(
@@ -600,6 +598,18 @@
             for i, (src, dst) in enumerate(zip(source, held))
         ]
 
+    def mine(origin):
+        return lax.rem(origin + group, 2) == 0
+
+    def start_pair(event, origin, first):
+        weights, rows = pair_copies(event, origin, first)
+        pl.when(mine(origin))(weights.start)
+        rows.start()
+
+    def twin_copy(event, origin):
+        held = w_out.at[:, 2 * origin + 1 - low]
+        return remote(held, held, g_send.at[event], g_recv.at[event], twin)
+
     def core_copy(event, origin, side, first):
         held, source = block(origin, side, first)
         return remote(source[1], held[1], c_send.at[event], c_recv.at[event], core)
@@ -624,8 +634,7 @@
 
     for d in (0, 1):
         start_line(d, 0)
-    for copy in pair_copies(0, high, True):
-        copy.start()
+    start_pair(0, high, True)
     for copy in across:
         copy.start()
     core_copy(0, high, low, True).start()
@@ -647,21 +656,34 @@
                     for copy in line_copies(d, k + 1):
                         copy.start()
 
-            for copy in pair_copies(number, origin, False):
-                copy.start()
+            start_pair(number, origin, False)
             core_copy(number, origin, low, False).start()
 
     def finish(number, event):
         origin = origin_of(event)
         held, _ = block(origin, 1 - low, False)
-        for i, ref in enumerate(held):
-            remote(ref, ref, p_send.at[number, i], p_recv.at[number, i], pair).wait_recv()
+
+        def pass_on():
+            ref = held[0]
+            remote(ref, ref, p_send.at[number, 0], p_recv.at[number, 0], pair).wait_recv()
+            twin_copy(number, origin).start()
+
+        pl.when(mine(origin))(pass_on)
+        ref = held[1]
+        remote(ref, ref, p_send.at[number, 1], p_recv.at[number, 1], pair).wait_recv()
         core_copy(len(events) + number, origin, 1 - low, False).start()
 
     def drain(number, event):
         origin = origin_of(event)
-        for copy in pair_copies(number, origin, event is None):
-            copy.wait_send()
+        weights, rows = pair_copies(number, origin, event is None)
+        rows.wait_send()
+
+        def sent():
+            weights.wait_send()
+            twin_copy(number, origin).wait_send()
+
+        pl.when(mine(origin))(sent)
+        pl.when(jnp.logical_not(mine(origin)))(twin_copy(number, origin).wait_recv)
         for place, side in ((number, low), (len(events) + number, 1 - low)):
             copy = core_copy(place, origin, side, event is None and side is low)
             copy.wait_send()
@@ -714,6 +736,8 @@
             dma((2, count - 1, 2)),
             dma((events, 2)),
             dma((events, 2)),
+            dma((events,)),
+            dma((events,)),
             dma((2 * events,)),
             dma((2 * events,)),
         ],
@@ -806,10 +830,11 @@
     owners = 2 * lax.axis_size("fsdp")
     columns = [slice(i, i + width) for i in range(0, g_w1.shape[1], width)]
     g_ffn = per_owner([g_w2] + [g_w1[:, cols] for cols in columns])
+    grad_pre, g_ffn = lax.optimization_barrier((grad_pre, g_ffn))
+    g_ffn = scatter_sum(g_ffn)
     grad_second = grad3 + mm_nt(grad_pre, w1)
     grad2, gain2, bias2 = norm_back(grad_second, hat2, scale2, norms[1])
-    low2, g_ffn = lax.optimization_barrier((grad2.astype(BF), g_ffn))
-    g_ffn = scatter_sum(g_ffn)
+    low2 = grad2.astype(BF)
     g_wco = mm_tn(cross, low2)
     grad_cross = mm_nt(low2, wco).astype(BF)
     grad_cq, grad_ck, grad_cv = cross_backward(cq, enc_kv, cross, grad_cross, cross_sum, rows_c)
@@ -840,7 +865,7 @@
     last = jnp.concatenate([v.astype(BF).reshape(chips, -1, hg) for v in last], 1)
     last, g_mixed = lax.optimization_barrier((last.reshape(-1, hg), g_mixed))
     last = lax.psum_scatter(last, "fsdp", scatter_dimension=0, tiled=True)
-    q_low, q_high = both_halves(over_groups(last[: 3 * shard]))
+    q_low, q_high = total_halves(last[: 3 * shard])
     g_qkv = [v.reshape(3, shard, hg) for v in (q_low, q_high)]
     g_qkv = jnp.concatenate([g_qkv[i % 2][i // 2] for i in range(6)], 1).astype(F32)
     grad_x = sum(
@@ -854,7 +879,7 @@
     prompt_x = exchange((grad_x[:, rows_c:].astype(F32) + grad_pr.astype(F32)).astype(BF))
     grad_prompt = grad1[rows_c:] + prompt_x[0].astype(F32) + prompt_x[1].astype(F32)
 
-    both = both_halves(over_groups(g_ffn))
+    both = total_halves(g_ffn)
     g_w2 = jnp.concatenate([v[: 2 * shard] for v in both], 0).astype(F32)
     mine = shard // 2
     g_w1 = [
@@ -865,7 +890,7 @@
     used = 5 * mine
     grad_enc = g_mixed[used : used + rows_p].astype(F32)
     g_mixed = jnp.concatenate([g_mixed[:used], g_mixed[used + rows_p :]], 0)
-    both = both_halves(over_groups(g_mixed))
+    both = total_halves(g_mixed)
     g_wo, g_wcq, g_wco, g_wck, g_wcv = (
         jnp.concatenate([v[i * mine : (i + 1) * mine] for v in both], 0).astype(F32)
         for i in range(5)

time: 638 us -> 616 us (0.966)
  waiting for transfers between devices: 95.2 us -> 76 us
    ppermute x0 -> x3, waiting for transfers between devices: none -> 18 us  [total_halves(): lax.ppermute(part, ('grp', 'seq'), across)]
    reduce_scatter x2, waiting for transfers between devices: 20.5 us -> 4.36 us  [scatter_sum(): lax.psum_scatter(value, ('fsdp', 'seq'), scatter_dimension=0, tiled=True)]
    ppermute x6, waiting for transfers between devices: 18.9 us -> 6.21 us  [swap(): return lax.ppermute(value, axis, [(0, 1), (1, 0)])]
    reduce_scatter x1, waiting for transfers between devices: 32 us -> 25.2 us  [on_device(): last = lax.psum_scatter(last, 'fsdp', scatter_dimension=0, tiled=True)]
    unnamed x171 -> x127, local copies, waits for them, and re-layouts: 28.5 us -> 27.7 us
  transfers between devices with their start and end apart: 15 -> 17, of which waited for: 7 -> 8; matrix products, arithmetic and copies ran while one was open for 23% -> 26% of each run, Pallas kernels for 31% -> 33%
where the time goes in v4:
time: 616 us; the launch traced here: 607 us
  Pallas kernels  251 us (41%)
  matrix products  155 us (25%)
  waiting for transfers between devices  76 us (12%)
  local copies, waits for them, and re-layouts  52.1 us (8%)
  other arithmetic  31 us (5%)
  starting transfers between devices  16.2 us (3%)
  between operations  15.5 us (3%)
  blocking collectives  10.5 us (2%)
    pallas_call x1, Pallas kernels, self_backward(): pl.pallas_call(functools.partial(self_backward_kernel, half=half, count=c...  70.5 us
    dot_general x13, matrix products, mm_nt(): lax.dot_general(a, b, (((1,), (1,)), ((), ())), preferred_element_type=F32)  63 us
    dot_general x12, matrix products, mm(): return jnp.dot(a, b, preferred_element_type=F32)  53.5 us
    pallas_call x1, Pallas kernels, gather_start(): pl.pallas_call(gather_kernel, out_shape=(jax.ShapeDtypeStruct((kinds, chi...  53.1 us
    pallas_call x1, Pallas kernels, self_forward(): pl.pallas_call(functools.partial(self_forward_kernel, half=half, count=co...  47.6 us
    pallas_call x1, Pallas kernels, cross_backward(): pl.pallas_call(functools.partial(cross_backward_kernel, full=full, rest=r...  45.4 us
    dot_general x13, matrix products, mm_tn(): lax.dot_general(a, b, (((0,), (0,)), ((), ())), preferred_element_type=F32)  38.9 us
    pallas_call x1, Pallas kernels, cross_forward(): pl.pallas_call(functools.partial(cross_forward_kernel, full=full, rest=ro...  34.1 us
  transfers between devices with their start and end apart: 17, of which 8 were waited for; matrix products, arithmetic and copies ran while one was open for 26% of the time, Pallas kernels for 33%

profile of v4, /device:TPU:0, one launch (start us, length us, event | category | flops | bytes accessed | tf_op | source)
XLA Modules:
  0.0 607.4 jit_solution(16176589535093156168)
XLA Ops:
  14.1 53.1 %gather_start.1 = (bf16[3,8,96,384]{3,2,1,0:T(8,128)(2,1)}, bf16[2,8,2,64,768]{4,3,2,1,0:T(8,128)(2,1)}, bf16[2,1088,768]{2,1,0:T(8,128)(2,1)}) custom-call(bf16[3,96,384]{2,1,0:T(8,128)(2,1)} %bitcast.207, bf16[2,64,768]{2,1,0:T(8,128)(2,1)} %pad_maximum_fusion.4.s_ref, bf16[1024,768]{1,0:T(8,128)(2,1)} %bitcast.170, bf16[64,768]{1,0:T(8,128)(2,1)} %bitcast.205), custom_call_target="tpu_custom_call" | custom-call | tf_op jit(solution)/shard_map/gather_start/pallas_call | solution.py:723
  73.3 3.1 convolution_convert_fusion.2
  76.4 3.1 convolution_convert_fusion.3
  84.6 3.4 convolution_convert_fusion.15.pk_ref
  88.0 3.1 convolution_convert_fusion.4
  91.0 47.6 %self_forward.1 = (bf16[2,1088,384]{2,1,0:T(8,128)(2,1)}, f32[3,5,8,512]{3,2,1,0:T(8,128)}) custom-call(s32[3]{0:T(128)} %pad_add_fusion.info, bf16[2,1088,384]{2,1,0:T(8,128)(2,1)} %bitcast.224, bf16[2,1088,384]{2,1,0:T(8,128)(2,1)} %bitcast.222, bf16[2,1088,384]{2,1,0:T(8,128)(2,1)} %bitcast.220, bf16[1024,384]{1,0:T(8,128)(2,1)} %convolution_convert_fusion.15.pk_ref, ...), custom_call_target="tpu_custom_call" | custom-call | flops 10066329600 | bytes 6586368 | tf_op jit(solution)/shard_map/self_forward/pallas_call | solution.py:366
  138.6 3.7 all-to-all-start
  155.4 4.2 convolution_convert_fusion.5.k_ref.v_ref
  159.6 34.1 %cross_forward.1 = (bf16[1088,768]{1,0:T(8,128)(2,1)}, f32[6,3,8,512]{3,2,1,0:T(8,128)}) custom-call(bf16[1088,768]{1,0:T(8,128)(2,1)} %convolution_convert_fusion.7.q_ref, bf16[1024,1536]{1,0:T(8,128)(2,1)} %convolution_convert_fusion.5.k_ref.v_ref, bf16[1024,1536]{1,0:T(8,128)(2,1)} %convolution_convert_fusion.5.k_ref.v_ref), custom_call_target="tpu_custom_call" | custom-call | flops 6845104128 | bytes 4816896 | tf_op jit(solution)/shard_map/cross_forward/pallas_call | solution.py:486
  193.6 3.5 fusion.69
  199.5 12.5 %multiply_convert_fusion = (bf16[1088,3072]{1,0:T(8,128)(2,1)}, f32[1088,3072]{1,0:T(8,128)}) fusion(bf16[768,3072]{1,0:T(8,128)(2,1)} %all-gather.6.cloned.1.call-done, f32[1088,768]{1,0:T(8,128)} %copy-done.7, f32[768]{0:T(1024)S(1)} %get-tuple-element.75, f32[768]{0:T(1024)S(1)} %get-tuple-element.76, f32[1088]{0:T(1024)S(1)} %add_rsqrt_fusion.1, ...), kind=kOutput, calls=%fused_computation.7 | convolution fusion | flops 5154717696 | bytes 28129792 | tf_op jit(solution)/shard_map/dot_general | solution.py:22
  212.0 21.8 %all-gather.8.cloned.1.call-done = bf16[3072,768]{1,0:T(8,128)(2,1)} async-done(((bf16[192,768]{1,0:T(8,128)(2,1)}), bf16[3072,768]{1,0:T(8,128)(2,1)}) %all-gather.8.cloned.1.call-update) | async-done | bytes 4718608 | tf_op jit(solution)/shard_map/all_gather | solution.py:43
  233.8 11.1 %fusion.70 = (f32[1088]{0:T(1024)S(1)}, f32[1088,768]{1,0:T(8,128)S(1)}) fusion(bf16[1088,3072]{1,0:T(8,128)(2,1)} %get-tuple-element.128, bf16[3072,768]{1,0:T(8,128)(2,1)} %all-gather.8.cloned.1.call-done, f32[768]{0:T(1024)S(1)} %get-tuple-element.75, f32[768]{0:T(1024)S(1)} %get-tuple-element.76, f32[1088]{0:T(1024)S(1)} %add_rsqrt_fusion.1, ...), kind=kOutput, calls=%fused_computation.211 | convolution fusion | flops 5138840576 | bytes 18107136 | tf_op jit(solution)/shard_map/dot_general | solution.py:22
  247.5 4.0 fusion.13
  251.5 10.2 %convolution_convert_fusion.1 = bf16[3072,768]{1,0:T(8,128)(2,1)S(1)} fusion(bf16[1088,3072]{1,0:T(8,128)(2,1)} %get-tuple-element.128, f32[1088,768]{1,0:T(8,128)S(1)} %get-tuple-element.131, f32[1088]{0:T(1024)S(1)} %get-tuple-element.134, f32[1088]{0:T(1024)S(1)} %get-tuple-element.135, f32[768]{0:T(1024)S(1)} %get-tuple-element.73, ...), kind=kOutput, calls=%fused_computation.12 | convolution fusion | flops 5146214400 | bytes 16437248 | tf_op jit(solution)/shard_map/dot_general | solution.py:26
  261.8 17.6 %fusion.5 = bf16[1088,3072]{1,0:T(8,128)(2,1)} fusion(bf16[3072,768]{1,0:T(8,128)(2,1)S(1)} %bitcast.218, f32[1088,3072]{1,0:T(8,128)} %get-tuple-element.129, f32[1088,768]{1,0:T(8,128)S(1)} %get-tuple-element.131, f32[1088]{0:T(1024)S(1)} %get-tuple-element.134, f32[1088]{0:T(1024)S(1)} %get-tuple-element.135, f32[768]{0:T(1024)S(1)} %get-tuple-element.73, ...), kind=kOutput, calls=%fused_computation.9 | convolution fusion | flops 5183963136 | bytes 29806592 | tf_op jit(solution)/shard_map/dot_general | solution.py:30
  279.4 10.0 %convolution_convert_fusion = bf16[768,3072]{1,0:T(8,128)(2,1)S(1)} fusion(bf16[1088,3072]{1,0:T(8,128)(2,1)} %fusion.5, f32[1088,768]{1,0:T(8,128)S(1)} %copy-done.8, f32[768]{0:T(1024)S(1)} %get-tuple-element.75, f32[768]{0:T(1024)S(1)} %get-tuple-element.76, f32[1088]{0:T(1024)S(1)} %add_rsqrt_fusion.1, f32[1088]{0:T(1024)S(1)} %broadcast_multiply_fusion.7), kind=kOutput, calls=%fused_computation.11 | convolution fusion | flops 5140365312 | bytes 14760448 | tf_op jit(solution)/shard_map/dot_general | solution.py:26
  298.7 15.2 %multiply_reduce_fusion = (bf16[768]{0:T(1024)(128)(2,1)S(1)}, f32[1088]{0:T(1024)S(1)}, f32[1088]{0:T(1024)S(1)}, bf16[768]{0:T(1024)(128)(2,1)S(1)}, f32[1088,768]{1,0:T(8,128)S(1)}) fusion(f32[1088,768]{1,0:T(8,128)} %copy-done.7, f32[1088]{0:T(1024)S(1)} %add_rsqrt_fusion.1, f32[1088]{0:T(1024)S(1)} %broadcast_multiply_fusion.7, ...), kind=kOutput, calls=%fused_computation.34 | convolution fusion | flops 5151371264 | bytes 23145472 | tf_op jit(solution)/shard_map/dot_general | solution.py:30
  315.0 5.0 convolution_convert_fusion.6.grad_ref
  320.1 45.4 %cross_backward.1 = (bf16[1088,768]{1,0:T(8,128)(2,1)}, bf16[1024,768]{1,0:T(8,128)(2,1)}, bf16[1024,768]{1,0:T(8,128)(2,1)}) custom-call(bf16[1088,768]{1,0:T(8,128)(2,1)} %convolution_convert_fusion.7.q_ref, bf16[1024,1536]{1,0:T(8,128)(2,1)} %convolution_convert_fusion.5.k_ref.v_ref, bf16[1024,1536]{1,0:T(8,128)(2,1)} %convolution_convert_fusion.5.k_ref.v_ref, ...), custom_call_target="tpu_custom_call" | custom-call | flops 17112760320 | bytes 8159232 | tf_op jit(solution)/shard_map/cross_backward/pallas_call | solution.py:506
  365.4 6.8 %multiply_reduce_fusion.1 = (bf16[768]{0:T(1024)(128)(2,1)S(1)}, f32[1088]{0:T(1024)S(1)}, f32[1088]{0:T(1024)S(1)}, bf16[768]{0:T(1024)(128)(2,1)S(1)}, f32[1088,768]{1,0:T(8,128)}) fusion(f32[1088,768]{1,0:T(8,128)S(1)} %get-tuple-element.125, f32[1088]{0:T(1024)S(1)} %add_rsqrt_fusion.2, f32[1088]{0:T(1024)S(1)} %broadcast_multiply_fusion.8, ...), kind=kOutput, calls=%fused_computation.35 | convolution fusion | flops 1291809280 | bytes 12901376 | tf_op jit(solution)/shard_map/dot_general | solution.py:30
  372.8 3.8 fusion.56
  382.6 4.7 all-to-all-start.1
  412.7 70.5 %self_backward.1 = (bf16[3,2,1088,384]{3,2,1,0:T(8,128)(2,1)}, bf16[2,1024,384]{2,1,0:T(8,128)(2,1)}) custom-call(s32[3]{0:T(128)} %pad_add_fusion.info, bf16[2,1088,384]{2,1,0:T(8,128)(2,1)} %bitcast.225, bf16[2,1088,384]{2,1,0:T(8,128)(2,1)} %bitcast.223, bf16[2,1088,384]{2,1,0:T(8,128)(2,1)} %bitcast.221, ...), custom_call_target="tpu_custom_call" | custom-call | flops 25165824000 | bytes 14942208 | tf_op jit(solution)/shard_map/self_backward/pallas_call | solution.py:397
  483.2 3.1 fusion.57
  501.6 4.4 reduce-scatter.6.cloned.1.call-done
  518.9 6.7 %all_to_all.20 = bf16[2,1024,768]{2,1,0:T(8,128)(2,1)S(1)} all-to-all(bf16[2,1024,768]{2,1,0:T(8,128)(2,1)S(1)} %slice.383), channel_id=1, replica_groups=mesh['grp'=2,'fsdp'=8,'seq'=2] {'seq'}, dimensions={0} | all-to-all | bytes 6291456 | tf_op jit(solution)/shard_map/all_to_all | solution.py:750
  527.7 8.9 %collective-permute-done.8 = bf16[384,768]{1,0:T(8,128)(2,1)S(1)} collective-permute-done((bf16[384,768]{1,0:T(8,128)(2,1)S(1)}, bf16[384,768]{1,0:T(8,128)(2,1)S(1)}, u32[]{:S(2)}, u32[]{:S(2)}) %collective-permute-start.8) | collective-permute-done | bytes 589856 | tf_op jit(solution)/shard_map/ppermute | solution.py:59
  542.7 6.2 %collective-permute-done.3 = bf16[256,768]{1,0:T(8,128)(2,1)S(1)} collective-permute-done((bf16[256,768]{1,0:T(8,128)(2,1)S(1)}, bf16[256,768]{1,0:T(8,128)(2,1)S(1)}, u32[]{:S(2)}, u32[]{:S(2)}) %collective-permute-start.3) | collective-permute-done | bytes 393248 | tf_op jit(solution)/shard_map/ppermute | solution.py:34
  548.9 8.7 %collective-permute-done.5 = bf16[256,768]{1,0:T(8,128)(2,1)S(1)} collective-permute-done((bf16[256,768]{1,0:T(8,128)(2,1)S(1)}, bf16[256,768]{1,0:T(8,128)(2,1)S(1)}, u32[]{:S(2)}, u32[]{:S(2)}) %collective-permute-start.5) | collective-permute-done | bytes 393248 | tf_op jit(solution)/shard_map/ppermute | solution.py:59
  561.7 25.2 %reduce-scatter.8.cloned.1.call-done = bf16[544,384]{1,0:T(8,128)(2,1)} async-done(((bf16[4352,384]{1,0:T(8,128)(2,1)}), bf16[544,384]{1,0:T(8,128)(2,1)}) %reduce-scatter.8.cloned.1.call-update) | async-done | bytes 417808 | tf_op jit(solution)/shard_map/reduce_scatter | solution.py:867
  592.0 3.9 all_to_all.21
  (262 shorter events, 127.3 us)
Async XLA Ops:
  7.2 60.8 %copy-start = (bf16[96,3072]{1,0:T(8,128)(2,1)S(1)}, bf16[96,3072]{1,0:T(8,128)(2,1)}, u32[]{:S(2)}) copy-start(bf16[96,3072]{1,0:T(8,128)(2,1)} %param.26) | copy-start | bytes 1769476
  7.2 6.8 %copy-start.40 = (bf16[96,768]{1,0:T(8,128)(2,1)S(1)}, bf16[96,768]{1,0:T(8,128)(2,1)}, u32[]{:S(2)}) copy-start(bf16[96,768]{1,0:T(8,128)(2,1)} %param.25) | copy-start | bytes 442372
  7.2 6.8 %copy-start.39 = (bf16[96,1536]{1,0:T(8,128)(2,1)S(1)}, bf16[96,1536]{1,0:T(8,128)(2,1)}, u32[]{:S(2)}) copy-start(bf16[96,1536]{1,0:T(8,128)(2,1)} %param.24) | copy-start | bytes 884740
  7.2 135.2 %all-gather.4.cloned.1.call-start = ((), (), s32[]{:S(2)}) async-start(), calls=%async_computation.7 | async-start | bytes 6475776 | tf_op jit(solution)/shard_map/all_gather | solution.py:43
  68.0 131.5 %all-gather.6.cloned.1.call-start = ((), (), s32[]{:S(2)}) async-start(), calls=%async_computation.8 | async-start | bytes 5013504 | tf_op jit(solution)/shard_map/all_gather | solution.py:43
  68.8 165.0 %all-gather.8.cloned.1.call-start = ((), (), s32[]{:S(2)}) async-start(), calls=%async_computation.9 | async-start | bytes 5013504 | tf_op jit(solution)/shard_map/all_gather | solution.py:43
  73.2 7.7 %copy-start.16 = (bf16[1,8,96,384]{3,2,1,0:T(8,128)(2,1)}, bf16[1,8,96,384]{3,2,1,0:T(8,128)(2,1)S(1)}, u32[]{:S(2)}) copy-start(bf16[1,8,96,384]{3,2,1,0:T(8,128)(2,1)S(1)} %get-tuple-element.93) | copy-start | bytes 1769476
  138.6 6.2 %all-to-all-start = ((bf16[2,1088,384]{2,1,0:T(8,128)(2,1)}), bf16[2,1088,384]{2,1,0:T(8,128)(2,1)S(1)}, u32[]{:S(2)}, u32[]{:S(2)}) async-start(bf16[2,1088,384]{2,1,0:T(8,128)(2,1)} %get-tuple-element.43.out_ref), calls=%async_computation | async-start | bytes 3342336 | tf_op jit(solution)/shard_map/all_to_all | solution.py:750
  142.3 270.1 %reduce-scatter.4.cloned.1.call-start = ((), (), s32[]{:S(2)}) async-start(), calls=%async_computation.10 | async-start | bytes 10027008 | tf_op jit(solution)/shard_map/reduce_scatter | solution.py:47
  244.9 16.8 %copy-start.11 = (f32[1088,768]{1,0:T(8,128)}, f32[1088,768]{1,0:T(8,128)S(1)}, u32[]{:S(2)}) copy-start(f32[1088,768]{1,0:T(8,128)S(1)} %get-tuple-element.131) | copy-start | bytes 10027012
  247.5 14.2 %slice-start = ((s8[4718592]{0:T(1024)(128)(4,1)}), s8[4194304]{0:T(1024)(128)(4,1)S(1)}, s32[]{:S(2)}) async-start(s8[4718592]{0:T(1024)(128)(4,1)} %bitcast.217), calls=%async_computation.13 | async-start | bytes 8388608
  251.5 10.2 %slice-start.1 = ((s8[4718592]{0:T(1024)(128)(4,1)}), s8[524288]{0:T(1024)(128)(4,1)S(1)}, s32[]{:S(2)}) async-start(s8[4718592]{0:T(1024)(128)(4,1)} %bitcast.217), calls=%async_computation.14 | async-start | bytes 1048576
  261.8 17.7 %copy-start.8 = (f32[1088,768]{1,0:T(8,128)S(1)}, f32[1088,768]{1,0:T(8,128)}, u32[]{:S(2)}) copy-start(f32[1088,768]{1,0:T(8,128)} %copy-done.7) | copy-start | bytes 10027012
  298.6 15.2 %copy-start.9 = (f32[1088,768]{1,0:T(8,128)S(1)}, f32[1088,768]{1,0:T(8,128)}, u32[]{:S(2)}) copy-start(f32[1088,768]{1,0:T(8,128)} %copy-done.7) | copy-start | bytes 10027012
  382.6 29.8 %all-to-all-start.1 = ((bf16[2,1088,384]{2,1,0:T(8,128)(2,1)}), bf16[2,1088,384]{2,1,0:T(8,128)(2,1)}, u32[]{:S(2)}, u32[]{:S(2)}) async-start(bf16[2,1088,384]{2,1,0:T(8,128)(2,1)} %pad_maximum_fusion.1), calls=%async_computation.1 | async-start | bytes 3342336 | tf_op jit(solution)/shard_map/all_to_all | solution.py:750
  387.3 118.7 %reduce-scatter.6.cloned.1.call-start = ((), (), s32[]{:S(2)}) async-start(), calls=%async_computation.11 | async-start | bytes 8355840 | tf_op jit(solution)/shard_map/reduce_scatter | solution.py:47
  412.4 174.4 %reduce-scatter.8.cloned.1.call-start = ((), (), s32[]{:S(2)}) async-start(), calls=%async_computation.12 | async-start | bytes 3760128 | tf_op jit(solution)/shard_map/reduce_scatter | solution.py:867
  486.3 7.2 %copy-start.4 = (bf16[1,2,1088,384]{3,2,1,0:T(8,128)(2,1)}, bf16[1,2,1088,384]{3,2,1,0:T(8,128)(2,1)S(1)}, u32[]{:S(2)}) copy-start(bf16[1,2,1088,384]{3,2,1,0:T(8,128)(2,1)S(1)} %get-tuple-element.81) | copy-start | bytes 5013508
  506.0 6.4 %copy-start.21 = (bf16[1,8,96,384]{3,2,1,0:T(8,128)(2,1)S(1)}, bf16[1,8,96,384]{3,2,1,0:T(8,128)(2,1)}, u32[]{:S(2)}) copy-start(bf16[1,8,96,384]{3,2,1,0:T(8,128)(2,1)} %copy-done.19) | copy-start | bytes 1769476
  510.3 17.3 %collective-permute-start.6 = (bf16[384,768]{1,0:T(8,128)(2,1)S(1)}, bf16[384,768]{1,0:T(8,128)(2,1)S(1)}, u32[]{:S(2)}, u32[]{:S(2)}) collective-permute-start(bf16[384,768]{1,0:T(8,128)(2,1)S(1)} %copy-done.35), channel_id=1, source_target_pairs={{0,16},{16,0},{1,17},{17,1},{2,18},{18,2},{3,19},{19,3},{4,20},{20... | collective-permute-start | bytes 1769480 | tf_op jit(solution)/shard_map/ppermute | solution.py:34
  511.8 15.9 %collective-permute-start.7 = (bf16[384,768]{1,0:T(8,128)(2,1)S(1)}, bf16[384,768]{1,0:T(8,128)(2,1)S(1)}, u32[]{:S(2)}, u32[]{:S(2)}) collective-permute-start(bf16[384,768]{1,0:T(8,128)(2,1)S(1)} %copy-done.35), channel_id=1, source_target_pairs={{0,1},{1,0},{2,3},{3,2},{4,5},{5,4},{6,7},{7,6},{8,9},{9,8},{10,11... | collective-permute-start | bytes 1769480 | tf_op jit(solution)/shard_map/ppermute | solution.py:34
  511.8 24.8 %collective-permute-start.8 = (bf16[384,768]{1,0:T(8,128)(2,1)S(1)}, bf16[384,768]{1,0:T(8,128)(2,1)S(1)}, u32[]{:S(2)}, u32[]{:S(2)}) collective-permute-start(bf16[384,768]{1,0:T(8,128)(2,1)S(1)} %copy-done.35), channel_id=1, source_target_pairs={{0,17},{1,16},{16,1},{17,0},{2,19},{3,18},{18,3},{19,2},{4,21},{5,... | collective-permute-start | bytes 1769480 | tf_op jit(solution)/shard_map/ppermute | solution.py:59
  518.7 6.9 %copy-start.6 = (bf16[2176,768]{1,0:T(8,128)(2,1)}, bf16[2176,768]{1,0:T(8,128)(2,1)S(1)}, u32[]{:S(2)}) copy-start(bf16[2176,768]{1,0:T(8,128)(2,1)S(1)} %add_convert_fusion) | copy-start | bytes 10027012
  518.9 6.7 %copy-start.10 = (f32[1088,768]{1,0:T(8,128)S(1)}, f32[1088,768]{1,0:T(8,128)}, u32[]{:S(2)}) copy-start(f32[1088,768]{1,0:T(8,128)} %get-tuple-element.80) | copy-start | bytes 10027012
  527.7 9.4 %copy-start.36 = (bf16[320,768]{1,0:T(8,128)(2,1)S(1)}, bf16[320,768]{1,0:T(8,128)(2,1)}, u32[]{:S(2)}) copy-start(bf16[320,768]{1,0:T(8,128)(2,1)} %reduce-scatter.6.cloned.1.call-done) | copy-start | bytes 1474564
  537.1 11.8 %collective-permute-start.3 = (bf16[256,768]{1,0:T(8,128)(2,1)S(1)}, bf16[256,768]{1,0:T(8,128)(2,1)S(1)}, u32[]{:S(2)}, u32[]{:S(2)}) collective-permute-start(bf16[256,768]{1,0:T(8,128)(2,1)S(1)} %pad_maximum_fusion.3), channel_id=1, source_target_pairs={{0,16},{16,0},{1,17},{17,1},{2,18},{18,2},{3,19},{19,3},{4,20},{20... | collective-permute-start | bytes 1179656 | tf_op jit(solution)/shard_map/ppermute | solution.py:34
  538.1 10.8 %collective-permute-start.4 = (bf16[256,768]{1,0:T(8,128)(2,1)S(1)}, bf16[256,768]{1,0:T(8,128)(2,1)S(1)}, u32[]{:S(2)}, u32[]{:S(2)}) collective-permute-start(bf16[256,768]{1,0:T(8,128)(2,1)S(1)} %pad_maximum_fusion.3), channel_id=1, source_target_pairs={{0,1},{1,0},{2,3},{3,2},{4,5},{5,4},{6,7},{7,6},{8,9},{9,8},{10,11... | collective-permute-start | bytes 1179656 | tf_op jit(solution)/shard_map/ppermute | solution.py:34
  539.6 18.0 %collective-permute-start.5 = (bf16[256,768]{1,0:T(8,128)(2,1)S(1)}, bf16[256,768]{1,0:T(8,128)(2,1)S(1)}, u32[]{:S(2)}, u32[]{:S(2)}) collective-permute-start(bf16[256,768]{1,0:T(8,128)(2,1)S(1)} %pad_maximum_fusion.3), channel_id=1, source_target_pairs={{0,17},{1,16},{16,1},{17,0},{2,19},{3,18},{18,3},{19,2},{4,21},{5,... | collective-permute-start | bytes 1179656 | tf_op jit(solution)/shard_map/ppermute | solution.py:59
  560.8 39.3 %copy-start.1 = (bf16[96,3072]{1,0:T(8,128)(2,1)S(1)}, bf16[96,3072]{1,0:T(8,128)(2,1)}, u32[]{:S(2)}) copy-start(bf16[96,3072]{1,0:T(8,128)(2,1)} %param.26) | copy-start | bytes 1769476
  587.8 9.7 %collective-permute-start = (bf16[288,384]{1,0:T(8,128)(2,1)S(1)}, bf16[288,384]{1,0:T(8,128)(2,1)S(1)}, u32[]{:S(2)}, u32[]{:S(2)}) collective-permute-start(bf16[288,384]{1,0:T(8,128)(2,1)S(1)} %slice.386), channel_id=1, source_target_pairs={{0,16},{16,0},{1,17},{17,1},{2,18},{18,2},{3,19},{19,3},{4,20},{20... | collective-permute-start | bytes 663560 | tf_op jit(solution)/shard_map/ppermute | solution.py:34
  589.4 8.1 %collective-permute-start.1 = (bf16[288,384]{1,0:T(8,128)(2,1)S(1)}, bf16[288,384]{1,0:T(8,128)(2,1)S(1)}, u32[]{:S(2)}, u32[]{:S(2)}) collective-permute-start(bf16[288,384]{1,0:T(8,128)(2,1)S(1)} %slice.386), channel_id=1, source_target_pairs={{0,1},{1,0},{2,3},{3,2},{4,5},{5,4},{6,7},{7,6},{8,9},{9,8},{10,11... | collective-permute-start | bytes 663560 | tf_op jit(solution)/shard_map/ppermute | solution.py:34
  589.4 8.5 %collective-permute-start.2 = (bf16[288,384]{1,0:T(8,128)(2,1)S(1)}, bf16[288,384]{1,0:T(8,128)(2,1)S(1)}, u32[]{:S(2)}, u32[]{:S(2)}) collective-permute-start(bf16[288,384]{1,0:T(8,128)(2,1)S(1)} %slice.386), channel_id=1, source_target_pairs={{0,17},{1,16},{16,1},{17,0},{2,19},{3,18},{18,3},{19,2},{4,21},{5,... | collective-permute-start | bytes 663560 | tf_op jit(solution)/shard_map/ppermute | solution.py:59
  (33 other events, 95.9 us)
Sparse Core Ops, SparseCore 0:
  68.1 56.3 all-gather.3
  127.3 51.7 all-gather.5
  182.0 51.7 all-gather.7
  296.9 109.7 reduce-scatter.3
  412.6 93.3 reduce-scatter.5
  509.4 77.3 reduce-scatter.7

commit v5 on v4

--- a/solution.py
+++ b/solution.py
@@ -39,8 +39,8 @@
     return lax.dynamic_slice_in_dim(value, lax.axis_index("seq") * half, half, 0)
 
 
-def gather_rows(shard):
-    return lax.all_gather(half_rows(shard), ("fsdp", "seq"), axis=0, tiled=True)
+def gather_rows(half):
+    return lax.all_gather(half, ("fsdp", "seq"), axis=0, tiled=True)
 
 
 def scatter_sum(value):
@@ -601,11 +601,6 @@
     def mine(origin):
         return lax.rem(origin + group, 2) == 0
 
-    def start_pair(event, origin, first):
-        weights, rows = pair_copies(event, origin, first)
-        pl.when(mine(origin))(weights.start)
-        rows.start()
-
     def twin_copy(event, origin):
         held = w_out.at[:, 2 * origin + 1 - low]
         return remote(held, held, g_send.at[event], g_recv.at[event], twin)
@@ -634,7 +629,9 @@
 
     for d in (0, 1):
         start_line(d, 0)
-    start_pair(0, high, True)
+    weights, rows = pair_copies(0, high, True)
+    pl.when(mine(high))(weights.start)
+    rows.start()
     for copy in across:
         copy.start()
     core_copy(0, high, low, True).start()
@@ -647,16 +644,15 @@
         def _():
             origin = origin_of(event)
             held, _ = block(origin, low, False)
+            to_pair = pair_copies(number, origin, False)
             for i, ref in enumerate(held):
                 remote(ref, ref, z_send.at[d, k, i], z_recv.at[d, k, i], pair).wait_recv()
-            if k + 1 < count - 1:
-
-                @pl.when(inside(high + signs[d]))
-                def _():
-                    for copy in line_copies(d, k + 1):
-                        copy.start()
-
-            start_pair(number, origin, False)
+                if k + 1 < count - 1:
+                    pl.when(inside(high + signs[d]))(line_copies(d, k + 1)[i].start)
+                if i == 0:
+                    pl.when(mine(origin))(to_pair[0].start)
+                else:
+                    to_pair[1].start()
             core_copy(number, origin, low, False).start()
 
     def finish(number, event):
@@ -777,25 +773,26 @@
     rows_c = count * half
     reach = prefix[0]
 
+    norms = jnp.concatenate([norm_gain, norm_bias], 0).T
+    norms = jnp.pad(norms, ((0, 0), (0, 128 - norms.shape[1])))
+    early = gather_rows(half_rows(jnp.concatenate([w_attn_out, norms], 1)))
+    mixed = half_rows(jnp.concatenate([w_cross_q, w_cross_out, w_cross_kv, w_ffn_in], 1))
+    w2 = half_rows(w_ffn_out)
     own = lax.dynamic_index_in_dim(w_qkv.reshape(shard, 3, 2, hg), seq, 2, False).swapaxes(0, 1)
+    own, mixed, w2 = lax.optimization_barrier((own, mixed, w2))
     pair = jnp.stack([prompt_in[0], enc_in[0]], 0)
     wq, shared, x_all = gather_start(own, pair, cont_in[0].reshape(rows_c, width), prompt_in[0])
     wq = wq.reshape(3, -1, hg)
     prompt_all = shared[0].reshape(-1, width)
     enc_all = shared[1].reshape(-1, width)
-    norms = jnp.concatenate([norm_gain, norm_bias], 0).T
-    norms = jnp.pad(norms, ((0, 0), (0, 128 - norms.shape[1])))
-    mixed = jnp.concatenate([w_attn_out, w_cross_q, w_cross_out, w_cross_kv, norms], 1)
-    mixed, x_all = lax.optimization_barrier((mixed, x_all))
-    mixed = gather_rows(mixed)
-    wo = mixed[:, :width]
-    wcq = mixed[:, width : 2 * width]
-    wco = mixed[:, 2 * width : 3 * width]
-    wckv = mixed[:, 3 * width : 5 * width]
-    norms = mixed[:, 5 * width :].astype(F32).T
-    w_ffn_in, w_ffn_out, x_all = lax.optimization_barrier((w_ffn_in, w_ffn_out, x_all))
-    w1 = gather_rows(w_ffn_in)
-    w2 = gather_rows(w_ffn_out)
+    mixed, w2, x_all = lax.optimization_barrier((mixed, w2, x_all))
+    mixed, w2 = gather_rows(mixed), gather_rows(w2)
+    wo = early[:, :width]
+    norms = early[:, width:].astype(F32).T
+    wcq = mixed[:, :width]
+    wco = mixed[:, width : 2 * width]
+    wckv = mixed[:, 2 * width : 4 * width]
+    w1 = mixed[:, 4 * width :]
 
     mine = jnp.concatenate([cont_in[0].reshape(rows_c, width), prompt_in[0]], 0)
     flat = x_all.reshape(-1, width)

time: 616 us -> 596 us (0.968)
  waiting for transfers between devices: 76 us -> 58 us
    all_gather x3, waiting for transfers between devices: 21.9 us -> 0.06 us  [gather_rows(): return lax.all_gather(half, ('fsdp', 'seq'), axis=0, tiled=True)]
    unnamed x127 -> x137, local copies, waits for them, and re-layouts: 27.7 us -> 24.2 us
  transfers between devices with their start and end apart: 17 -> 17, of which waited for: 8 -> 7; matrix products, arithmetic and copies ran while one was open for 26% -> 27% of each run, Pallas kernels for 33% -> 43%
where the time goes in v5:
time: 596 us; the launch traced here: 588 us
  Pallas kernels  255 us (43%)
  matrix products  155 us (26%)
  waiting for transfers between devices  58 us (10%)
  local copies, waits for them, and re-layouts  46 us (8%)
  other arithmetic  32.4 us (5%)
  starting transfers between devices  16 us (3%)
  between operations  15.3 us (3%)
  blocking collectives  10.5 us (2%)
    pallas_call x1, Pallas kernels, self_backward(): pl.pallas_call(functools.partial(self_backward_kernel, half=half, count=c...  70.8 us
    dot_general x13, matrix products, mm_nt(): lax.dot_general(a, b, (((1,), (1,)), ((), ())), preferred_element_type=F32)  59.9 us
    pallas_call x1, Pallas kernels, gather_start(): pl.pallas_call(gather_kernel, out_shape=(jax.ShapeDtypeStruct((kinds, chi...  56.8 us
    dot_general x12, matrix products, mm(): return jnp.dot(a, b, preferred_element_type=F32)  55.6 us
    pallas_call x1, Pallas kernels, self_forward(): pl.pallas_call(functools.partial(self_forward_kernel, half=half, count=co...  47.6 us
    pallas_call x1, Pallas kernels, cross_backward(): pl.pallas_call(functools.partial(cross_backward_kernel, full=full, rest=r...  45.5 us
    dot_general x13, matrix products, mm_tn(): lax.dot_general(a, b, (((0,), (0,)), ((), ())), preferred_element_type=F32)  39.1 us
    pallas_call x1, Pallas kernels, cross_forward(): pl.pallas_call(functools.partial(cross_forward_kernel, full=full, rest=ro...  34.3 us
  transfers between devices with their start and end apart: 17, of which 7 were waited for; matrix products, arithmetic and copies ran while one was open for 27% of the time, Pallas kernels for 43%

profile of v5, /device:TPU:0, one launch (start us, length us, event | category | flops | bytes accessed | tf_op | source)
XLA Modules:
  0.0 588.0 jit_solution(5554978340849128118)
XLA Ops:
  14.5 56.8 %gather_start.1 = (bf16[3,8,96,384]{3,2,1,0:T(8,128)(2,1)}, bf16[2,8,2,64,768]{4,3,2,1,0:T(8,128)(2,1)}, bf16[2,1088,768]{2,1,0:T(8,128)(2,1)}) custom-call(bf16[3,96,384]{2,1,0:T(8,128)(2,1)} %bitcast.205, bf16[2,64,768]{2,1,0:T(8,128)(2,1)} %pad_maximum_fusion.4.s_ref, bf16[1024,768]{1,0:T(8,128)(2,1)} %bitcast.168, bf16[64,768]{1,0:T(8,128)(2,1)} %bitcast.203), custom_call_target="tpu_custom_call" | custom-call | tf_op jit(solution)/shard_map/gather_start/pallas_call | solution.py:719
  74.8 3.1 convolution_convert_fusion.2
  77.8 3.1 convolution_convert_fusion.3
  86.0 3.4 convolution_convert_fusion.15.pk_ref
  89.4 3.1 convolution_convert_fusion.4
  92.5 47.6 %self_forward.1 = (bf16[2,1088,384]{2,1,0:T(8,128)(2,1)}, f32[3,5,8,512]{3,2,1,0:T(8,128)}) custom-call(s32[3]{0:T(128)} %pad_add_fusion.info, bf16[2,1088,384]{2,1,0:T(8,128)(2,1)} %bitcast.224, bf16[2,1088,384]{2,1,0:T(8,128)(2,1)} %bitcast.222, bf16[2,1088,384]{2,1,0:T(8,128)(2,1)} %bitcast.220, bf16[1024,384]{1,0:T(8,128)(2,1)} %convolution_convert_fusion.15.pk_ref, ...), custom_call_target="tpu_custom_call" | custom-call | flops 10066329600 | bytes 6586368 | tf_op jit(solution)/shard_map/self_forward/pallas_call | solution.py:366
  140.1 3.7 all-to-all-start
  153.2 4.3 convolution_convert_fusion.7.q_ref
  157.5 6.1 %convolution_convert_fusion.5.k_ref.v_ref = bf16[1024,1536]{1,0:T(8,128)(2,1)} fusion(bf16[1024,768]{1,0:T(8,128)(2,1)S(1)} %bitcast.196, bf16[768,6144]{1,0:T(8,128)(2,1)} %all-gather.6.cloned.1.call-done), kind=kOutput, calls=%fused_computation.31 | convolution fusion | flops 2417491968 | bytes 7077888 | tf_op jit(solution)/shard_map/dot_general | solution.py:22
  163.6 34.3 %cross_forward.1 = (bf16[1088,768]{1,0:T(8,128)(2,1)}, f32[6,3,8,512]{3,2,1,0:T(8,128)}) custom-call(bf16[1088,768]{1,0:T(8,128)(2,1)} %convolution_convert_fusion.7.q_ref, bf16[1024,1536]{1,0:T(8,128)(2,1)} %convolution_convert_fusion.5.k_ref.v_ref, bf16[1024,1536]{1,0:T(8,128)(2,1)} %convolution_convert_fusion.5.k_ref.v_ref), custom_call_target="tpu_custom_call" | custom-call | flops 6845104128 | bytes 4816896 | tf_op jit(solution)/shard_map/cross_forward/pallas_call | solution.py:486
  197.9 3.7 fusion.80
  203.3 11.1 %multiply_convert_fusion = (bf16[1088,3072]{1,0:T(8,128)(2,1)}, f32[1088,3072]{1,0:T(8,128)}) fusion(bf16[768,6144]{1,0:T(8,128)(2,1)S(1)} %bitcast.216, f32[1088,768]{1,0:T(8,128)S(1)} %get-tuple-element.129, f32[768]{0:T(1024)S(1)} %get-tuple-element.77, f32[768]{0:T(1024)S(1)} %get-tuple-element.78, f32[1088]{0:T(1024)S(1)} %add_rsqrt_fusion.1, ...), kind=kOutput, calls=%fused_computation.7 | convolution fusion | flops 5154717696 | bytes 28139520 | tf_op jit(solution)/shard_map/dot_general | solution.py:22
  214.4 11.1 %fusion.81 = (f32[1088]{0:T(1024)S(1)}, f32[1088,768]{1,0:T(8,128)S(1)}) fusion(bf16[1088,3072]{1,0:T(8,128)(2,1)} %get-tuple-element.130, bf16[3072,768]{1,0:T(8,128)(2,1)} %all-gather.8.cloned.1.call-done, f32[768]{0:T(1024)S(1)} %get-tuple-element.77, f32[768]{0:T(1024)S(1)} %get-tuple-element.78, f32[1088]{0:T(1024)S(1)} %add_rsqrt_fusion.1, ...), kind=kOutput, calls=%fused_computation.219 | convolution fusion | flops 5138840576 | bytes 18107136 | tf_op jit(solution)/shard_map/dot_general | solution.py:22
  228.0 3.8 fusion.20
  231.9 10.2 %convolution_convert_fusion.1 = bf16[3072,768]{1,0:T(8,128)(2,1)S(1)} fusion(bf16[1088,3072]{1,0:T(8,128)(2,1)} %get-tuple-element.130, f32[1088,768]{1,0:T(8,128)S(1)} %get-tuple-element.133, f32[1088]{0:T(1024)S(1)} %get-tuple-element.136, f32[1088]{0:T(1024)S(1)} %get-tuple-element.137, f32[768]{0:T(1024)S(1)} %get-tuple-element.75, ...), kind=kOutput, calls=%fused_computation.12 | convolution fusion | flops 5146214400 | bytes 16437248 | tf_op jit(solution)/shard_map/dot_general | solution.py:26
  242.1 17.7 %fusion.5 = bf16[1088,3072]{1,0:T(8,128)(2,1)} fusion(bf16[3072,768]{1,0:T(8,128)(2,1)S(1)} %bitcast.218, f32[1088,3072]{1,0:T(8,128)} %get-tuple-element.131, f32[1088,768]{1,0:T(8,128)S(1)} %get-tuple-element.133, f32[1088]{0:T(1024)S(1)} %get-tuple-element.136, f32[1088]{0:T(1024)S(1)} %get-tuple-element.137, f32[768]{0:T(1024)S(1)} %get-tuple-element.75, ...), kind=kOutput, calls=%fused_computation.9 | convolution fusion | flops 5183963136 | bytes 29806592 | tf_op jit(solution)/shard_map/dot_general | solution.py:30
  259.8 10.1 %convolution_convert_fusion = bf16[768,3072]{1,0:T(8,128)(2,1)S(1)} fusion(bf16[1088,3072]{1,0:T(8,128)(2,1)} %fusion.5, f32[1088,768]{1,0:T(8,128)S(1)} %copy-done.8, f32[768]{0:T(1024)S(1)} %get-tuple-element.77, f32[768]{0:T(1024)S(1)} %get-tuple-element.78, f32[1088]{0:T(1024)S(1)} %add_rsqrt_fusion.1, f32[1088]{0:T(1024)S(1)} %broadcast_multiply_fusion.7), kind=kOutput, calls=%fused_computation.11 | convolution fusion | flops 5140365312 | bytes 14760448 | tf_op jit(solution)/shard_map/dot_general | solution.py:26
  279.2 14.9 %multiply_reduce_fusion = (bf16[768]{0:T(1024)(128)(2,1)S(1)}, f32[1088]{0:T(1024)S(1)}, f32[1088]{0:T(1024)S(1)}, bf16[768]{0:T(1024)(128)(2,1)S(1)}, f32[1088,768]{1,0:T(8,128)S(1)}) fusion(f32[1088,768]{1,0:T(8,128)} %copy-done.7, f32[1088]{0:T(1024)S(1)} %add_rsqrt_fusion.1, f32[1088]{0:T(1024)S(1)} %broadcast_multiply_fusion.7, ...), kind=kOutput, calls=%fused_computation.38 | convolution fusion | flops 5151371264 | bytes 23145472 | tf_op jit(solution)/shard_map/dot_general | solution.py:30
  295.3 5.0 convolution_convert_fusion.6.grad_ref
  300.3 45.5 %cross_backward.1 = (bf16[1088,768]{1,0:T(8,128)(2,1)}, bf16[1024,768]{1,0:T(8,128)(2,1)}, bf16[1024,768]{1,0:T(8,128)(2,1)}) custom-call(bf16[1088,768]{1,0:T(8,128)(2,1)} %convolution_convert_fusion.7.q_ref, bf16[1024,1536]{1,0:T(8,128)(2,1)} %convolution_convert_fusion.5.k_ref.v_ref, bf16[1024,1536]{1,0:T(8,128)(2,1)} %convolution_convert_fusion.5.k_ref.v_ref, ...), custom_call_target="tpu_custom_call" | custom-call | flops 17112760320 | bytes 8159232 | tf_op jit(solution)/shard_map/cross_backward/pallas_call | solution.py:506
  345.8 6.7 %multiply_reduce_fusion.1 = (bf16[768]{0:T(1024)(128)(2,1)S(1)}, f32[1088]{0:T(1024)S(1)}, f32[1088]{0:T(1024)S(1)}, bf16[768]{0:T(1024)(128)(2,1)S(1)}, f32[1088,768]{1,0:T(8,128)}) fusion(f32[1088,768]{1,0:T(8,128)S(1)} %get-tuple-element.127, f32[1088]{0:T(1024)S(1)} %add_rsqrt_fusion.2, f32[1088]{0:T(1024)S(1)} %broadcast_multiply_fusion.8, ...), kind=kOutput, calls=%fused_computation.39 | convolution fusion | flops 1291809280 | bytes 12901376 | tf_op jit(solution)/shard_map/dot_general | solution.py:30
  353.1 3.8 fusion.67
  360.4 4.7 all-to-all-start.1
  390.3 70.8 %self_backward.1 = (bf16[3,2,1088,384]{3,2,1,0:T(8,128)(2,1)}, bf16[2,1024,384]{2,1,0:T(8,128)(2,1)}) custom-call(s32[3]{0:T(128)} %pad_add_fusion.info, bf16[2,1088,384]{2,1,0:T(8,128)(2,1)} %bitcast.225, bf16[2,1088,384]{2,1,0:T(8,128)(2,1)} %bitcast.223, bf16[2,1088,384]{2,1,0:T(8,128)(2,1)} %bitcast.221, ...), custom_call_target="tpu_custom_call" | custom-call | flops 25165824000 | bytes 14942208 | tf_op jit(solution)/shard_map/self_backward/pallas_call | solution.py:397
  461.1 3.1 fusion.68
  479.6 7.3 %reduce-scatter.6.cloned.1.call-done = bf16[320,768]{1,0:T(8,128)(2,1)} async-done(((bf16[5120,768]{1,0:T(8,128)(2,1)}), bf16[320,768]{1,0:T(8,128)(2,1)}) %reduce-scatter.6.cloned.1.call-update) | async-done | bytes 491536 | tf_op jit(solution)/shard_map/reduce_scatter | solution.py:47
  499.7 6.7 %all_to_all.20 = bf16[2,1024,768]{2,1,0:T(8,128)(2,1)S(1)} all-to-all(bf16[2,1024,768]{2,1,0:T(8,128)(2,1)S(1)} %slice.388), channel_id=1, replica_groups=mesh['grp'=2,'fsdp'=8,'seq'=2] {'seq'}, dimensions={0} | all-to-all | bytes 6291456 | tf_op jit(solution)/shard_map/all_to_all | solution.py:746
  508.5 9.0 %collective-permute-done.8 = bf16[384,768]{1,0:T(8,128)(2,1)S(1)} collective-permute-done((bf16[384,768]{1,0:T(8,128)(2,1)S(1)}, bf16[384,768]{1,0:T(8,128)(2,1)S(1)}, u32[]{:S(2)}, u32[]{:S(2)}) %collective-permute-start.8) | collective-permute-done | bytes 589856 | tf_op jit(solution)/shard_map/ppermute | solution.py:59
  523.6 6.2 %collective-permute-done.3 = bf16[256,768]{1,0:T(8,128)(2,1)S(1)} collective-permute-done((bf16[256,768]{1,0:T(8,128)(2,1)S(1)}, bf16[256,768]{1,0:T(8,128)(2,1)S(1)}, u32[]{:S(2)}, u32[]{:S(2)}) %collective-permute-start.3) | collective-permute-done | bytes 393248 | tf_op jit(solution)/shard_map/ppermute | solution.py:34
  529.8 8.7 %collective-permute-done.5 = bf16[256,768]{1,0:T(8,128)(2,1)S(1)} collective-permute-done((bf16[256,768]{1,0:T(8,128)(2,1)S(1)}, bf16[256,768]{1,0:T(8,128)(2,1)S(1)}, u32[]{:S(2)}, u32[]{:S(2)}) %collective-permute-start.5) | collective-permute-done | bytes 393248 | tf_op jit(solution)/shard_map/ppermute | solution.py:59
  542.6 25.2 %reduce-scatter.8.cloned.1.call-done = bf16[544,384]{1,0:T(8,128)(2,1)} async-done(((bf16[4352,384]{1,0:T(8,128)(2,1)}), bf16[544,384]{1,0:T(8,128)(2,1)}) %reduce-scatter.8.cloned.1.call-update) | async-done | bytes 417808 | tf_op jit(solution)/shard_map/reduce_scatter | solution.py:864
  572.8 3.9 all_to_all.21
  (272 shorter events, 118.1 us)
Async XLA Ops:
  7.2 5.7 copy-start.42
  7.2 6.6 %copy-start.35 = (bf16[1,64,768]{2,1,0:T(8,128)(2,1)S(1)}, bf16[1,64,768]{2,1,0:T(8,128)(2,1)}, u32[]{:S(2)}) copy-start(bf16[1,64,768]{2,1,0:T(8,128)(2,1)} %param.15) | copy-start | bytes 294916
  7.3 6.5 %copy-start.44 = (bf16[1,64,768]{2,1,0:T(8,128)(2,1)S(1)}, bf16[1,64,768]{2,1,0:T(8,128)(2,1)}, u32[]{:S(2)}) copy-start(bf16[1,64,768]{2,1,0:T(8,128)(2,1)} %param.17) | copy-start | bytes 294916
  7.3 136.6 %all-gather.4.cloned.1.call-start = ((), (), s32[]{:S(2)}) async-start(), calls=%async_computation.7 | async-start | bytes 1462272 | tf_op jit(solution)/shard_map/all_gather | solution.py:43
  9.8 143.4 %all-gather.6.cloned.1.call-start = ((), (), s32[]{:S(2)}) async-start(), calls=%async_computation.8 | async-start | bytes 10027008 | tf_op jit(solution)/shard_map/all_gather | solution.py:43
  71.4 143.0 %all-gather.8.cloned.1.call-start = ((), (), s32[]{:S(2)}) async-start(), calls=%async_computation.9 | async-start | bytes 5013504 | tf_op jit(solution)/shard_map/all_gather | solution.py:43
  74.8 7.6 %copy-start.16 = (bf16[1,8,96,384]{3,2,1,0:T(8,128)(2,1)}, bf16[1,8,96,384]{3,2,1,0:T(8,128)(2,1)S(1)}, u32[]{:S(2)}) copy-start(bf16[1,8,96,384]{3,2,1,0:T(8,128)(2,1)S(1)} %get-tuple-element.95) | copy-start | bytes 1769476
  140.1 6.4 %all-to-all-start = ((bf16[2,1088,384]{2,1,0:T(8,128)(2,1)}), bf16[2,1088,384]{2,1,0:T(8,128)(2,1)S(1)}, u32[]{:S(2)}, u32[]{:S(2)}) async-start(bf16[2,1088,384]{2,1,0:T(8,128)(2,1)} %get-tuple-element.46.out_ref), calls=%async_computation | async-start | bytes 3342336 | tf_op jit(solution)/shard_map/all_to_all | solution.py:746
  143.8 246.2 %reduce-scatter.4.cloned.1.call-start = ((), (), s32[]{:S(2)}) async-start(), calls=%async_computation.10 | async-start | bytes 10027008 | tf_op jit(solution)/shard_map/reduce_scatter | solution.py:47
  225.5 16.6 %copy-start.11 = (f32[1088,768]{1,0:T(8,128)}, f32[1088,768]{1,0:T(8,128)S(1)}, u32[]{:S(2)}) copy-start(f32[1088,768]{1,0:T(8,128)S(1)} %get-tuple-element.133) | copy-start | bytes 10027012
  228.0 14.1 %slice-start.3 = ((s8[4718592]{0:T(1024)(128)(4,1)}), s8[4194304]{0:T(1024)(128)(4,1)S(1)}, s32[]{:S(2)}) async-start(s8[4718592]{0:T(1024)(128)(4,1)} %bitcast.217), calls=%async_computation.16 | async-start | bytes 8388608
  231.9 10.3 %slice-start.4 = ((s8[4718592]{0:T(1024)(128)(4,1)}), s8[524288]{0:T(1024)(128)(4,1)S(1)}, s32[]{:S(2)}) async-start(s8[4718592]{0:T(1024)(128)(4,1)} %bitcast.217), calls=%async_computation.17 | async-start | bytes 1048576
  242.1 17.7 %copy-start.8 = (f32[1088,768]{1,0:T(8,128)S(1)}, f32[1088,768]{1,0:T(8,128)}, u32[]{:S(2)}) copy-start(f32[1088,768]{1,0:T(8,128)} %copy-done.7) | copy-start | bytes 10027012
  279.2 14.9 %copy-start.9 = (f32[1088,768]{1,0:T(8,128)S(1)}, f32[1088,768]{1,0:T(8,128)}, u32[]{:S(2)}) copy-start(f32[1088,768]{1,0:T(8,128)} %copy-done.7) | copy-start | bytes 10027012
  360.4 29.6 %all-to-all-start.1 = ((bf16[2,1088,384]{2,1,0:T(8,128)(2,1)}), bf16[2,1088,384]{2,1,0:T(8,128)(2,1)}, u32[]{:S(2)}, u32[]{:S(2)}) async-start(bf16[2,1088,384]{2,1,0:T(8,128)(2,1)} %pad_maximum_fusion.1), calls=%async_computation.1 | async-start | bytes 3342336 | tf_op jit(solution)/shard_map/all_to_all | solution.py:746
  365.0 121.8 %reduce-scatter.6.cloned.1.call-start = ((), (), s32[]{:S(2)}) async-start(), calls=%async_computation.11 | async-start | bytes 8355840 | tf_op jit(solution)/shard_map/reduce_scatter | solution.py:47
  390.1 177.7 %reduce-scatter.8.cloned.1.call-start = ((), (), s32[]{:S(2)}) async-start(), calls=%async_computation.12 | async-start | bytes 3760128 | tf_op jit(solution)/shard_map/reduce_scatter | solution.py:864
  464.2 7.2 %copy-start.4 = (bf16[1,2,1088,384]{3,2,1,0:T(8,128)(2,1)}, bf16[1,2,1088,384]{3,2,1,0:T(8,128)(2,1)S(1)}, u32[]{:S(2)}) copy-start(bf16[1,2,1088,384]{3,2,1,0:T(8,128)(2,1)S(1)} %get-tuple-element.83) | copy-start | bytes 5013508
  486.9 6.4 %copy-start.21 = (bf16[1,8,96,384]{3,2,1,0:T(8,128)(2,1)S(1)}, bf16[1,8,96,384]{3,2,1,0:T(8,128)(2,1)}, u32[]{:S(2)}) copy-start(bf16[1,8,96,384]{3,2,1,0:T(8,128)(2,1)} %copy-done.19) | copy-start | bytes 1769476
  491.2 17.3 %collective-permute-start.6 = (bf16[384,768]{1,0:T(8,128)(2,1)S(1)}, bf16[384,768]{1,0:T(8,128)(2,1)S(1)}, u32[]{:S(2)}, u32[]{:S(2)}) collective-permute-start(bf16[384,768]{1,0:T(8,128)(2,1)S(1)} %copy-done.38), channel_id=1, source_target_pairs={{0,16},{16,0},{1,17},{17,1},{2,18},{18,2},{3,19},{19,3},{4,20},{20... | collective-permute-start | bytes 1769480 | tf_op jit(solution)/shard_map/ppermute | solution.py:34
  492.7 15.8 %collective-permute-start.7 = (bf16[384,768]{1,0:T(8,128)(2,1)S(1)}, bf16[384,768]{1,0:T(8,128)(2,1)S(1)}, u32[]{:S(2)}, u32[]{:S(2)}) collective-permute-start(bf16[384,768]{1,0:T(8,128)(2,1)S(1)} %copy-done.38), channel_id=1, source_target_pairs={{0,1},{1,0},{2,3},{3,2},{4,5},{5,4},{6,7},{7,6},{8,9},{9,8},{10,11... | collective-permute-start | bytes 1769480 | tf_op jit(solution)/shard_map/ppermute | solution.py:34
  492.7 24.8 %collective-permute-start.8 = (bf16[384,768]{1,0:T(8,128)(2,1)S(1)}, bf16[384,768]{1,0:T(8,128)(2,1)S(1)}, u32[]{:S(2)}, u32[]{:S(2)}) collective-permute-start(bf16[384,768]{1,0:T(8,128)(2,1)S(1)} %copy-done.38), channel_id=1, source_target_pairs={{0,17},{1,16},{16,1},{17,0},{2,19},{3,18},{18,3},{19,2},{4,21},{5,... | collective-permute-start | bytes 1769480 | tf_op jit(solution)/shard_map/ppermute | solution.py:59
  499.5 9.0 %copy-start.6 = (bf16[2176,768]{1,0:T(8,128)(2,1)}, bf16[2176,768]{1,0:T(8,128)(2,1)S(1)}, u32[]{:S(2)}) copy-start(bf16[2176,768]{1,0:T(8,128)(2,1)S(1)} %add_convert_fusion) | copy-start | bytes 10027012
  499.7 6.7 %copy-start.10 = (f32[1088,768]{1,0:T(8,128)S(1)}, f32[1088,768]{1,0:T(8,128)}, u32[]{:S(2)}) copy-start(f32[1088,768]{1,0:T(8,128)} %get-tuple-element.82) | copy-start | bytes 10027012
  508.5 9.4 %copy-start.39 = (bf16[320,768]{1,0:T(8,128)(2,1)S(1)}, bf16[320,768]{1,0:T(8,128)(2,1)}, u32[]{:S(2)}) copy-start(bf16[320,768]{1,0:T(8,128)(2,1)} %reduce-scatter.6.cloned.1.call-done) | copy-start | bytes 1474564
  518.0 11.8 %collective-permute-start.3 = (bf16[256,768]{1,0:T(8,128)(2,1)S(1)}, bf16[256,768]{1,0:T(8,128)(2,1)S(1)}, u32[]{:S(2)}, u32[]{:S(2)}) collective-permute-start(bf16[256,768]{1,0:T(8,128)(2,1)S(1)} %pad_maximum_fusion.3), channel_id=1, source_target_pairs={{0,16},{16,0},{1,17},{17,1},{2,18},{18,2},{3,19},{19,3},{4,20},{20... | collective-permute-start | bytes 1179656 | tf_op jit(solution)/shard_map/ppermute | solution.py:34
  519.0 10.8 %collective-permute-start.4 = (bf16[256,768]{1,0:T(8,128)(2,1)S(1)}, bf16[256,768]{1,0:T(8,128)(2,1)S(1)}, u32[]{:S(2)}, u32[]{:S(2)}) collective-permute-start(bf16[256,768]{1,0:T(8,128)(2,1)S(1)} %pad_maximum_fusion.3), channel_id=1, source_target_pairs={{0,1},{1,0},{2,3},{3,2},{4,5},{5,4},{6,7},{7,6},{8,9},{9,8},{10,11... | collective-permute-start | bytes 1179656 | tf_op jit(solution)/shard_map/ppermute | solution.py:34
  520.5 18.0 %collective-permute-start.5 = (bf16[256,768]{1,0:T(8,128)(2,1)S(1)}, bf16[256,768]{1,0:T(8,128)(2,1)S(1)}, u32[]{:S(2)}, u32[]{:S(2)}) collective-permute-start(bf16[256,768]{1,0:T(8,128)(2,1)S(1)} %pad_maximum_fusion.3), channel_id=1, source_target_pairs={{0,17},{1,16},{16,1},{17,0},{2,19},{3,18},{18,3},{19,2},{4,21},{5,... | collective-permute-start | bytes 1179656 | tf_op jit(solution)/shard_map/ppermute | solution.py:59
  541.7 39.2 %copy-start.1 = (bf16[384,768]{1,0:T(8,128)(2,1)S(1)}, bf16[384,768]{1,0:T(8,128)(2,1)}, u32[]{:S(2)}) copy-start(bf16[384,768]{1,0:T(8,128)(2,1)} %param.27) | copy-start | bytes 1769476
  568.7 9.7 %collective-permute-start = (bf16[288,384]{1,0:T(8,128)(2,1)S(1)}, bf16[288,384]{1,0:T(8,128)(2,1)S(1)}, u32[]{:S(2)}, u32[]{:S(2)}) collective-permute-start(bf16[288,384]{1,0:T(8,128)(2,1)S(1)} %slice.391), channel_id=1, source_target_pairs={{0,16},{16,0},{1,17},{17,1},{2,18},{18,2},{3,19},{19,3},{4,20},{20... | collective-permute-start | bytes 663560 | tf_op jit(solution)/shard_map/ppermute | solution.py:34
  570.2 8.2 %collective-permute-start.1 = (bf16[288,384]{1,0:T(8,128)(2,1)S(1)}, bf16[288,384]{1,0:T(8,128)(2,1)S(1)}, u32[]{:S(2)}, u32[]{:S(2)}) collective-permute-start(bf16[288,384]{1,0:T(8,128)(2,1)S(1)} %slice.391), channel_id=1, source_target_pairs={{0,1},{1,0},{2,3},{3,2},{4,5},{5,4},{6,7},{7,6},{8,9},{9,8},{10,11... | collective-permute-start | bytes 663560 | tf_op jit(solution)/shard_map/ppermute | solution.py:34
  570.2 8.6 %collective-permute-start.2 = (bf16[288,384]{1,0:T(8,128)(2,1)S(1)}, bf16[288,384]{1,0:T(8,128)(2,1)S(1)}, u32[]{:S(2)}, u32[]{:S(2)}) collective-permute-start(bf16[288,384]{1,0:T(8,128)(2,1)S(1)} %slice.391), channel_id=1, source_target_pairs={{0,17},{1,16},{16,1},{17,0},{2,19},{3,18},{18,3},{19,2},{4,21},{5,... | collective-permute-start | bytes 663560 | tf_op jit(solution)/shard_map/ppermute | solution.py:59
  (40 other events, 132.1 us)
Sparse Core Ops, SparseCore 0:
  10.8 44.9 all-gather.3
  71.5 80.2 all-gather.5
  154.7 51.5 all-gather.7
  277.5 110.6 reduce-scatter.3
  392.1 94.7 reduce-scatter.5
  490.3 77.3 reduce-scatter.7
